TPU v7x, 32 devices: a whole 2x2x4 slice. The times are simulated.
32 devices in a mesh: head: 4 (over y, core), shard: 8 (over z, x).
Axes of the slice: x: 2, y: 2, z: 4, core: 2. Of those that a mesh axis runs over, the one named last changes fastest.
Arguments:
- inputs: bfloat16 [4, 8, 4, 64, 2048], P(None, 'shard', 'head'), may hold values from -6 to 6
- segments: int32 [4, 8, 4, 64], P(None, 'shard'), may hold values from 0 to 2047, as said below
- query_weight: bfloat16 [2048, 256], P(('head', 'shard')), may hold values from -0.125 to 0.125
- key_weight: bfloat16 [2048, 256], P(('head', 'shard')), may hold values from -0.125 to 0.125
- value_weight: bfloat16 [2048, 2048], P(('head', 'shard')), may hold values from -0.125 to 0.125
- project_weight: bfloat16 [2048, 2048], P(('head', 'shard')), may hold values from -1.5 to 1.5
- attend_gain: bfloat16 [2048], P(('head', 'shard')), may hold values from 0.5 to 1.5
- gate_weight: bfloat16 [2048, 5632], P('shard', 'head'), may hold values from -0.125 to 0.125
- up_weight: bfloat16 [2048, 5632], P('shard', 'head'), may hold values from -0.125 to 0.125
- down_weight: bfloat16 [5632, 2048], P('head', 'shard'), may hold values from -0.078125 to 0.078125
- forward_gain: bfloat16 [2048], P(('head', 'shard')), may hold values from 0.5 to 1.5
- upstream: bfloat16 [4, 8, 4, 64, 2048], P(None, 'shard', 'head'), may hold values from -6 to 6
Outputs:
- outputs: bfloat16 [4, 8, 4, 64, 2048], P(None, 'shard', 'head')
- inputs_grad: float32 [4, 8, 4, 64, 2048], P(None, 'shard', 'head')
- query_grad: float32 [2048, 256], P(('head', 'shard'))
- key_grad: float32 [2048, 256], P(('head', 'shard'))
- value_grad: float32 [2048, 2048], P(('head', 'shard'))
- project_grad: float32 [2048, 2048], P(('head', 'shard'))
- attend_grad: float32 [2048], P(('head', 'shard'))
- gate_grad: float32 [2048, 5632], P('shard', 'head')
- up_grad: float32 [2048, 5632], P('shard', 'head')
- down_grad: float32 [5632, 2048], P('head', 'shard')
- forward_grad: float32 [2048], P(('head', 'shard'))
Inputs may be any that keep to these rules, and one draw needn't show every extreme that they name: `segments`: A token's segment number is the position within its sequence of the first token of its document, so the numbers start at 0 and never fall from one token to the next; one of the 4 sequences is a single document, and another ends with a document of one token.
All inputs are finite; a program needn't handle non-finite values.
Results may differ from a plain program's by a relative error of at most 0.017.
Values may be sent and summed in bfloat16 or wider, within the bound.
No kernel may reach another device: no remote copies, remote signals or barrier semaphores. Data moves between devices by JAX's collectives and lax.ppermute only.
A program may use at most 576 MiB of HBM per device.

v0:
```python
import math

import jax
import jax.numpy as jnp
from jax import lax
from jax.sharding import PartitionSpec as P

D = 2048
HEADS = 16
QK = 16
VD = 128


EPS_NORM = 1e-05
HIGH = lax.Precision.HIGHEST


def carried_in(value, axis, combine, identity):
    size, here = (lax.axis_size(axis), lax.axis_index(axis))
    everything = jax.tree.map(lambda part: lax.all_gather(part, axis), value)
    start = jax.tree.map(
        lambda part, zero: jnp.broadcast_to(jnp.asarray(zero, part.dtype), part.shape),
        value,
        identity,
    )

    def carried_turn(k, before):
        reached = k < here
        new = combine(before, jax.tree.map(lambda part: part[k], everything))
        return jax.tree.map(lambda a, b: jnp.where(reached, a, b), new, before)

    return lax.fori_loop(0, size, carried_turn, start)


def prefix(value, axis, combine, identity):
    size, here = (lax.axis_size(axis), lax.axis_index(axis))
    everything = jax.tree.map(
        lambda part, kind: lax.all_gather(part.astype(kind), axis),
        value,
        jax.tree.map(lambda a: jnp.bfloat16 if a.dtype == jnp.float32 else a.dtype, value),
    )
    start = jax.tree.map(
        lambda part, zero: jnp.broadcast_to(jnp.asarray(zero, part.dtype), part.shape),
        value,
        identity,
    )

    def prefix_turn(k, before):
        at = size - 1 - k
        reached = at > here
        new = combine(
            before, jax.tree.map(lambda part, own: part[at].astype(own.dtype), everything, value)
        )
        return jax.tree.map(lambda a, b: jnp.where(reached, a, b), new, before)

    return lax.fori_loop(0, size, prefix_turn, start)


def features(values):
    qk_size = values.shape[-1]
    square = (values[..., :, None] * values[..., None, :]).reshape(
        values.shape[:-1] + (qk_size * qk_size,)
    )
    ones_col = jnp.ones(values.shape[:-1] + (1,), jnp.float32)
    return jnp.concatenate(
        [ones_col, values * qk_size ** (-0.25), square / math.sqrt(2.0 * qk_size)], axis=-1
    )


def features_back(values, grad_feats):
    qk_size = values.shape[-1]
    linear = grad_feats[..., 1 : 1 + qk_size]
    square = grad_feats[..., 1 + qk_size :].reshape(grad_feats.shape[:-1] + (qk_size, qk_size))
    paired = jnp.einsum("...ij,...j->...i", square, values, precision=HIGH) + jnp.einsum(
        "...ji,...j->...i", square, values, precision=HIGH
    )
    return linear * qk_size ** (-0.25) + paired / math.sqrt(2.0 * qk_size)


def normalize(rows_in):
    inverse = lax.rsqrt(jnp.mean(rows_in * rows_in, axis=-1, keepdims=True) + EPS_NORM)
    return (rows_in * inverse, inverse)


def normalize_back(normed, inverse, grad_normed):
    return inverse * (grad_normed - normed * jnp.mean(grad_normed * normed, axis=-1, keepdims=True))


def forward_combine(earlier, latter):
    keep_old = (latter[2] <= earlier[2]).astype(jnp.float32)
    return (
        latter[0] + keep_old[..., None, None, None] * earlier[0],
        latter[1] + keep_old[..., None, None] * earlier[1],
        jnp.maximum(earlier[2], latter[2]),
    )


def backward_combine(earlier, latter):
    keep_old = (earlier[2] <= latter[2]).astype(jnp.float32)
    return (
        latter[0] + keep_old[..., None, None, None] * earlier[0],
        latter[1] + keep_old[..., None, None] * earlier[1],
        jnp.minimum(earlier[2], latter[2]),
    )


def product(left, right):
    return jnp.dot(left, right, preferred_element_type=jnp.float32)


def contract(pattern, left, right):
    return jnp.einsum(pattern, left, right, precision=HIGH)


def swiglu_pass(active_rows, grad_rows, gate_mat, up_mat, down_mat):
    gate_pre = product(active_rows, gate_mat)
    up_pre = product(active_rows, up_mat)
    sigmoid_gate = jax.nn.sigmoid(gate_pre)
    silu_gate = gate_pre * sigmoid_gate
    hidden_act = (silu_gate * up_pre).astype(jnp.bfloat16)
    down_out = product(hidden_act, down_mat)
    grad_hidden = product(grad_rows, down_mat.T)
    grad_gate = (
        grad_hidden * up_pre * (sigmoid_gate * (1.0 + gate_pre * (1.0 - sigmoid_gate)))
    ).astype(jnp.bfloat16)
    grad_up = (grad_hidden * silu_gate).astype(jnp.bfloat16)
    down_sum = product(hidden_act.T, grad_rows)
    gate_sum = product(active_rows.T, grad_gate)
    up_sum = product(active_rows.T, grad_up)
    grad_active = product(grad_gate, gate_mat.T) + product(grad_up, up_mat.T)
    return (down_out, grad_active, gate_sum, up_sum, down_sum)


def body(
    inputs,
    segments,
    query_weight,
    key_weight,
    value_weight,
    project_weight,
    attend_gain,
    gate_weight,
    up_weight,
    down_weight,
    forward_gain,
    upstream,
):
    groups = lax.axis_size("head")
    per_group = HEADS // groups
    seq_count = inputs.shape[0]
    sub_rows = inputs.shape[3]
    block_len = groups * sub_rows
    token_rows = seq_count * sub_rows
    root_qk = math.sqrt(QK)
    attend_set = (
        lax.all_gather(query_weight, ("head", "shard"), axis=0, tiled=True),
        lax.all_gather(key_weight, ("head", "shard"), axis=0, tiled=True),
        lax.all_gather(value_weight, ("head", "shard"), axis=0, tiled=True),
        lax.all_gather(project_weight, ("head", "shard"), axis=0, tiled=True),
        lax.all_gather(attend_gain, ("head", "shard"), axis=0, tiled=True),
        lax.all_gather(forward_gain, ("head", "shard"), axis=0, tiled=True),
    )
    full_query, full_key, full_value, full_project, full_gain_one, full_gain_two = attend_set
    hidden_in = inputs.reshape(token_rows, D).astype(jnp.float32)
    normed_one, inverse_one = normalize(hidden_in)
    gain_one = full_gain_one.astype(jnp.float32)
    active_one = (normed_one * gain_one).astype(jnp.bfloat16)
    query_rows = product(active_one, full_query).astype(jnp.bfloat16)
    key_rows = product(active_one, full_key).astype(jnp.bfloat16)
    value_rows = product(active_one, full_value).astype(jnp.bfloat16)

    def to_groups(rows_in):
        return rows_in.reshape(seq_count, 1, 1, sub_rows, rows_in.shape[-1])

    def to_heads(shards, head_size):
        return (
            shards.reshape(seq_count, block_len, per_group, head_size)
            .transpose(0, 2, 1, 3)
            .astype(jnp.float32)
        )

    def from_heads(head_arr):
        return (
            head_arr.astype(jnp.bfloat16)
            .transpose(0, 2, 1, 3)
            .reshape(seq_count, 1, groups, sub_rows, per_group * head_arr.shape[-1])
        )

    query_parts, key_parts, value_parts = (
        lax.all_to_all(to_groups(query_rows), "head", split_axis=4, concat_axis=2, tiled=True),
        lax.all_to_all(to_groups(key_rows), "head", split_axis=4, concat_axis=2, tiled=True),
        lax.all_to_all(to_groups(value_rows), "head", split_axis=4, concat_axis=2, tiled=True),
    )
    query_head = to_heads(query_parts, QK)
    key_head = to_heads(key_parts, QK)
    value_head = to_heads(value_parts, VD)
    seg_float = segments.reshape(seq_count, block_len).astype(jnp.float32)
    causal = lax.broadcasted_iota(jnp.int32, (block_len, block_len), 0) >= lax.broadcasted_iota(
        jnp.int32, (block_len, block_len), 1
    )
    visible = (causal[None] & (seg_float[:, :, None] == seg_float[:, None, :])).astype(jnp.float32)[
        :, None
    ]
    scores = contract("bhtd,bhsd->bhts", query_head, key_head) / root_qk
    weights = (1.0 + scores + 0.5 * scores * scores) * visible
    feat_query = features(query_head)
    feat_key = features(key_head)
    last_seg = seg_float[:, -1]
    last_mask = (seg_float == last_seg[:, None]).astype(jnp.float32)[:, None, :, None]
    masked_key = feat_key * last_mask
    state_local = contract("bhtf,bhtc->bhfc", masked_key, value_head)
    norm_local = jnp.sum(masked_key, axis=2)
    start_state = (
        jnp.zeros_like(state_local),
        jnp.zeros_like(norm_local),
        jnp.full_like(last_seg, -1.0),
    )
    state_in, norm_in, last_in = carried_in(
        (state_local, norm_local, last_seg), "shard", forward_combine, start_state
    )
    use_in = (seg_float == last_in[:, None]).astype(jnp.float32)[:, None, :, None]
    numerator = contract("bhts,bhsc->bhtc", weights, value_head) + use_in * contract(
        "bhtf,bhfc->bhtc", feat_query, state_in
    )
    denominator = jnp.sum(weights, axis=-1) + use_in[..., 0] * contract(
        "bhtf,bhf->bht", feat_query, norm_in
    )
    attended = numerator / denominator[..., None]
    mixed_rows = lax.all_to_all(
        from_heads(attended), "head", split_axis=2, concat_axis=4, tiled=True
    ).reshape(token_rows, HEADS * VD)
    attend_out = product(mixed_rows, full_project)
    residual = hidden_in + attend_out
    rows_gate, rows_up, rows_down = (
        lax.all_gather(gate_weight, "shard", axis=0, tiled=True),
        lax.all_gather(up_weight, "shard", axis=0, tiled=True),
        lax.all_gather(down_weight, "shard", axis=1, tiled=True),
    )
    normed_two, inverse_two = normalize(residual)
    gain_two = full_gain_two.astype(jnp.float32)
    active_two = (normed_two * gain_two).astype(jnp.bfloat16)
    grad_out = upstream.reshape(token_rows, D)
    full_gate, full_up, full_down = (
        lax.all_gather(rows_gate, "head", axis=1, tiled=True),
        lax.all_gather(rows_up, "head", axis=1, tiled=True),
        lax.all_gather(rows_down, "head", axis=0, tiled=True),
    )
    down_out, grad_active_two, gate_whole, up_whole, down_whole = swiglu_pass(
        active_two, grad_out, full_gate, full_up, full_down
    )
    gate_part, up_part, down_part = (
        lax.psum_scatter(
            gate_whole.astype(jnp.bfloat16), "head", scatter_dimension=1, tiled=True
        ).astype(jnp.float32),
        lax.psum_scatter(
            up_whole.astype(jnp.bfloat16), "head", scatter_dimension=1, tiled=True
        ).astype(jnp.float32),
        lax.psum_scatter(
            down_whole.astype(jnp.bfloat16), "head", scatter_dimension=0, tiled=True
        ).astype(jnp.float32),
    )
    result = residual + down_out
    outputs = result.astype(jnp.bfloat16).reshape(inputs.shape)
    gate_grad, up_grad, down_grad = (
        lax.psum_scatter(
            gate_part.astype(jnp.bfloat16), "shard", scatter_dimension=0, tiled=True
        ).astype(jnp.float32),
        lax.psum_scatter(
            up_part.astype(jnp.bfloat16), "shard", scatter_dimension=0, tiled=True
        ).astype(jnp.float32),
        lax.psum_scatter(
            down_part.astype(jnp.bfloat16), "shard", scatter_dimension=1, tiled=True
        ).astype(jnp.float32),
    )
    gain_two_sum = jnp.sum(grad_active_two * normed_two, axis=0)
    grad_resid = grad_out.astype(jnp.float32) + normalize_back(
        normed_two, inverse_two, grad_active_two * gain_two
    )
    grad_attend = grad_resid.astype(jnp.bfloat16)
    project_sum = product(mixed_rows.T, grad_attend)
    grad_mixed = product(grad_attend, full_project.T).astype(jnp.bfloat16)
    grad_parts = lax.all_to_all(
        to_groups(grad_mixed), "head", split_axis=4, concat_axis=2, tiled=True
    )
    grad_head = to_heads(grad_parts, VD)
    grad_numer = grad_head / denominator[..., None]
    grad_denom = -jnp.sum(grad_head * attended, axis=-1) / denominator
    grad_value = contract("bhts,bhtc->bhsc", weights, grad_numer)
    grad_weights = contract("bhtc,bhsc->bhts", grad_numer, value_head) + grad_denom[..., None]
    grad_scores = grad_weights * (1.0 + scores) * visible
    grad_query = contract("bhts,bhsd->bhtd", grad_scores, key_head) / root_qk
    grad_key = contract("bhts,bhtd->bhsd", grad_scores, query_head) / root_qk
    grad_feat_query = use_in * (
        contract("bhtc,bhfc->bhtf", grad_numer, state_in)
        + grad_denom[..., None] * norm_in[:, :, None, :]
    )
    grad_state_in = contract("bhtf,bhtc->bhfc", feat_query, use_in * grad_numer)
    grad_norm_in = contract("bhtf,bht->bhf", feat_query, use_in[..., 0] * grad_denom)
    end_state = (
        jnp.zeros_like(grad_state_in),
        jnp.zeros_like(grad_norm_in),
        jnp.full_like(last_in, 1000000000.0),
    )
    grad_state_out, grad_norm_out, unused_keys = prefix(
        (grad_state_in, grad_norm_in, last_in), "shard", backward_combine, end_state
    )
    grad_feat_key = last_mask * (
        contract("bhfc,bhtc->bhtf", grad_state_out, value_head) + grad_norm_out[:, :, None, :]
    )
    grad_value = grad_value + last_mask * contract("bhtf,bhfc->bhtc", feat_key, grad_state_out)
    grad_query = grad_query + features_back(query_head, grad_feat_query)
    grad_key = grad_key + features_back(key_head, grad_feat_key)
    query_back, key_back, value_back = (
        lax.all_to_all(from_heads(grad_query), "head", split_axis=2, concat_axis=4, tiled=True),
        lax.all_to_all(from_heads(grad_key), "head", split_axis=2, concat_axis=4, tiled=True),
        lax.all_to_all(from_heads(grad_value), "head", split_axis=2, concat_axis=4, tiled=True),
    )
    query_back = query_back.reshape(token_rows, HEADS * QK)
    key_back = key_back.reshape(token_rows, HEADS * QK)
    value_back = value_back.reshape(token_rows, HEADS * VD)
    query_sum = product(active_one.T, query_back)
    key_sum = product(active_one.T, key_back)
    value_sum = product(active_one.T, value_back)
    grad_active_one = (
        product(query_back, full_query.T)
        + product(key_back, full_key.T)
        + product(value_back, full_value.T)
    )
    gain_one_sum = jnp.sum(grad_active_one * normed_one, axis=0)
    query_grad, key_grad, value_grad, project_grad, attend_grad, forward_grad = (
        lax.psum_scatter(query_sum, ("head", "shard"), scatter_dimension=0, tiled=True),
        lax.psum_scatter(key_sum, ("head", "shard"), scatter_dimension=0, tiled=True),
        lax.psum_scatter(value_sum, ("head", "shard"), scatter_dimension=0, tiled=True),
        lax.psum_scatter(project_sum, ("head", "shard"), scatter_dimension=0, tiled=True),
        lax.psum_scatter(gain_one_sum, ("head", "shard"), scatter_dimension=0, tiled=True),
        lax.psum_scatter(gain_two_sum, ("head", "shard"), scatter_dimension=0, tiled=True),
    )
    inputs_grad = (
        grad_resid + normalize_back(normed_one, inverse_one, grad_active_one * gain_one)
    ).reshape(inputs.shape)
    return (
        outputs,
        inputs_grad,
        query_grad,
        key_grad,
        value_grad,
        project_grad,
        attend_grad,
        gate_grad,
        up_grad,
        down_grad,
        forward_grad,
    )


def solution(mesh):
    in_specs = (
        P(None, "shard", "head", None, None),
        P(None, "shard", None, None),
        P(("head", "shard"), None),
        P(("head", "shard"), None),
        P(("head", "shard"), None),
        P(("head", "shard"), None),
        P(("head", "shard")),
        P("shard", "head"),
        P("shard", "head"),
        P("head", "shard"),
        P(("head", "shard")),
        P(None, "shard", "head", None, None),
    )
    out_specs = (
        P(None, "shard", "head", None, None),
        P(None, "shard", "head", None, None),
        P(("head", "shard"), None),
        P(("head", "shard"), None),
        P(("head", "shard"), None),
        P(("head", "shard"), None),
        P(("head", "shard")),
        P("shard", "head"),
        P("shard", "head"),
        P("head", "shard"),
        P(("head", "shard")),
    )
    return jax.shard_map(body, mesh=mesh, in_specs=in_specs, out_specs=out_specs, check_vma=False)
```

profile of v0, /device:TPU:16, one launch (start us, length us, event | category | flops | bytes accessed | tf_op | source)
XLA Modules:
  0.0 3410.6 jit_solution(4737021666080043786)
XLA Ops:
  12.9 40.4 %all-reduce.7 = (bf16[2048]{0:T(1024)(128)(2,1)S(1)}, bf16[2048]{0:T(1024)(128)(2,1)S(1)}) all-reduce(bf16[2048]{0:T(1024)(128)(2,1)S(1)} %dynamic-update-slice, bf16[2048]{0:T(1024)(128)(2,1)S(1)} %dynamic-update-slice.2), channel_id=1, replica_groups=mesh['head'=4,'shard'=8] {'head','shard'}, use_global_device_ids=true, to_apply=%add | all-reduce | flops 4096 | bytes 16384
  76.1 68.8 %all-gather.23.cloned.1.call-done = bf16[2048,2048]{1,0:T(8,128)(2,1)} async-done(((bf16[64,2048]{1,0:T(8,128)(2,1)}), bf16[2048,2048]{1,0:T(8,128)(2,1)}) %all-gather.23.cloned.1.call-update) | async-done | bytes 8388624 | tf_op jit(solution)/shard_map/all_gather | solution.py:158
  203.5 34.4 %all-gather.27.cloned.1.call-done = bf16[2048,1408]{1,0:T(8,128)(2,1)} async-done(((bf16[256,1408]{1,0:T(8,128)(2,1)}), bf16[2048,1408]{1,0:T(8,128)(2,1)}) %all-gather.27.cloned.1.call-update) | async-done | bytes 5767184 | tf_op jit(solution)/shard_map/all_gather | solution.py:235
  238.0 92.8 %all-gather.31.cloned.1.call-done = bf16[2048,1408]{1,0:T(8,128)(2,1)} async-done(((bf16[256,1408]{1,0:T(8,128)(2,1)}), bf16[2048,1408]{1,0:T(8,128)(2,1)}) %all-gather.31.cloned.1.call-update) | async-done | bytes 5767184 | tf_op jit(solution)/shard_map/all_gather | solution.py:236
  330.9 93.6 %all-gather.35.cloned.1.call-done = bf16[1408,2048]{1,0:T(8,128)(2,1)} async-done(((bf16[1408,256]{1,0:T(8,128)(2,1)}), bf16[1408,2048]{1,0:T(8,128)(2,1)}) %all-gather.35.cloned.1.call-update) | async-done | bytes 5767184 | tf_op jit(solution)/shard_map/all_gather | solution.py:237
  427.0 52.1 %all-gather.19.cloned.1.call-done = bf16[2048,256]{1,0:T(8,128)(2,1)} async-done(((bf16[64,256]{1,0:T(8,128)(2,1)}), bf16[2048,256]{1,0:T(8,128)(2,1)}) %all-gather.19.cloned.1.call-update) | async-done | bytes 1048592 | tf_op jit(solution)/shard_map/all_gather | solution.py:156
  485.3 37.2 %all-reduce.1 = f32[32]{0:T(128)S(1)} all-reduce(f32[32]{0:T(128)S(1)} %bitcast_dynamic-update-slice_fusion), channel_id=3, replica_groups=mesh['head'=4,'shard'=8] {'shard'}, use_global_device_ids=true, to_apply=%add.1 | all-reduce | flops 32 | bytes 256
  529.9 43.1 %all-gather.2 = f32[32,4,273]{2,1,0:T(4,128)} all-gather(f32[4,4,273]{2,1,0:T(4,128)S(1)} %multiply_reduce_fusion), channel_id=4, replica_groups=mesh['head'=4,'shard'=8] {'shard'}, dimensions={0}, use_global_device_ids=true | all-gather | bytes 157248 | tf_op jit(solution)/shard_map/all_gather | solution.py:20
  583.5 245.6 %all-gather.39.cloned.1.call-done = f32[32,4,273,128]{3,1,2,0:T(4,128)} async-done(((f32[4,4,273,128]{3,1,2,0:T(4,128)}), f32[32,4,273,128]{3,1,2,0:T(4,128)}) %all-gather.39.cloned.1.call-update) | async-done | bytes 17891344 | tf_op jit(solution)/shard_map/all_gather | solution.py:20
  829.1 29.9 while.38
  883.6 24.2 all-to-all-done.3
  924.8 138.8 %all-gather.29.cloned.1.call-done = bf16[2048,5632]{1,0:T(8,128)(2,1)} async-done(((bf16[2048,1408]{1,0:T(8,128)(2,1)}), bf16[2048,5632]{1,0:T(8,128)(2,1)}) %all-gather.29.cloned.1.call-update) | async-done | bytes 23068688 | tf_op jit(solution)/shard_map/all_gather | solution.py:244
  1077.9 130.2 %all-gather.33.cloned.1.call-done = bf16[2048,5632]{1,0:T(8,128)(2,1)} async-done(((bf16[2048,1408]{1,0:T(8,128)(2,1)}), bf16[2048,5632]{1,0:T(8,128)(2,1)}) %all-gather.33.cloned.1.call-update) | async-done | bytes 23068688 | tf_op jit(solution)/shard_map/all_gather | solution.py:245
  1222.4 130.6 %all-gather.37.cloned.1.call-done = bf16[5632,2048]{1,0:T(8,128)(2,1)} async-done(((bf16[1408,2048]{1,0:T(8,128)(2,1)}), bf16[5632,2048]{1,0:T(8,128)(2,1)}) %all-gather.37.cloned.1.call-update) | async-done | bytes 23068688 | tf_op jit(solution)/shard_map/all_gather | solution.py:246
  1353.0 17.4 multiply_convert_fusion
  1382.9 30.6 copy.215
  1413.7 18.0 convolution_convert_fusion.1
  1431.7 31.0 copy.217
  1515.7 29.6 all_to_all.114
  1568.2 23.5 reduce-scatter.31.cloned.1.call-done
  1600.1 161.2 %reduce-scatter.33.cloned.1.call-done = bf16[1408,2048]{1,0:T(8,128)(2,1)} async-done(((bf16[5632,2048]{1,0:T(8,128)(2,1)}), bf16[1408,2048]{1,0:T(8,128)(2,1)}) %reduce-scatter.33.cloned.1.call-update) | async-done | bytes 5767184
  1769.8 160.8 %reduce-scatter.27.cloned.1.call-done = bf16[1408,2048]{1,0:T(8,128)(2,1)} async-done(((bf16[5632,2048]{1,0:T(8,128)(2,1)}), bf16[1408,2048]{1,0:T(8,128)(2,1)}) %reduce-scatter.27.cloned.1.call-update) | async-done | bytes 5767184 | tf_op jit(solution)/shard_map/reduce_scatter | solution.py:258
  1983.8 34.3 %all-gather.5 = bf16[32,4,273]{2,1,0:T(4,128)(2,1)} all-gather(bf16[4,4,273]{2,1,0:T(4,128)(2,1)S(1)} %bitcast.327), channel_id=7, replica_groups=mesh['head'=4,'shard'=8] {'shard'}, dimensions={0}, use_global_device_ids=true | all-gather | bytes 78624 | tf_op jit(solution)/shard_map/all_gather | solution.py:38
  2023.9 42.6 %all-gather.41.cloned.1.call-done = bf16[32,4,273,128]{3,1,2,0:T(4,128)(2,1)} async-done(((bf16[4,4,273,128]{3,1,2,0:T(4,128)(2,1)}), bf16[32,4,273,128]{3,1,2,0:T(4,128)(2,1)}) %all-gather.41.cloned.1.call-update) | async-done | bytes 8945680 | tf_op jit(solution)/shard_map/all_gather | solution.py:38
  2066.6 28.3 while.39
  2201.9 41.1 %all-reduce.6 = (f32[2048]{0:T(1024)S(1)}, f32[2048]{0:T(1024)S(1)}) all-reduce(f32[2048]{0:T(1024)S(1)} %get-tuple-element.499, f32[2048]{0:T(1024)S(1)} %get-tuple-element.497), channel_id=12, replica_groups=mesh['head'=4,'shard'=8] {'head','shard'}, use_global_device_ids=true, to_apply=%region_16.17.clone | all-reduce | flops 4096 | bytes 32768
  2250.0 44.7 %reduce-scatter.25.cloned.1.call-done = bf16[256,1408]{1,0:T(8,128)(2,1)} async-done(((bf16[2048,1408]{1,0:T(8,128)(2,1)}), bf16[256,1408]{1,0:T(8,128)(2,1)}) %reduce-scatter.25.cloned.1.call-update) | async-done | bytes 720912 | tf_op jit(solution)/shard_map/reduce_scatter | solution.py:268
  2297.0 111.9 %reduce-scatter.29.cloned.1.call-done = bf16[1408,256]{1,0:T(8,128)(2,1)} async-done(((bf16[1408,2048]{1,0:T(8,128)(2,1)}), bf16[1408,256]{1,0:T(8,128)(2,1)}) %reduce-scatter.29.cloned.1.call-update) | async-done | bytes 720912 | tf_op jit(solution)/shard_map/reduce_scatter | solution.py:271
  2411.2 132.9 %reduce-scatter.15.cloned.1.call-done = f32[64,256]{1,0:T(8,128)} async-done(((f32[2048,256]{1,0:T(8,128)}), f32[64,256]{1,0:T(8,128)}) %reduce-scatter.15.cloned.1.call-update) | async-done | bytes 65552 | tf_op jit(solution)/shard_map/reduce_scatter | solution.py:331
  2544.1 137.1 %reduce-scatter.17.cloned.1.call-done = f32[64,256]{1,0:T(8,128)} async-done(((f32[2048,256]{1,0:T(8,128)}), f32[64,256]{1,0:T(8,128)}) %reduce-scatter.17.cloned.1.call-update) | async-done | bytes 65552 | tf_op jit(solution)/shard_map/reduce_scatter | solution.py:332
  2681.2 362.0 %reduce-scatter.21.cloned.1.call-done = f32[64,2048]{1,0:T(8,128)} async-done(((f32[2048,2048]{1,0:T(8,128)}), f32[64,2048]{1,0:T(8,128)}) %reduce-scatter.21.cloned.1.call-update) | async-done | bytes 524304 | tf_op jit(solution)/shard_map/reduce_scatter | solution.py:334
  3043.2 360.3 %reduce-scatter.19.cloned.1.call-done = f32[64,2048]{1,0:T(8,128)} async-done(((f32[2048,2048]{1,0:T(8,128)}), f32[64,2048]{1,0:T(8,128)}) %reduce-scatter.19.cloned.1.call-update) | async-done | bytes 524304 | tf_op jit(solution)/shard_map/reduce_scatter | solution.py:333
  (412 shorter events, 522.7 us)
Async XLA Ops:
  7.2 57.5 %all-gather.21.cloned.1.call-start = ((), (), s32[]{:S(2)}) async-start(), calls=%async_computation.19 | async-start | bytes 1081344 | tf_op jit(solution)/shard_map/all_gather | solution.py:157
  7.9 136.9 %all-gather.23.cloned.1.call-start = ((), (), s32[]{:S(2)}) async-start(), calls=%async_computation.20 | async-start | bytes 8650752 | tf_op jit(solution)/shard_map/all_gather | solution.py:158
  8.7 229.2 %all-gather.27.cloned.1.call-start = ((), (), s32[]{:S(2)}) async-start(), calls=%async_computation.22 | async-start | bytes 6488064 | tf_op jit(solution)/shard_map/all_gather | solution.py:235
  9.4 321.4 %all-gather.31.cloned.1.call-start = ((), (), s32[]{:S(2)}) async-start(), calls=%async_computation.24 | async-start | bytes 6488064 | tf_op jit(solution)/shard_map/all_gather | solution.py:236
  10.0 414.5 %all-gather.35.cloned.1.call-start = ((), (), s32[]{:S(2)}) async-start(), calls=%async_computation.26 | async-start | bytes 6488064 | tf_op jit(solution)/shard_map/all_gather | solution.py:237
  10.6 468.5 %all-gather.19.cloned.1.call-start = ((), (), s32[]{:S(2)}) async-start(), calls=%async_computation.18 | async-start | bytes 1081344 | tf_op jit(solution)/shard_map/all_gather | solution.py:156
  67.5 7.9 all-to-all-start.1
  70.9 455.6 %copy-start.52 = (f32[4,256]{1,0:T(4,128)}, f32[4,256]{1,0:T(4,128)S(1)}, u32[]{:S(2)}) copy-start(f32[4,256]{1,0:T(4,128)S(1)} %compare_convert_fusion.3) | copy-start | bytes 12292
  70.9 794.8 %copy-start.58 = (f32[273]{0:T(512)}, f32[273]{0:T(512)S(1)}, u32[]{:S(2)}) copy-start(f32[273]{0:T(512)S(1)} %pad.3.clone) | copy-start | bytes 3280
  160.0 18.8 all-to-all-start.2
  164.3 664.8 %all-gather.39.cloned.1.call-start = ((), (), s32[]{:S(2)}) async-start(), calls=%async_computation.36 | async-start | bytes 20127744 | tf_op jit(solution)/shard_map/all_gather | solution.py:20
  202.7 715.6 %all-gather.25.cloned.1.call-start = ((), (), s32[]{:S(2)}) async-start(), calls=%async_computation.21 | async-start | bytes 8650752 | tf_op jit(solution)/shard_map/all_gather | solution.py:159
  203.5 860.1 %all-gather.29.cloned.1.call-start = ((), (), s32[]{:S(2)}) async-start(), calls=%async_computation.23 | async-start | bytes 28835840 | tf_op jit(solution)/shard_map/all_gather | solution.py:244
  237.9 970.2 %all-gather.33.cloned.1.call-start = ((), (), s32[]{:S(2)}) async-start(), calls=%async_computation.25 | async-start | bytes 28835840 | tf_op jit(solution)/shard_map/all_gather | solution.py:245
  330.8 1022.1 %all-gather.37.cloned.1.call-start = ((), (), s32[]{:S(2)}) async-start(), calls=%async_computation.27 | async-start | bytes 28835840 | tf_op jit(solution)/shard_map/all_gather | solution.py:246
  481.8 40.7 %all-to-all-start = ((bf16[4,2,8192]{2,1,0:T(2,128)(2,1)}), bf16[4,2,8192]{2,1,0:T(2,128)(2,1)S(1)}, u32[]{:S(2)}, u32[]{:S(2)}) async-start(bf16[4,2,8192]{2,1,0:T(2,128)(2,1)} %reshape.352), calls=%async_computation | async-start | bytes 262144 | tf_op jit(solution)/shard_map/all_to_all | solution.py:190
  880.0 27.8 all-to-all-start.3
  883.5 708.3 %reduce-scatter.31.cloned.1.call-start = ((), (), s32[]{:S(2)}) async-start(), calls=%async_computation.38 | async-start | bytes 28835840
  924.5 579.3 %copy-start.14 = (f32[256,2048]{1,0:T(8,128)}, f32[256,2048]{1,0:T(8,128)S(1)}, u32[]{:S(2)}) copy-start(f32[256,2048]{1,0:T(8,128)S(1)} %get-tuple-element.551) | copy-start | bytes 6291460
  1413.6 347.7 %reduce-scatter.33.cloned.1.call-start = ((), (), s32[]{:S(2)}) async-start(), calls=%async_computation.39 | async-start | bytes 28835840
  1462.7 468.0 %reduce-scatter.27.cloned.1.call-start = ((), (), s32[]{:S(2)}) async-start(), calls=%async_computation.34 | async-start | bytes 28835840 | tf_op jit(solution)/shard_map/reduce_scatter | solution.py:258
  1477.1 589.5 %all-gather.41.cloned.1.call-start = ((), (), s32[]{:S(2)}) async-start(), calls=%async_computation.37 | async-start | bytes 10063872 | tf_op jit(solution)/shard_map/all_gather | solution.py:38
  1568.2 679.5 %reduce-scatter.23.cloned.1.call-start = ((), (), s32[]{:S(2)}) async-start(), calls=%async_computation.32 | async-start | bytes 6488064 | tf_op jit(solution)/shard_map/reduce_scatter | solution.py:265
  1600.1 694.6 %reduce-scatter.25.cloned.1.call-start = ((), (), s32[]{:S(2)}) async-start(), calls=%async_computation.33 | async-start | bytes 6488064 | tf_op jit(solution)/shard_map/reduce_scatter | solution.py:268
  1769.7 160.9 %copy-start.3 = (bf16[4,1,1,64,2048]{4,3,2,1,0:T(8,128)(2,1)S(1)}, bf16[4,1,1,64,2048]{4,3,2,1,0:T(8,128)(2,1)}, u32[]{:S(2)}) copy-start(bf16[4,1,1,64,2048]{4,3,2,1,0:T(8,128)(2,1)} %param.16) | copy-start | bytes 3145732
  1769.8 162.3 %copy-start.55 = (f32[4]{0:T(128)S(1)}, f32[4]{0:T(128)}, u32[]{:S(2)}) copy-start(f32[4]{0:T(128)} %copy-done.54) | copy-start | bytes 52
  1769.8 639.1 %reduce-scatter.29.cloned.1.call-start = ((), (), s32[]{:S(2)}) async-start(), calls=%async_computation.35 | async-start | bytes 6488064 | tf_op jit(solution)/shard_map/reduce_scatter | solution.py:271
  1973.4 44.7 %all-to-all-start.5 = ((bf16[4,2,8192]{2,1,0:T(2,128)(2,1)}), bf16[4,2,8192]{2,1,0:T(2,128)(2,1)S(1)}, u32[]{:S(2)}, u32[]{:S(2)}) async-start(bf16[4,2,8192]{2,1,0:T(2,128)(2,1)} %reshape.356), calls=%async_computation.5 | async-start | bytes 262144 | tf_op jit(solution)/shard_map/all_to_all | solution.py:314
  1976.7 567.4 %reduce-scatter.15.cloned.1.call-start = ((), (), s32[]{:S(2)}) async-start(), calls=%async_computation.28 | async-start | bytes 2162688 | tf_op jit(solution)/shard_map/reduce_scatter | solution.py:331
  2023.9 657.3 %reduce-scatter.17.cloned.1.call-start = ((), (), s32[]{:S(2)}) async-start(), calls=%async_computation.29 | async-start | bytes 2162688 | tf_op jit(solution)/shard_map/reduce_scatter | solution.py:332
  2122.8 920.4 %reduce-scatter.21.cloned.1.call-start = ((), (), s32[]{:S(2)}) async-start(), calls=%async_computation.31 | async-start | bytes 17301504 | tf_op jit(solution)/shard_map/reduce_scatter | solution.py:334
  2132.9 1270.6 %reduce-scatter.19.cloned.1.call-start = ((), (), s32[]{:S(2)}) async-start(), calls=%async_computation.30 | async-start | bytes 17301504 | tf_op jit(solution)/shard_map/reduce_scatter | solution.py:333
  (60 other events, 1339.8 us)
Sparse Core Ops, SparseCore 0:
  11.0 53.6 all-gather.20
  67.7 77.1 all-gather.22
  147.0 90.8 all-gather.26
  239.9 90.8 all-gather.30
  332.7 91.7 all-gather.34
  427.4 51.6 all-gather.18
  480.6 348.4 all-gather.38
  832.1 86.2 all-gather.24
  919.9 143.6 all-gather.28
  1065.0 143.1 all-gather.32
  1209.7 143.2 all-gather.36
  1413.7 178.0 reduce-scatter.30
  1594.6 166.7 reduce-scatter.32
  1763.8 166.7 reduce-scatter.26
  1933.4 133.0 all-gather.40
  2070.5 108.9 reduce-scatter.22
  2183.4 111.2 reduce-scatter.24
  2298.7 110.1 reduce-scatter.28
  2411.8 132.2 reduce-scatter.14
  2546.8 134.4 reduce-scatter.16
  2684.2 358.9 reduce-scatter.20
  3046.1 357.3 reduce-scatter.18
where the time goes:
time: 3420 us; the launch traced here: 3410 us
  waiting for transfers between devices  2590 us (76%)
  blocking collectives  267 us (8%)
  matrix products  254 us (7%)
  local copies, waits for them, and re-layouts  202 us (6%)
  other arithmetic  65.8 us (2%)
    reduce_scatter x1, waiting for transfers between devices, body(): lax.psum_scatter(project_sum, ('head', 'shard'), scatter_dimension=0, til...  362 us
    reduce_scatter x1, waiting for transfers between devices, body(): lax.psum_scatter(value_sum, ('head', 'shard'), scatter_dimension=0, tiled...  360 us
    all_gather x1, waiting for transfers between devices, carried_in(): everything = jax.tree.map(lambda part: lax.all_gather(part, axis), value)  246 us
    unnamed x24, waiting for transfers between devices  189 us
    dot_general x21, matrix products, product(): return jnp.dot(left, right, preferred_element_type=jnp.float32)  180 us
    reduce_scatter x1, waiting for transfers between devices, body(): lax.psum_scatter(down_whole.astype(jnp.bfloat16), 'head', scatter_dimensi...  161 us
    all_gather x1, waiting for transfers between devices, body(): lax.all_gather(rows_gate, 'head', axis=1, tiled=True)  139 us
    reduce_scatter x1, waiting for transfers between devices, body(): lax.psum_scatter(key_sum, ('head', 'shard'), scatter_dimension=0, tiled=T...  137 us
  transfers between devices with their start and end apart: 27, of which 24 were waited for; matrix products, arithmetic and copies ran while one was open for 13% of the time, Pallas kernels for 0%

commit v1 on v0

v1 whole, which is shorter than its diff:
```python
import functools
import math

import numpy as np

import jax
import jax.numpy as jnp
from jax import lax
from jax.experimental import pallas as pl
from jax.experimental.pallas import tpu as pltpu
from jax.sharding import Mesh
from jax.sharding import PartitionSpec as P

D = 2048
HEADS = 16
QK = 16
VD = 128
EPS = 1e-05
F32 = jnp.float32
BF16 = jnp.bfloat16
GROUP = ("hi", "core", "col")
FEAT = 1 + QK + QK * (QK + 1) // 2
FPAD = 256
FROWS = 160
PAYLOAD = 384


def feature_constants():
    left = np.zeros((128, FPAD), np.float32)
    right = np.zeros((128, FPAD), np.float32)
    rows = np.zeros((8, 2 * FPAD), np.float32)
    at = 0
    for i in range(QK):
        for j in range(i, QK):
            left[i, at] = 1.0
            right[j, at] = 1.0
            rows[1, at] = (1.0 if i == j else math.sqrt(2.0)) / math.sqrt(2.0 * QK)
            at += 1
    for i in range(QK):
        left[i, at] = 1.0
        rows[0, FPAD + at] = 1.0
        rows[1, at] = QK ** (-0.25)
        at += 1
    rows[0, at] = 1.0
    rows[0, FPAD + at] = 1.0
    rows[1, at] = 1.0
    align = np.zeros((4, 128, 128), np.float32)
    for part in range(4):
        for i in range(QK):
            align[part, part * QK + i, i] = 1.0
    return (
        jnp.asarray(np.concatenate([left, right], 1), BF16),
        jnp.asarray(rows, F32),
        jnp.asarray(align.transpose(1, 0, 2).reshape(128, 512), BF16),
    )


def dot(a, b):
    return jnp.dot(a, b, preferred_element_type=F32)


def dot_t(a, b):
    return lax.dot_general(a, b, (((1,), (1,)), ((), ())), preferred_element_type=F32)


def t_dot(a, b):
    return lax.dot_general(a, b, (((0,), (0,)), ((), ())), preferred_element_type=F32)


def swap(value, axis):
    return lax.ppermute(value, axis, [(0, 1), (1, 0)])


def gather8(own):
    half = own.shape[0] // 2
    over_x = swap(own, "col")
    over_y = swap(own, "hi")
    over_c = swap(own, "core")
    top = swap(over_y[:half], "col")
    low = swap(over_x[half:], "hi")
    over_xc = swap(over_x, "core")
    over_yc = swap(over_y, "core")
    over_xy = jnp.concatenate([top, low], 0)
    over_xyc = swap(over_xy, "core")
    return [own, over_c, over_y, over_yc, over_x, over_xc, over_xy, over_xyc]


def scatter8(parts):
    half = parts[0].shape[0] // 2
    low = [p.astype(BF16) for p in parts]

    def core_sum(j):
        return low[j].astype(F32) + swap(low[j + 1], "core").astype(F32)

    diag = core_sum(6).astype(BF16)
    from_x = swap(diag[:half], "col").astype(F32)
    from_y = swap(diag[half:], "hi").astype(F32)
    sum_x = core_sum(4)
    sum_y = core_sum(2)
    first_x = swap(sum_x[:half].astype(BF16), "col")
    first_y = swap(sum_y[half:].astype(BF16), "hi")
    last_x = swap((sum_x[half:] + from_y).astype(BF16), "col")
    last_y = swap((sum_y[:half] + from_x).astype(BF16), "hi")
    own = core_sum(0)
    got_x = jnp.concatenate([first_x, last_x], 0).astype(F32)
    got_y = jnp.concatenate([last_y, first_y], 0).astype(F32)
    return own + got_x + got_y


def walk(value, mask_of, up):
    rows = lax.axis_size("row")
    pairs = [(i, i + 1) if up else (i + 1, i) for i in range(rows - 1)]
    total = None
    now = value
    for hop in range(1, rows):
        now = lax.ppermute(now, "row", pairs)
        term = mask_of(hop)[:, None, None, None] * now.astype(F32)
        total = term if total is None else total + term
    return total


def ordered(ref, me, lanes=slice(None)):
    return jnp.concatenate([ref[p ^ me, 0, :, lanes] for p in range(8)], 0)


def put_ordered(ref, me, value, lanes=slice(None)):
    sub = value.shape[0] // 8
    for p in range(8):
        ref[p ^ me, 0, :, lanes] = value[p * sub : (p + 1) * sub]


def phi(aligned, feat, rows):
    both = dot(aligned, feat) + rows[0:1, :]
    a, b = both[:, :FPAD], both[:, FPAD:]
    return a, b, a * b * rows[1:2, :FPAD]


def phi_back(a, b, grad, feat, rows):
    scaled = grad * rows[1:2, :FPAD]
    return dot_t((scaled * b).astype(BF16), feat[:, :FPAD]) + dot_t(
        (scaled * a).astype(BF16), feat[:, FPAD:]
    )


def put_state(ref, head, state, norm):
    ref[0, head] = state[:FROWS].astype(BF16)
    high = norm.astype(BF16)
    low = (norm - high.astype(F32)).astype(BF16)
    ref[0, head, FEAT : FEAT + 1, :] = high[:, :128]
    ref[0, head, FEAT + 1 : FEAT + 2, :] = low[:, :128]
    ref[0, head, FEAT + 2 : FEAT + 3, :] = high[:, 128:]
    ref[0, head, FEAT + 3 : FEAT + 4, :] = low[:, 128:]


def get_state(ref, head):
    whole = ref[0, head]
    state = jnp.concatenate([whole, jnp.zeros((FPAD - FROWS, 128), F32)], 0)
    norm = jnp.concatenate(
        [
            whole[FEAT : FEAT + 1] + whole[FEAT + 1 : FEAT + 2],
            whole[FEAT + 2 : FEAT + 3] + whole[FEAT + 3 : FEAT + 4],
        ],
        1,
    )
    return state.astype(BF16), norm


def align4(qk, align_ref):
    out = dot(qk, align_ref[...]).astype(BF16)
    return [out[:, i * 128 : (i + 1) * 128] for i in range(4)]


def visible(cols, seg_row):
    t = cols.shape[0]
    causal = lax.broadcasted_iota(jnp.int32, (t, t), 0) >= lax.broadcasted_iota(jnp.int32, (t, t), 1)
    return causal & (cols[:, 0:1] == seg_row)


def state_kernel(me_ref, qkv_ref, cols_ref, feat_ref, rows_ref, align_ref, out_ref):
    me = me_ref[0]
    qk = ordered(qkv_ref, me, slice(256, 384))
    v = ordered(qkv_ref, me, slice(0, 256))
    last = cols_ref[0][:, 2:3]
    parts = align4(qk, align_ref)
    for head in range(2):
        _, _, feat = phi(parts[2 + head], feat_ref[...], rows_ref[...])
        feat = feat * last
        state = t_dot(feat.astype(BF16), v[:, head * 128 : (head + 1) * 128])
        put_state(out_ref, head, state, jnp.sum(feat, 0, keepdims=True))


def intra_kernel(me_ref, qkv_ref, cols_ref, seg_ref, align_ref, num_ref, den_ref):
    me = me_ref[0]
    qk = ordered(qkv_ref, me, slice(256, 384))
    v = ordered(qkv_ref, me, slice(0, 256))
    see = visible(cols_ref[0], seg_ref[0])
    parts = align4(qk, align_ref)
    den_ref[0] = jnp.zeros(den_ref.shape[1:], F32)
    for head in range(2):
        z = dot_t(parts[head], parts[2 + head])
        w = jnp.where(see, 1.0 + z * (0.25 + 0.03125 * z), 0.0)
        num_ref[0, :, head * 128 : (head + 1) * 128] = dot(
            w.astype(BF16), v[:, head * 128 : (head + 1) * 128]
        )
        den_ref[0, :, head : head + 1] = jnp.sum(w, 1, keepdims=True)


def output_kernel(
    me_ref, qkv_ref, cols_ref, feat_ref, rows_ref, align_ref, num_ref, den_ref, state_ref, o_ref, all_ref
):
    me = me_ref[0]
    qk = ordered(qkv_ref, me, slice(256, 384))
    use = cols_ref[0][:, 1:2]
    parts = align4(qk, align_ref)
    all_ref[0] = jnp.zeros(all_ref.shape[1:], F32)
    for head in range(2):
        lanes = slice(head * 128, (head + 1) * 128)
        _, _, feat = phi(parts[head], feat_ref[...], rows_ref[...])
        state, norm = get_state(state_ref, head)
        num = num_ref[0, :, lanes] + use * dot(feat.astype(BF16), state)
        den = den_ref[0, :, head : head + 1] + use * jnp.sum(feat * norm, 1, keepdims=True)
        all_ref[0, :, head : head + 1] = den
        put_ordered(o_ref, me, (num / den).astype(BF16), lanes)


def back_parts(me, o_ref, do_ref, den_ref, head):
    lanes = slice(head * 128, (head + 1) * 128)
    inv = 1.0 / den_ref[0, :, head : head + 1]
    do = ordered(do_ref, me, lanes).astype(F32)
    o = ordered(o_ref, me, lanes).astype(F32)
    return (do * inv).astype(BF16), -jnp.sum(do * o, 1, keepdims=True) * inv


def back_state_kernel(
    me_ref, qkv_ref, cols_ref, feat_ref, rows_ref, align_ref, o_ref, do_ref, den_ref, out_ref
):
    me = me_ref[0]
    qk = ordered(qkv_ref, me, slice(256, 384))
    use = cols_ref[0][:, 1:2]
    parts = align4(qk, align_ref)
    for head in range(2):
        g, c = back_parts(me, o_ref, do_ref, den_ref, head)
        _, _, feat = phi(parts[head], feat_ref[...], rows_ref[...])
        feat = feat * use
        put_state(out_ref, head, t_dot(feat.astype(BF16), g), jnp.sum(feat * c, 0, keepdims=True))


def back_intra_kernel(
    me_ref, qkv_ref, cols_ref, seg_ref, feat_ref, rows_ref, align_ref, o_ref, do_ref, den_ref, state_ref,
    dq_ref, dk_ref, dv_ref,
):
    me = me_ref[0]
    qk = ordered(qkv_ref, me, slice(256, 384))
    v = ordered(qkv_ref, me, slice(0, 256))
    use = cols_ref[0][:, 1:2]
    see = visible(cols_ref[0], seg_ref[0])
    parts = align4(qk, align_ref)
    for head in range(2):
        lanes = slice(head * 128, (head + 1) * 128)
        g, c = back_parts(me, o_ref, do_ref, den_ref, head)
        z = dot_t(parts[head], parts[2 + head])
        w = jnp.where(see, 1.0 + z * (0.25 + 0.03125 * z), 0.0)
        dv_ref[0, :, lanes] = t_dot(w.astype(BF16), g)
        dw = dot_t(g, v[:, lanes]) + c
        dz = jnp.where(see, dw * (0.25 + 0.0625 * z), 0.0).astype(BF16)
        a, b, _ = phi(parts[head], feat_ref[...], rows_ref[...])
        state, norm = get_state(state_ref, head)
        grad = use * (dot_t(g, state) + c * norm)
        dq_ref[0, :, lanes] = dot(dz, parts[2 + head]) + phi_back(a, b, grad, feat_ref[...], rows_ref[...])
        dk_ref[0, :, lanes] = t_dot(dz, parts[head])


def back_output_kernel(
    me_ref, qkv_ref, cols_ref, feat_ref, rows_ref, align_ref, state_ref, dq_ref, dk_ref, dv_ref, out_ref
):
    me = me_ref[0]
    qk = ordered(qkv_ref, me, slice(256, 384))
    v = ordered(qkv_ref, me, slice(0, 256))
    last = cols_ref[0][:, 2:3]
    parts = align4(qk, align_ref)
    packed = None
    for head in range(2):
        lanes = slice(head * 128, (head + 1) * 128)
        a, b, feat = phi(parts[2 + head], feat_ref[...], rows_ref[...])
        state, norm = get_state(state_ref, head)
        grad = last * (dot_t(v[:, lanes], state) + norm)
        dk = dk_ref[0, :, lanes] + phi_back(a, b, grad, feat_ref[...], rows_ref[...])
        dv = dv_ref[0, :, lanes] + last * dot(feat.astype(BF16), state)
        put_ordered(out_ref, me, dv.astype(BF16), lanes)
        place = align_ref[...]
        term = dot_t(dq_ref[0, :, lanes].astype(BF16), place[:, head * 128 : (head + 1) * 128]) + dot_t(
            dk.astype(BF16), place[:, (2 + head) * 128 : (3 + head) * 128]
        )
        packed = term if packed is None else packed + term
    put_ordered(out_ref, me, packed.astype(BF16), slice(256, 384))


def attention_call(kernel, me, ins, kinds, outs):
    def spec(a, kind):
        if kind == "s":
            return pl.BlockSpec((8, 1) + a.shape[2:], lambda i, m: (0, i, 0, 0))
        rest = len(a.shape) - 1
        if kind == "q":
            return pl.BlockSpec((1,) + a.shape[1:], lambda i, m: (i,) + (0,) * rest)
        return pl.BlockSpec(a.shape, lambda i, m: (0,) * (rest + 1))

    seqs = ins[0].shape[1]
    return pl.pallas_call(
        kernel,
        out_shape=[jax.ShapeDtypeStruct(a.shape, a.dtype) for a, _ in outs],
        grid_spec=pltpu.PrefetchScalarGridSpec(
            num_scalar_prefetch=1,
            grid=(seqs,),
            in_specs=[spec(a, k) for a, k in zip(ins, kinds)],
            out_specs=[spec(a, k) for a, k in outs],
        ),
        compiler_params=pltpu.CompilerParams(
            dimension_semantics=("arbitrary",), vmem_limit_bytes=48 * 1024 * 1024
        ),
        name=kernel.__name__,
    )(me, *ins)


def pick(cond, a, b):
    return jnp.where(cond, a, b)


def half_columns(gate, up, which, n_main, n_mid):
    mid = slice(n_main, n_main + 2 * n_mid)
    main = slice(0, n_main) if which == 0 else slice(n_main + 2 * n_mid, None)
    part = slice(0, n_mid) if which == 0 else slice(n_mid, None)
    return jnp.concatenate([gate[:, main], up[:, main], gate[:, mid][:, part], up[:, mid][:, part]], 1)


def body(inputs, segments, qw, kw, vw, pw, again, gw, uw, dw, fgain, upstream):
    hi, core, row, col = (lax.axis_index(a) for a in ("hi", "core", "row", "col"))
    rows = lax.axis_size("row")
    shards = 2 * rows
    me3 = (4 * col + 2 * hi + core).astype(jnp.int32)
    me = me3[None]
    seqs, sub = inputs.shape[0], inputs.shape[3]
    tokens = seqs * sub
    span = 8 * sub
    n_rows = qw.shape[0]
    is0 = col == 0
    ff = gw.shape[1]
    n_mid = 64
    n_main = ff // 2 - n_mid
    feat_c, rows_c, align_c = feature_constants()

    x = inputs.reshape(tokens, D)
    xs = jnp.stack(gather8(x))
    ups = jnp.stack(gather8(upstream.reshape(tokens, D)))

    gain_one = again.astype(F32)[:, None]
    seg_own = segments.reshape(seqs, 4 * sub)
    seg_other = swap(seg_own, "col")
    seg = jnp.concatenate([pick(is0, seg_own, seg_other), pick(is0, seg_other, seg_own)], 1)
    last_seg = seg[:, -1]

    def by_dest(w, scale):
        return (w.astype(F32) * scale).astype(BF16).reshape(n_rows, 8, -1)

    extra = jnp.zeros((n_rows, PAYLOAD - 320), F32)
    extra = extra.at[:, 0].set(fgain.astype(F32))
    extra = extra.at[:seqs, 1].set((last_seg // 128).astype(F32))
    extra = extra.at[:seqs, 2].set((last_seg % 128).astype(F32))
    payload = jnp.concatenate(
        [
            by_dest(vw, gain_one),
            by_dest(qw, gain_one),
            by_dest(kw, gain_one),
            jnp.broadcast_to(extra.astype(BF16)[:, None], (n_rows, 8, PAYLOAD - 320)),
        ],
        2,
    ).transpose(1, 0, 2)
    payload = lax.all_to_all(payload, GROUP, split_axis=0, concat_axis=0, tiled=True)
    gathered = lax.all_gather(payload, "row", axis=0, tiled=False)
    w_qkv = (
        gathered.reshape(rows, 4, 2, n_rows, PAYLOAD).transpose(1, 0, 2, 3, 4).reshape(D, PAYLOAD)
    )
    gain_two = w_qkv[:, 320].astype(F32)[None, :]
    lasts = gathered[:, 0, :seqs, 321:323].astype(F32)
    lasts = lasts[:, :, 0] * 128.0 + lasts[:, :, 1]

    shard_pairs = [(s, (s % rows) * 2 + s // rows) for s in range(shards)]
    moved = lax.ppermute(pw, ("row", "col"), shard_pairs)
    w_proj = lax.all_gather(moved, "row", axis=0, tiled=True)

    mine = pick(is0, half_columns(gw, uw, 0, n_main, n_mid), half_columns(gw, uw, 1, n_main, n_mid))
    theirs = pick(is0, half_columns(gw, uw, 1, n_main, n_mid), half_columns(gw, uw, 0, n_main, n_mid))
    got = swap(theirs, "col")
    gu_rows = jnp.concatenate([pick(is0, mine, got), pick(is0, got, mine)], 0)
    w_gu = lax.all_gather(gu_rows, "row", axis=0, tiled=True)
    down0 = dw[: n_main + n_mid]
    down1 = jnp.concatenate([dw[n_main + 2 * n_mid :], dw[n_main + n_mid : n_main + 2 * n_mid]], 0)
    d_mine, d_theirs = pick(is0, down0, down1), pick(is0, down1, down0)
    d_got = swap(d_theirs, "col")
    d_cols = jnp.stack([pick(is0, d_mine, d_got), pick(is0, d_got, d_mine)])
    w_down = lax.all_gather(d_cols, "row", axis=0, tiled=True)
    w_down = w_down.transpose(1, 0, 2).reshape(ff // 2, D)

    segf = seg.astype(F32)
    before = jnp.where(row > 0, lasts[jnp.maximum(row - 1, 0)], -1.0)
    here = lasts[row]
    use_in = (segf == before[:, None]).astype(F32)
    is_last = (segf == here[:, None]).astype(F32)
    cols = jnp.stack([segf, use_in, is_last] + [segf] * 5, -1)
    seg_row = segf[:, None, :]

    def mask_up(hop):
        other = lasts[jnp.maximum(row - hop, 0)]
        return ((other == before) & (row >= hop)).astype(F32)

    def mask_down(hop):
        other = lasts[jnp.minimum(row + hop - 1, rows - 1)]
        return ((other == here) & (row + hop < rows)).astype(F32)

    xf = xs.reshape(8 * tokens, D)
    xf32 = xf.astype(F32)
    inv_one = lax.rsqrt(jnp.mean(xf32 * xf32, -1, keepdims=True) + EPS)
    qkv = (dot(xf, w_qkv) * inv_one).astype(BF16).reshape(8, seqs, sub, PAYLOAD)
    sds = jax.ShapeDtypeStruct
    st = sds((seqs, 2, FROWS, 128), BF16)
    (state,) = attention_call(
        state_kernel, me, [qkv, cols, feat_c, rows_c, align_c], "sqccc", [(st, "q")]
    )
    num, den_in = attention_call(
        intra_kernel, me, [qkv, cols, seg_row, align_c], "sqqc",
        [(sds((seqs, span, 256), F32), "q"), (sds((seqs, span, 8), F32), "q")],
    )
    state_in = walk(state, mask_up, True)
    o, den = attention_call(
        output_kernel, me, [qkv, cols, feat_c, rows_c, align_c, num, den_in, state_in], "sqcccqqq",
        [(sds((8, seqs, sub, 256), BF16), "s"), (sds((seqs, span, 8), F32), "q")],
    )
    of = o.reshape(8 * tokens, 256)
    att = dot(of, w_proj).reshape(8, tokens, D)
    residual = x.astype(F32) + scatter8([att[j] for j in range(8)])

    inv_two = lax.rsqrt(jnp.mean(residual * residual, -1, keepdims=True) + EPS)
    normed_two = residual * inv_two
    a2 = jnp.stack(gather8((normed_two * gain_two).astype(BF16))).reshape(8 * tokens, D)
    up_rows = ups.reshape(8 * tokens, D)
    gu = dot(a2, w_gu)
    dh = dot_t(up_rows, w_down)
    g = jnp.concatenate([gu[:, :n_main], gu[:, 2 * n_main : 2 * n_main + n_mid]], 1)
    u = jnp.concatenate([gu[:, n_main : 2 * n_main], gu[:, 2 * n_main + n_mid :]], 1)
    sg = jax.nn.sigmoid(g)
    silu = g * sg
    h = (silu * u).astype(BF16)
    dg = (dh * u * (sg * (1.0 + g * (1.0 - sg)))).astype(BF16)
    du = (dh * silu).astype(BF16)
    dgu = jnp.concatenate([dg[:, :n_main], du[:, :n_main], dg[:, n_main:], du[:, n_main:]], 1)
    da2 = dot_t(dgu, w_gu).reshape(8, tokens, D)
    grad_a2 = scatter8([da2[j] for j in range(8)])
    down_out = dot(h, w_down).reshape(8, tokens, D)
    outputs = (residual + scatter8([down_out[j] for j in range(8)])).astype(BF16)
    down_g = t_dot(h, up_rows)
    gu_g = t_dot(a2, dgu)
    gain_two_part = jnp.sum(gu_g * w_gu.astype(F32), 1)

    down_g = down_g.astype(BF16).reshape(ff // 2, rows, 2, D // shards).transpose(1, 2, 0, 3)
    down_g = lax.psum_scatter(down_g, "row", scatter_dimension=0, tiled=False)
    gu_g = lax.psum_scatter(gu_g.astype(BF16), "row", scatter_dimension=0, tiled=True)

    dy = upstream.reshape(tokens, D).astype(F32)
    e = grad_a2 * gain_two
    grad_r = dy + inv_two * (e - normed_two * jnp.mean(e * normed_two, -1, keepdims=True))
    datt = jnp.stack(gather8(grad_r.astype(BF16))).reshape(8 * tokens, D)
    do = dot_t(datt, w_proj).astype(BF16).reshape(8, seqs, sub, 256)
    proj_g = t_dot(of, datt).astype(BF16)
    proj_g = lax.psum_scatter(proj_g, "row", scatter_dimension=0, tiled=True)
    project_grad = lax.ppermute(proj_g, ("row", "col"), [(b, a) for a, b in shard_pairs]).astype(F32)

    (dstate,) = attention_call(
        back_state_kernel, me, [qkv, cols, feat_c, rows_c, align_c, o, do, den], "sqcccssq", [(st, "q")]
    )
    part = sds((seqs, span, 256), F32)
    dq, dk, dv = attention_call(
        back_intra_kernel, me, [qkv, cols, seg_row, feat_c, rows_c, align_c, o, do, den, state_in],
        "sqqcccssqq", [(part, "q")] * 3,
    )
    dstate_out = walk(dstate, mask_down, False)
    (dqkv,) = attention_call(
        back_output_kernel, me, [qkv, cols, feat_c, rows_c, align_c, dstate_out, dq, dk, dv], "sqcccqqqq",
        [(sds((8, seqs, sub, PAYLOAD), BF16), "s")],
    )
    dqkv = dqkv.reshape(8 * tokens, PAYLOAD)
    f_part = dot_t(dqkv, w_qkv).reshape(8, tokens, D)
    f = scatter8([f_part[j] for j in range(8)])
    inv_own = inv_one[:tokens]
    normed_one = x.astype(F32) * inv_own
    inputs_grad = grad_r + inv_own * (f - normed_one * jnp.mean(f * normed_one, -1, keepdims=True))

    scaled = (dqkv.astype(F32) * inv_one).astype(BF16)
    qkv_g = t_dot(xf, scaled)
    lane = lax.broadcasted_iota(jnp.int32, (1, PAYLOAD), 1)
    qkv_g = jnp.where(lane == 320, gain_two_part[:, None], qkv_g).astype(BF16)
    qkv_g = qkv_g.reshape(4, rows, 2, n_rows, PAYLOAD).transpose(1, 0, 2, 3, 4)
    qkv_g = lax.psum_scatter(qkv_g, "row", scatter_dimension=0, tiled=False)
    qkv_g = lax.all_to_all(
        qkv_g.reshape(8, n_rows, PAYLOAD), GROUP, split_axis=0, concat_axis=0, tiled=True
    ).astype(F32)
    per_row = qkv_g.transpose(1, 0, 2)
    v_g = per_row[:, :, :256].reshape(n_rows, -1)
    q_g = per_row[:, :, 256:288].reshape(n_rows, -1)
    k_g = per_row[:, :, 288:320].reshape(n_rows, -1)
    forward_grad = jnp.sum(per_row[:, :, 320], 1) / fgain.astype(F32)
    attend_grad = (
        jnp.sum(v_g * vw.astype(F32), 1) + jnp.sum(q_g * qw.astype(F32), 1) + jnp.sum(k_g * kw.astype(F32), 1)
    )

    d_keep, d_send = pick(is0, down_g[0], down_g[1]), pick(is0, down_g[1], down_g[0])
    d_got = swap(d_send, "col")
    d0, d1 = pick(is0, d_keep, d_got).astype(F32), pick(is0, d_got, d_keep).astype(F32)
    down_grad = jnp.concatenate([d0, d1[n_main:], d1[:n_main]], 0)
    block = gu_g.shape[0] // 2
    g_keep = pick(is0, gu_g[:block], gu_g[block:])
    g_got = swap(pick(is0, gu_g[block:], gu_g[:block]), "col")
    g0, g1 = pick(is0, g_keep, g_got).astype(F32), pick(is0, g_got, g_keep).astype(F32)
    m = 2 * n_main
    gate_grad = jnp.concatenate(
        [g0[:, :n_main], g0[:, m : m + n_mid], g1[:, m : m + n_mid], g1[:, :n_main]], 1
    )
    up_grad = jnp.concatenate(
        [g0[:, n_main:m], g0[:, m + n_mid :], g1[:, m + n_mid :], g1[:, n_main:m]], 1
    )
    return (
        outputs.reshape(inputs.shape),
        inputs_grad.reshape(inputs.shape),
        q_g * gain_one,
        k_g * gain_one,
        v_g * gain_one,
        project_grad,
        attend_grad,
        gate_grad,
        up_grad,
        down_grad,
        forward_grad,
    )


def solution(mesh):
    heads, shards = mesh.devices.shape
    fine = Mesh(mesh.devices.reshape(heads // 2, 2, shards // 2, 2), ("hi", "core", "row", "col"))
    h, s = ("hi", "core"), ("row", "col")
    every = P(h + s)
    tokens = P(None, s, h)
    return jax.shard_map(
        body,
        mesh=fine,
        in_specs=(
            tokens, P(None, s), every, every, every, every, every, P(s, h), P(s, h), P(h, s), every, tokens,
        ),
        out_specs=(
            tokens, tokens, every, every, every, every, every, P(s, h), P(s, h), P(h, s), every,
        ),
        check_vma=False,
    )
```

time: 3420 us -> 837 us (0.24)
  waiting for transfers between devices: 2590 us -> 307 us
  blocking collectives: 267 us -> 11.2 us
  matrix products: 254 us -> 135 us
  starting transfers between devices: 19.4 us -> 93.3 us
  local copies, waits for them, and re-layouts: 202 us -> 147 us
  Pallas kernels: 0 us -> 44 us
    reduce_scatter x8 -> x3, waiting for transfers between devices: 1310 us -> 77.3 us  [the longest x1 77.3 us: body(): lax.psum_scatter(gu_g.astype(BF16), 'row', scatter_dimension=0, tiled=True)]
    all_gather x12 -> x4, waiting for transfers between devices: 1050 us -> 0.01 us  [the longest x1 0.01 us: body(): gathered = lax.all_gather(payload, 'row', axis=0, tiled=False)]
    ppermute x0 -> x85, waiting for transfers between devices: none -> 209 us  [the longest x77 135 us: swap(): return lax.ppermute(value, axis, [(0, 1), (1, 0)])]
    unnamed x24 -> x9, waiting for transfers between devices: 189 us -> 20.8 us
    unnamed x4 -> x0, blocking collectives: 135 us -> none
    dot_general x35 -> x12, matrix products: 254 us -> 135 us  [the longest x4 49.5 us: t_dot(): lax.dot_general(a, b, (((0,), (0,)), ((), ())), preferred_element_type=F32)]
    ppermute x0 -> x85, starting transfers between devices: none -> 88.4 us  [the longest x77 57.8 us: swap(): return lax.ppermute(value, axis, [(0, 1), (1, 0)])]
    all_gather x2 -> x0, blocking collectives: 77.4 us -> none  [the longest x1 43.1 us: carried_in(): everything = jax.tree.map(lambda part: lax.all_gather(part, axis), value)]
  transfers between devices with their start and end apart: 27 -> 94, of which waited for: 24 -> 30; matrix products, arithmetic and copies ran while one was open for 13% -> 31% of each run, Pallas kernels for 0% -> 5%
where the time goes in v1:
time: 837 us; the launch traced here: 829 us
  waiting for transfers between devices  307 us (37%)
  local copies, waits for them, and re-layouts  147 us (18%)
  matrix products  135 us (16%)
  starting transfers between devices  93.3 us (11%)
  other arithmetic  74.7 us (9%)
  Pallas kernels  44 us (5%)
  between operations  16.2 us (2%)
  blocking collectives  11.2 us (1%)
    ppermute x77, waiting for transfers between devices, swap(): return lax.ppermute(value, axis, [(0, 1), (1, 0)])  135 us
    reduce_scatter x1, waiting for transfers between devices, body(): lax.psum_scatter(gu_g.astype(BF16), 'row', scatter_dimension=0, tiled=True)  77.3 us
    unnamed x188, local copies, waits for them, and re-layouts  65.8 us
    ppermute x77, starting transfers between devices, swap(): return lax.ppermute(value, axis, [(0, 1), (1, 0)])  57.8 us
    dot_general x4, matrix products, t_dot(): lax.dot_general(a, b, (((0,), (0,)), ((), ())), preferred_element_type=F32)  49.5 us
    ppermute x6, waiting for transfers between devices, walk(): now = lax.ppermute(now, 'row', pairs)  47.3 us
    dot_general x4, matrix products, dot_t(): lax.dot_general(a, b, (((1,), (1,)), ((), ())), preferred_element_type=F32)  44.6 us
    pallas_call x6, Pallas kernels, attention_call(): pl.pallas_call(kernel, out_shape=[jax.ShapeDtypeStruct(a.shape, a.dtype)...  44 us
  transfers between devices with their start and end apart: 94, of which 30 were waited for; matrix products, arithmetic and copies ran while one was open for 31% of the time, Pallas kernels for 5%

profile of v1, /device:TPU:16, one launch (start us, length us, event | category | flops | bytes accessed | tf_op | source)
XLA Modules:
  0.0 829.1 jit_solution(15897044337116891874)
XLA Ops:
  23.5 11.2 %all_to_all.10 = bf16[8,64,384]{2,1,0:T(8,128)(2,1)} all-to-all(bf16[8,64,384]{2,1,0:T(8,128)(2,1)S(1)} %copy.269), channel_id=1, replica_groups=mesh['hi'=2,'core'=2,'row'=4,'col'=2] {'hi','core','col'}, dimensions={0} | all-to-all | bytes 786432 | tf_op jit(solution)/shard_map/all_to_all | solution.py:377
  40.8 17.4 %collective-permute-done.12 = bf16[64,2048]{1,0:T(8,128)(2,1)} collective-permute-done((bf16[64,2048]{1,0:T(8,128)(2,1)}, bf16[64,2048]{1,0:T(8,128)(2,1)}, u32[]{:S(2)}, u32[]{:S(2)}) %collective-permute-start.12) | collective-permute-done | bytes 262176 | tf_op jit(solution)/shard_map/ppermute | solution.py:387
  109.9 8.9 %multiply_convert_fusion.4 = bf16[2048,384]{1,0:T(8,128)(2,1)S(1)} fusion(bf16[2048,2048]{1,0:T(8,128)(2,1)} %bitcast.225, bf16[2048,384]{1,0:T(8,128)(2,1)S(1)} %bitcast.232, f32[2048]{0:T(1024)S(1)} %bitcast.253), kind=kOutput, calls=%fused_computation.17 | convolution fusion | flops 3222798336 | bytes 11542528 | tf_op jit(solution)/shard_map/dot_general | solution.py:59
  122.2 8.9 %stack.130.cols_ref = f32[4,512,8]{2,1,0:T(8,128)S(1)} concatenate(f32[4,512,1]{2,1,0:T(8,128)} %copy.272, f32[4,512,1]{2,1,0:T(8,128)} %copy.273, f32[4,512,1]{2,1,0:T(8,128)} %copy.274, f32[4,512,1]{2,1,0:T(8,128)} %copy.272, f32[4,512,1]{2,1,0:T(8,128)} %copy.272, f32[4,512,1]{2,1,0:T(8,128)} %copy.272, f32[4,512,1]{2,1,0:T(8,128)} %copy.272, f32[4,512,1]{2,1,0:T(8,128)} %copy.272), dimensions={2} | concatenate | bytes 131072 | tf_op jit(solution)/shard_map/stack | solution.py:408
  142.2 19.4 %collective-permute-done.9 = bf16[4,2,160,128]{3,2,1,0:T(8,128)(2,1)S(1)} collective-permute-done((bf16[4,2,160,128]{3,2,1,0:T(8,128)(2,1)S(1)}, bf16[4,2,160,128]{3,2,1,0:T(8,128)(2,1)S(1)}, u32[]{:S(2)}, u32[]{:S(2)}) %collective-permute-start.9) | collective-permute-done | bytes 327712 | tf_op jit(solution)/shard_map/ppermute | solution.py:116
  167.5 8.1 collective-permute-done.10
  194.9 7.4 output_kernel.1
  222.1 9.3 %collective-permute-done.17 = bf16[128,2048]{1,0:T(8,128)(2,1)S(1)} collective-permute-done((bf16[128,2048]{1,0:T(8,128)(2,1)S(1)}, bf16[128,2048]{1,0:T(8,128)(2,1)S(1)}, u32[]{:S(2)}, u32[]{:S(2)}) %collective-permute-start.17) | collective-permute-done | bytes 524320 | tf_op jit(solution)/shard_map/ppermute | solution.py:71
  243.3 10.0 %collective-permute-done.18 = bf16[128,2048]{1,0:T(8,128)(2,1)S(1)} collective-permute-done((bf16[128,2048]{1,0:T(8,128)(2,1)S(1)}, bf16[128,2048]{1,0:T(8,128)(2,1)S(1)}, u32[]{:S(2)}, u32[]{:S(2)}) %collective-permute-start.18) | collective-permute-done | bytes 524320 | tf_op jit(solution)/shard_map/ppermute | solution.py:71
  265.2 15.4 %collective-permute-done.24 = bf16[256,2048]{1,0:T(8,128)(2,1)} collective-permute-done((bf16[256,2048]{1,0:T(8,128)(2,1)}, bf16[256,2048]{1,0:T(8,128)(2,1)}, u32[]{:S(2)}, u32[]{:S(2)}) %collective-permute-start.24) | collective-permute-done | bytes 1048608 | tf_op jit(solution)/shard_map/ppermute | solution.py:71
  299.6 18.9 %fusion.64 = f32[2048,1408]{0,1:T(8,128)} fusion(bf16[2048,2048]{1,0:T(8,128)(2,1)} %bitcast.247, bf16[2048,1408]{0,1:T(8,128)(2,1)} %all-gather.8.cloned.1.call-done), kind=kOutput, calls=%fused_computation.243 | convolution fusion | flops 11811160064 | bytes 25690112 | tf_op jit(solution)/shard_map/dot_general | solution.py:59
  318.5 7.8 fusion.43
  327.5 14.3 %multiply_convert_fusion.1 = (bf16[2048,704]{0,1:T(8,128)(2,1)}, bf16[2048,704]{0,1:T(8,128)(2,1)}, bf16[2048,704]{0,1:T(8,128)(2,1)}) fusion(f32[2048,64]{0,1:T(8,128)S(1)} %get-tuple-element.169, f32[2048,640]{0,1:T(8,128)} %get-tuple-element.167, f32[2048,64]{0,1:T(8,128)S(1)} %get-tuple-element.168, f32[2048,640]{0,1:T(8,128)S(1)} %get-tuple-element.166, ...), kind=kOutput, calls=%fused_computation.10 | convolution fusion | flops 5930090496 | bytes 31457280 | tf_op jit(solution)/shard_map/dot_general | solution.py:63
  345.8 18.3 %convolution_convert_fusion.1 = bf16[2048,2048]{1,0:T(8,128)(2,1)} fusion(bf16[2048,1408]{0,1:T(8,128)(2,1)} %all-gather.8.cloned.1.call-done, bf16[2048,64]{0,1:T(8,128)(2,1)S(1)} %slice.634, bf16[2048,64]{0,1:T(8,128)(2,1)S(1)} %slice.633, bf16[2048,640]{0,1:T(8,128)(2,1)S(1)} %slice.632, bf16[2048,640]{0,1:T(8,128)(2,1)S(1)} %slice.631), kind=kOutput, calls=%fused_computation.3 | convolution fusion | flops 11838423040 | bytes 19922944 | tf_op jit(solution)/shard_map/dot_general | solution.py:63
  369.2 9.4 %convolution_convert_fusion.2 = bf16[2048,2048]{1,0:T(8,128)(2,1)S(1)} fusion(bf16[2048,704]{0,1:T(8,128)(2,1)} %get-tuple-element.164, bf16[704,2048]{1,0:T(8,128)(2,1)S(1)} %bitcast.231), kind=kOutput, calls=%fused_computation.4 | convolution fusion | flops 5909774336 | bytes 14155776 | tf_op jit(solution)/shard_map/dot_general | solution.py:59
  393.7 6.8 collective-permute-done.55
  413.4 10.9 %collective-permute-done.53 = bf16[128,2048]{1,0:T(8,128)(2,1)S(1)} collective-permute-done((bf16[128,2048]{1,0:T(8,128)(2,1)S(1)}, bf16[128,2048]{1,0:T(8,128)(2,1)S(1)}, u32[]{:S(2)}, u32[]{:S(2)}) %collective-permute-start.53) | collective-permute-done | bytes 524320 | tf_op jit(solution)/shard_map/ppermute | solution.py:71
  426.3 9.2 %collective-permute-done.56 = bf16[128,2048]{1,0:T(8,128)(2,1)S(1)} collective-permute-done((bf16[128,2048]{1,0:T(8,128)(2,1)S(1)}, bf16[128,2048]{1,0:T(8,128)(2,1)S(1)}, u32[]{:S(2)}, u32[]{:S(2)}) %collective-permute-start.56) | collective-permute-done | bytes 524320 | tf_op jit(solution)/shard_map/ppermute | solution.py:71
  438.4 8.3 %collective-permute-done.35 = bf16[128,2048]{1,0:T(8,128)(2,1)S(1)} collective-permute-done((bf16[128,2048]{1,0:T(8,128)(2,1)S(1)}, bf16[128,2048]{1,0:T(8,128)(2,1)S(1)}, u32[]{:S(2)}, u32[]{:S(2)}) %collective-permute-start.35) | collective-permute-done | bytes 524320 | tf_op jit(solution)/shard_map/ppermute | solution.py:71
  446.7 10.5 %collective-permute-done.38 = bf16[128,2048]{1,0:T(8,128)(2,1)S(1)} collective-permute-done((bf16[128,2048]{1,0:T(8,128)(2,1)S(1)}, bf16[128,2048]{1,0:T(8,128)(2,1)S(1)}, u32[]{:S(2)}, u32[]{:S(2)}) %collective-permute-start.38) | collective-permute-done | bytes 524320 | tf_op jit(solution)/shard_map/ppermute | solution.py:71
  467.0 10.8 %convolution_convert_fusion.4 = bf16[704,2048]{1,0:T(8,128)(2,1)} fusion(bf16[2048,704]{0,1:T(8,128)(2,1)S(1)} %copy-done.65, bf16[2048,2048]{1,0:T(8,128)(2,1)} %bitcast.57), kind=kOutput, calls=%fused_computation.14 | convolution fusion | flops 5907021824 | bytes 14155776 | tf_op jit(solution)/shard_map/dot_general | solution.py:67
  477.9 7.9 reshape.582
  498.3 6.9 collective-permute-done.66
  526.9 19.6 %collective-permute-done.69 = bf16[4,2,160,128]{3,2,1,0:T(8,128)(2,1)} collective-permute-done((bf16[4,2,160,128]{3,2,1,0:T(8,128)(2,1)S(1)}, bf16[4,2,160,128]{3,2,1,0:T(8,128)(2,1)}, u32[]{:S(2)}, u32[]{:S(2)}) %collective-permute-start.69) | collective-permute-done | bytes 327712 | tf_op jit(solution)/shard_map/ppermute | solution.py:116
  564.4 22.8 %fusion.42 = (bf16[2048,1408]{0,1:T(8,128)(2,1)}, bf16[2048]{0:T(1024)(128)(2,1)}) fusion(bf16[2048,1408]{0,1:T(8,128)(2,1)} %all-gather.8.cloned.1.call-done, bf16[2048,2048]{1,0:T(8,128)(2,1)} %bitcast.248, bf16[2048,64]{0,1:T(8,128)(2,1)} %copy-done.53, bf16[2048,64]{0,1:T(8,128)(2,1)S(1)} %copy-done.52, bf16[2048,640]{0,1:T(8,128)(2,1)} %copy-done.39, ...), kind=kOutput, calls=%fused_computation.221 | convolution fusion | flops 11845761024 | bytes 25694208 | tf_op jit(solution)/shard_map/dot_general | solution.py:67
  589.7 14.2 %back_intra_kernel.1 = (f32[4,512,256]{2,1,0:T(8,128)}, f32[4,512,256]{2,1,0:T(8,128)}, f32[4,512,256]{2,1,0:T(8,128)}) custom-call(s32[1]{0:T(128)} %bitcast.1.me_ref, bf16[8,4,64,384]{3,2,1,0:T(8,128)(2,1)} %bitcast.211, f32[4,512,8]{2,1,0:T(8,128)S(1)} %stack.130.cols_ref, f32[4,1,512]{2,1,0:T(1,128)S(1)} %copy-done.17, bf16[128,512]{1,0:T(8,128)(2,1)S(1)} %copy-done.12, ...), custom_call_target="tpu_custom_call" | custom-call | tf_op jit(solution)/shard_map/back_intra_kernel/pallas_call | solution.py:308
  605.6 8.0 back_output_kernel.1
  614.4 9.1 %select_convert_fusion = bf16[2048,384]{1,0:T(8,128)(2,1)} fusion(bf16[2048,2048]{1,0:T(8,128)(2,1)} %bitcast.226, bf16[2048,384]{1,0:T(8,128)(2,1)S(1)} %bitcast.240, bf16[2048]{0:T(1024)(128)(2,1)S(1)} %copy-done.66, pred[384]{0:T(512)(128)(4,1)S(1)} %copy-done.64), kind=kOutput, calls=%fused_computation.15 | convolution fusion | flops 3222011904 | bytes 11538816 | tf_op jit(solution)/shard_map/dot_general | solution.py:67
  661.7 9.2 %collective-permute-done.82 = bf16[64,2048]{1,0:T(8,128)(2,1)S(1)} collective-permute-done((bf16[64,2048]{1,0:T(8,128)(2,1)}, bf16[64,2048]{1,0:T(8,128)(2,1)S(1)}, u32[]{:S(2)}, u32[]{:S(2)}) %collective-permute-start.82) | collective-permute-done | bytes 262176 | tf_op jit(solution)/shard_map/ppermute | solution.py:474
  671.7 20.0 %all-reduce.4.cloned.1.call-done = bf16[4,4,2,64,384]{4,3,2,0,1:T(8,128)(2,1)} async-done(((bf16[4,4,2,64,384]{4,3,2,0,1:T(8,128)(2,1)}), bf16[4,4,2,64,384]{4,3,2,0,1:T(8,128)(2,1)}) %all-reduce.4.cloned.1.call-update) | async-done | bytes 1572880
  721.3 77.3 %reduce-scatter.9.cloned.1.call-done = bf16[512,1408]{0,1:T(8,128)(2,1)} async-done(((bf16[2048,1408]{0,1:T(8,128)(2,1)}), bf16[512,1408]{0,1:T(8,128)(2,1)}) %reduce-scatter.9.cloned.1.call-update) | async-done | bytes 1441808 | tf_op jit(solution)/shard_map/reduce_scatter | solution.py:465
  806.5 11.5 %collective-permute-done.83 = bf16[256,1408]{0,1:T(8,128)(2,1)S(1)} collective-permute-done((bf16[256,1408]{0,1:T(8,128)(2,1)S(1)}, bf16[256,1408]{0,1:T(8,128)(2,1)S(1)}, u32[]{:S(2)}, u32[]{:S(2)}) %collective-permute-start.83) | collective-permute-done | bytes 720928 | tf_op jit(solution)/shard_map/ppermute | solution.py:71
  (516 shorter events, 365.1 us)
Async XLA Ops:
  7.2 100.2 %all-gather.12.cloned.1.call-start = ((), (), s32[]{:S(2)}) async-start(), calls=%async_computation.11 | async-start | bytes 1966080 | tf_op jit(solution)/shard_map/all_gather | solution.py:378
  34.8 169.4 %all-gather.6.cloned.1.call-start = ((), (), s32[]{:S(2)}) async-start(), calls=%async_computation.5 | async-start | bytes 1310720 | tf_op jit(solution)/shard_map/all_gather | solution.py:388
  34.8 40.6 %collective-permute-start.1 = (bf16[256,2048]{1,0:T(8,128)(2,1)S(1)}, bf16[256,2048]{1,0:T(8,128)(2,1)}, u32[]{:S(2)}, u32[]{:S(2)}) collective-permute-start(bf16[256,2048]{1,0:T(8,128)(2,1)S(1)} %bitcast.220), channel_id=1, source_target_pairs={{0,16},{16,0},{1,17},{17,1},{2,18},{18,2},{3,19},{19,3},{4,20},{20... | collective-permute-start | bytes 3145736 | tf_op jit(solution)/shard_map/ppermute | solution.py:71
  35.4 46.2 %collective-permute-start = (bf16[256,2048]{1,0:T(8,128)(2,1)S(1)}, bf16[256,2048]{1,0:T(8,128)(2,1)}, u32[]{:S(2)}, u32[]{:S(2)}) collective-permute-start(bf16[256,2048]{1,0:T(8,128)(2,1)S(1)} %bitcast.221), channel_id=1, source_target_pairs={{0,8},{8,0},{1,9},{9,1},{2,10},{10,2},{3,11},{11,3},{4,12},{12,4},... | collective-permute-start | bytes 3145736 | tf_op jit(solution)/shard_map/ppermute | solution.py:71
  35.4 43.6 %collective-permute-start.3 = (bf16[256,2048]{1,0:T(8,128)(2,1)S(1)}, bf16[256,2048]{1,0:T(8,128)(2,1)}, u32[]{:S(2)}, u32[]{:S(2)}) collective-permute-start(bf16[256,2048]{1,0:T(8,128)(2,1)S(1)} %bitcast.222), channel_id=1, source_target_pairs={{0,1},{1,0},{2,3},{3,2},{4,5},{5,4},{6,7},{7,6},{8,9},{9,8},{10,11... | collective-permute-start | bytes 3145736 | tf_op jit(solution)/shard_map/ppermute | solution.py:71
  40.0 32.9 %collective-permute-start.32 = (bf16[704,256]{1,0:T(8,128)(2,1)}, bf16[704,256]{1,0:T(8,128)(2,1)}, u32[]{:S(2)}, u32[]{:S(2)}) collective-permute-start(bf16[704,256]{1,0:T(8,128)(2,1)} %broadcast_select_fusion.7), channel_id=1, source_target_pairs={{0,1},{1,0},{2,3},{3,2},{4,5},{5,4},{6,7},{7,6},{8,9},{9,8},{10,11... | collective-permute-start | bytes 1081352 | tf_op jit(solution)/shard_map/ppermute | solution.py:71
  58.2 122.4 %collective-permute-start.44 = (bf16[256,2048]{1,0:T(8,128)(2,1)}, bf16[256,2048]{1,0:T(8,128)(2,1)}, u32[]{:S(2)}, u32[]{:S(2)}) collective-permute-start(bf16[256,2048]{1,0:T(8,128)(2,1)} %bitcast.48), channel_id=1, source_target_pairs={{0,16},{16,0},{1,17},{17,1},{2,18},{18,2},{3,19},{19,3},{4,20},{20... | collective-permute-start | bytes 3145736 | tf_op jit(solution)/shard_map/ppermute | solution.py:71
  59.3 202.1 %all-gather.10.cloned.1.call-start = ((), (), s32[]{:S(2)}) async-start(), calls=%async_computation.7 | async-start | bytes 3604480 | tf_op jit(solution)/shard_map/all_gather | solution.py:400
  72.9 135.9 %collective-permute-start.43 = (bf16[256,2048]{1,0:T(8,128)(2,1)}, bf16[256,2048]{1,0:T(8,128)(2,1)}, u32[]{:S(2)}, u32[]{:S(2)}) collective-permute-start(bf16[256,2048]{1,0:T(8,128)(2,1)} %bitcast.48), channel_id=1, source_target_pairs={{0,8},{8,0},{1,9},{9,1},{2,10},{10,2},{3,11},{11,3},{4,12},{12,4},... | collective-permute-start | bytes 3145736 | tf_op jit(solution)/shard_map/ppermute | solution.py:71
  75.1 224.4 %all-gather.8.cloned.1.call-start = ((), (), s32[]{:S(2)}) async-start(), calls=%async_computation.6 | async-start | bytes 7208960 | tf_op jit(solution)/shard_map/all_gather | solution.py:394
  91.6 92.4 %collective-permute-start.46 = (bf16[256,2048]{1,0:T(8,128)(2,1)}, bf16[256,2048]{1,0:T(8,128)(2,1)}, u32[]{:S(2)}, u32[]{:S(2)}) collective-permute-start(bf16[256,2048]{1,0:T(8,128)(2,1)} %bitcast.48), channel_id=1, source_target_pairs={{0,1},{1,0},{2,3},{3,2},{4,5},{5,4},{6,7},{7,6},{8,9},{9,8},{10,11... | collective-permute-start | bytes 3145736 | tf_op jit(solution)/shard_map/ppermute | solution.py:71
  98.2 67.7 %collective-permute-start.31 = (bf16[256,1408]{0,1:T(8,128)(2,1)}, bf16[256,1408]{0,1:T(8,128)(2,1)}, u32[]{:S(2)}, u32[]{:S(2)}) collective-permute-start(bf16[256,1408]{0,1:T(8,128)(2,1)} %broadcast_select_fusion.4), channel_id=1, source_target_pairs={{0,1},{1,0},{2,3},{3,2},{4,5},{5,4},{6,7},{7,6},{8,9},{9,8},{10,11... | collective-permute-start | bytes 2162696 | tf_op jit(solution)/shard_map/ppermute | solution.py:71
  135.5 26.1 %collective-permute-start.9 = (bf16[4,2,160,128]{3,2,1,0:T(8,128)(2,1)S(1)}, bf16[4,2,160,128]{3,2,1,0:T(8,128)(2,1)S(1)}, u32[]{:S(2)}, u32[]{:S(2)}) collective-permute-start(bf16[4,2,160,128]{3,2,1,0:T(8,128)(2,1)S(1)} %state_kernel.1), channel_id=1, source_target_pairs={{0,2},{2,4},{4,6},{1,3},{3,5},{5,7},{8,10},{10,12},{12,14},{9,11},... | collective-permute-start | bytes 983048 | tf_op jit(solution)/shard_map/ppermute | solution.py:116
  180.2 457.0 %reduce-scatter.11.cloned.1.call-start = ((), (), s32[]{:S(2)}) async-start(), calls=%async_computation.10 | async-start | bytes 3604480 | tf_op jit(solution)/shard_map/reduce_scatter | solution.py:464
  182.5 31.0 %collective-permute-start.48 = (bf16[128,2048]{1,0:T(8,128)(2,1)}, bf16[128,2048]{1,0:T(8,128)(2,1)}, u32[]{:S(2)}, u32[]{:S(2)}) collective-permute-start(bf16[128,2048]{1,0:T(8,128)(2,1)} %slice.629), channel_id=1, source_target_pairs={{0,1},{1,0},{2,3},{3,2},{4,5},{5,4},{6,7},{7,6},{8,9},{9,8},{10,11... | collective-permute-start | bytes 1572872 | tf_op jit(solution)/shard_map/ppermute | solution.py:71
  185.9 31.3 %collective-permute-start.49 = (bf16[128,2048]{1,0:T(8,128)(2,1)}, bf16[128,2048]{1,0:T(8,128)(2,1)S(1)}, u32[]{:S(2)}, u32[]{:S(2)}) collective-permute-start(bf16[128,2048]{1,0:T(8,128)(2,1)} %slice.630), channel_id=1, source_target_pairs={{0,16},{16,0},{1,17},{17,1},{2,18},{18,2},{3,19},{19,3},{4,20},{20... | collective-permute-start | bytes 1572872 | tf_op jit(solution)/shard_map/ppermute | solution.py:71
  258.2 26.2 %collective-permute-start.23 = (bf16[256,2048]{1,0:T(8,128)(2,1)}, bf16[256,2048]{1,0:T(8,128)(2,1)}, u32[]{:S(2)}, u32[]{:S(2)}) collective-permute-start(bf16[256,2048]{1,0:T(8,128)(2,1)} %get-tuple-element.154), channel_id=1, source_target_pairs={{0,8},{8,0},{1,9},{9,1},{2,10},{10,2},{3,11},{11,3},{4,12},{12,4},... | collective-permute-start | bytes 3145736 | tf_op jit(solution)/shard_map/ppermute | solution.py:71
  380.6 25.3 %collective-permute-start.51 = (bf16[256,2048]{1,0:T(8,128)(2,1)S(1)}, bf16[256,2048]{1,0:T(8,128)(2,1)S(1)}, u32[]{:S(2)}, u32[]{:S(2)}) collective-permute-start(bf16[256,2048]{1,0:T(8,128)(2,1)S(1)} %get-tuple-element.177), channel_id=1, source_target_pairs={{0,8},{8,0},{1,9},{9,1},{2,10},{10,2},{3,11},{11,3},{4,12},{12,4},... | collective-permute-start | bytes 3145736 | tf_op jit(solution)/shard_map/ppermute | solution.py:71
  405.8 29.7 %collective-permute-start.56 = (bf16[128,2048]{1,0:T(8,128)(2,1)S(1)}, bf16[128,2048]{1,0:T(8,128)(2,1)S(1)}, u32[]{:S(2)}, u32[]{:S(2)}) collective-permute-start(bf16[128,2048]{1,0:T(8,128)(2,1)S(1)} %fusion.10), channel_id=1, source_target_pairs={{0,1},{1,0},{2,3},{3,2},{4,5},{5,4},{6,7},{7,6},{8,9},{9,8},{10,11... | collective-permute-start | bytes 1572872 | tf_op jit(solution)/shard_map/ppermute | solution.py:71
  411.6 25.4 %collective-permute-start.59 = (bf16[128,2048]{1,0:T(8,128)(2,1)S(1)}, bf16[128,2048]{1,0:T(8,128)(2,1)S(1)}, u32[]{:S(2)}, u32[]{:S(2)}) collective-permute-start(bf16[128,2048]{1,0:T(8,128)(2,1)S(1)} %fusion.9), channel_id=1, source_target_pairs={{0,16},{16,0},{1,17},{17,1},{2,18},{18,2},{3,19},{19,3},{4,20},{20... | collective-permute-start | bytes 1572872 | tf_op jit(solution)/shard_map/ppermute | solution.py:71
  413.1 25.2 %collective-permute-start.33 = (bf16[256,2048]{1,0:T(8,128)(2,1)S(1)}, bf16[256,2048]{1,0:T(8,128)(2,1)S(1)}, u32[]{:S(2)}, u32[]{:S(2)}) collective-permute-start(bf16[256,2048]{1,0:T(8,128)(2,1)S(1)} %get-tuple-element.190), channel_id=1, source_target_pairs={{0,8},{8,0},{1,9},{9,1},{2,10},{10,2},{3,11},{11,3},{4,12},{12,4},... | collective-permute-start | bytes 3145736 | tf_op jit(solution)/shard_map/ppermute | solution.py:71
  465.6 26.8 %collective-permute-start.64 = (bf16[256,2048]{1,0:T(8,128)(2,1)}, bf16[256,2048]{1,0:T(8,128)(2,1)S(1)}, u32[]{:S(2)}, u32[]{:S(2)}) collective-permute-start(bf16[256,2048]{1,0:T(8,128)(2,1)} %get-tuple-element.152), channel_id=1, source_target_pairs={{0,1},{1,0},{2,3},{3,2},{4,5},{5,4},{6,7},{7,6},{8,9},{9,8},{10,11... | collective-permute-start | bytes 3145736 | tf_op jit(solution)/shard_map/ppermute | solution.py:71
  467.0 26.6 %collective-permute-start.61 = (bf16[256,2048]{1,0:T(8,128)(2,1)}, bf16[256,2048]{1,0:T(8,128)(2,1)}, u32[]{:S(2)}, u32[]{:S(2)}) collective-permute-start(bf16[256,2048]{1,0:T(8,128)(2,1)} %get-tuple-element.152), channel_id=1, source_target_pairs={{0,8},{8,0},{1,9},{9,1},{2,10},{10,2},{3,11},{11,3},{4,12},{12,4},... | collective-permute-start | bytes 3145736 | tf_op jit(solution)/shard_map/ppermute | solution.py:71
  489.7 162.3 %reduce-scatter.7.cloned.1.call-start = ((), (), s32[]{:S(2)}) async-start(), calls=%async_computation.8 | async-start | bytes 1310720 | tf_op jit(solution)/shard_map/reduce_scatter | solution.py:473
  559.7 132.0 %all-reduce.4.cloned.1.call-start = ((), (), s32[]{:S(2)}) async-start(), calls=%async_computation.12 | async-start | bytes 3145728
  560.0 43.9 %collective-permute-start.71 = (bf16[4,2,160,128]{3,2,1,0:T(8,128)(2,1)}, bf16[4,2,160,128]{3,2,1,0:T(8,128)(2,1)}, u32[]{:S(2)}, u32[]{:S(2)}) collective-permute-start(bf16[4,2,160,128]{3,2,1,0:T(8,128)(2,1)} %collective-permute-done.70), channel_id=1, source_target_pairs={{2,0},{4,2},{6,4},{3,1},{5,3},{7,5},{10,8},{12,10},{14,12},{11,9},... | collective-permute-start | bytes 983048 | tf_op jit(solution)/shard_map/ppermute | solution.py:116
  623.5 175.1 %reduce-scatter.9.cloned.1.call-start = ((), (), s32[]{:S(2)}) async-start(), calls=%async_computation.9 | async-start | bytes 7208960 | tf_op jit(solution)/shard_map/reduce_scatter | solution.py:465
  636.6 74.6 %collective-permute-start.72 = (bf16[256,2048]{1,0:T(8,128)(2,1)}, bf16[256,2048]{1,0:T(8,128)(2,1)S(1)}, u32[]{:S(2)}, u32[]{:S(2)}) collective-permute-start(bf16[256,2048]{1,0:T(8,128)(2,1)} %get-tuple-element.170), channel_id=1, source_target_pairs={{0,8},{8,0},{1,9},{9,1},{2,10},{10,2},{3,11},{11,3},{4,12},{12,4},... | collective-permute-start | bytes 3145736 | tf_op jit(solution)/shard_map/ppermute | solution.py:71
  648.6 49.5 %collective-permute-start.76 = (bf16[128,2048]{1,0:T(8,128)(2,1)}, bf16[128,2048]{1,0:T(8,128)(2,1)}, u32[]{:S(2)}, u32[]{:S(2)}) collective-permute-start(bf16[128,2048]{1,0:T(8,128)(2,1)} %get-tuple-element.216), channel_id=1, source_target_pairs={{0,16},{16,0},{1,17},{17,1},{2,18},{18,2},{3,19},{19,3},{4,20},{20... | collective-permute-start | bytes 1572872 | tf_op jit(solution)/shard_map/ppermute | solution.py:71
  656.7 45.8 %collective-permute-start.79 = (bf16[128,2048]{1,0:T(8,128)(2,1)}, bf16[128,2048]{1,0:T(8,128)(2,1)}, u32[]{:S(2)}, u32[]{:S(2)}) collective-permute-start(bf16[128,2048]{1,0:T(8,128)(2,1)} %get-tuple-element.217), channel_id=1, source_target_pairs={{0,1},{1,0},{2,3},{3,2},{4,5},{5,4},{6,7},{7,6},{8,9},{9,8},{10,11... | collective-permute-start | bytes 1572872 | tf_op jit(solution)/shard_map/ppermute | solution.py:71
  660.2 51.0 %collective-permute-start.74 = (bf16[128,2048]{1,0:T(8,128)(2,1)}, bf16[128,2048]{1,0:T(8,128)(2,1)}, u32[]{:S(2)}, u32[]{:S(2)}) collective-permute-start(bf16[128,2048]{1,0:T(8,128)(2,1)} %slice.789), channel_id=1, source_target_pairs={{0,1},{1,0},{2,3},{3,2},{4,5},{5,4},{6,7},{7,6},{8,9},{9,8},{10,11... | collective-permute-start | bytes 1572872 | tf_op jit(solution)/shard_map/ppermute | solution.py:71
  670.9 40.4 %collective-permute-start.81 = (bf16[128,2048]{1,0:T(8,128)(2,1)}, bf16[128,2048]{1,0:T(8,128)(2,1)}, u32[]{:S(2)}, u32[]{:S(2)}) collective-permute-start(bf16[128,2048]{1,0:T(8,128)(2,1)} %slice.788), channel_id=1, source_target_pairs={{0,16},{16,0},{1,17},{17,1},{2,18},{18,2},{3,19},{19,3},{4,20},{20... | collective-permute-start | bytes 1572872 | tf_op jit(solution)/shard_map/ppermute | solution.py:71
  (131 other events, 1797.0 us)
Sparse Core Ops, SparseCore 0:
  34.9 38.6 all-gather.11
  75.1 28.6 all-gather.5
  105.3 64.7 all-gather.9
  180.3 104.9 all-gather.7
  489.8 62.3 reduce-scatter.10
  559.8 29.0 reduce-scatter.6
  623.6 68.0 all-reduce.3
  694.1 104.4 reduce-scatter.8

commit v2 on v1

v2 whole, which is shorter than its diff:
```python
import math

import numpy as np

import jax
import jax.numpy as jnp
from jax import lax
from jax.experimental import pallas as pl
from jax.experimental.pallas import tpu as pltpu
from jax.sharding import Mesh
from jax.sharding import PartitionSpec as P

D = 2048
HEADS = 16
QK = 16
VD = 128
EPS = 1e-05
F32 = jnp.float32
BF16 = jnp.bfloat16
GROUP = ("hi", "core", "col")
FEAT = 1 + QK + QK * (QK + 1) // 2
FPAD = 256
FROWS = 160
PAYLOAD = 384


def feature_constants():
    left = np.zeros((128, FPAD), np.float32)
    right = np.zeros((128, FPAD), np.float32)
    rows = np.zeros((8, 2 * FPAD), np.float32)
    at = 0
    for i in range(QK):
        for j in range(i, QK):
            left[i, at] = 1.0
            right[j, at] = 1.0
            rows[1, at] = (1.0 if i == j else math.sqrt(2.0)) / math.sqrt(2.0 * QK)
            at += 1
    for i in range(QK):
        left[i, at] = 1.0
        rows[0, FPAD + at] = 1.0
        rows[1, at] = QK ** (-0.25)
        at += 1
    rows[0, at] = 1.0
    rows[0, FPAD + at] = 1.0
    rows[1, at] = 1.0
    align = np.zeros((4, 128, 128), np.float32)
    for part in range(4):
        for i in range(QK):
            align[part, part * QK + i, i] = 1.0
    return (
        jnp.asarray(np.concatenate([left, right], 1), BF16),
        jnp.asarray(rows, F32),
        jnp.asarray(align.transpose(1, 0, 2).reshape(128, 512), BF16),
    )


def dot(a, b):
    return jnp.dot(a, b, preferred_element_type=F32)


def dot_t(a, b):
    return lax.dot_general(a, b, (((1,), (1,)), ((), ())), preferred_element_type=F32)


def t_dot(a, b):
    return lax.dot_general(a, b, (((0,), (0,)), ((), ())), preferred_element_type=F32)


def swap(value, axis):
    return lax.ppermute(value, axis, [(0, 1), (1, 0)])


def after(value, *others):
    if not others:
        return value

    def gate(*refs):
        pass

    return pl.pallas_call(
        gate,
        in_specs=[pl.BlockSpec(memory_space=pl.ANY)] * (1 + len(others)),
        out_specs=pl.BlockSpec(memory_space=pl.ANY),
        out_shape=jax.ShapeDtypeStruct(value.shape, value.dtype),
        input_output_aliases={0: 0},
        cost_estimate=pl.CostEstimate(flops=0, transcendentals=0, bytes_accessed=0),
        name="gate",
    )(value, *others)


def gather8(own, first=None):
    half = own.shape[0] // 2
    over_x = swap(own, "col")
    over_y = swap(own, "hi")
    over_c = swap(own, "core")
    if first is not None:
        done = first(own)
        over_x, over_y = after(over_x, done), after(over_y, done)
    top = swap(over_y[:half], "col")
    low = swap(over_x[half:], "hi")
    return [
        (own, 0, 0),
        (over_c, 1, 0),
        (over_y, 2, 0),
        (swap(over_y, "core"), 3, 0),
        (over_x, 4, 0),
        (swap(over_x, "core"), 5, 0),
        (top, 6, 0),
        (low, 6, half),
        (swap(top, "core"), 7, 0),
        (swap(low, "core"), 7, half),
    ]


def scatter_steps(parts):
    def both(one, two, start, end):
        return one[start:end].astype(F32) + two[start:end].astype(F32)

    own, other, y, yc, x, xc, xy, xyc = parts
    n = xy.shape[0]
    half = n // 2
    xyc = swap(xyc, "core")
    xc = swap(xc, "core")
    yc = swap(yc, "core")
    other = swap(other, "core")
    to_x = both(xy, xyc, 0, half).astype(BF16)
    to_y = both(xy, xyc, half, n).astype(BF16)
    near_x = both(x, xc, 0, half).astype(BF16)
    near_y = both(y, yc, half, n).astype(BF16)
    from_x, from_y = swap(to_x, "col"), swap(to_y, "hi")
    first_x, first_y = swap(near_x, "col"), swap(near_y, "hi")
    done = yield [to_x, to_y, near_x, near_y]
    from_x, from_y = after(from_x, *done), after(from_y, *done)
    far_x = (both(x, xc, half, n) + from_y.astype(F32)).astype(BF16)
    far_y = (both(y, yc, 0, half) + from_x.astype(F32)).astype(BF16)
    last_x, last_y = swap(far_x, "col"), swap(far_y, "hi")
    done = yield [far_x, far_y]
    last_x, last_y = after(last_x, *done), after(last_y, *done)
    return own, other, first_x, last_y, last_x, first_y


def walk_steps(value, linked, joined, up):
    rows = lax.axis_size("row")
    total = None
    now = value
    step = 1
    while step < rows:
        pairs = [(i, i + step) if up else (i + step, i) for i in range(rows - step)]
        came = lax.ppermute(now, "row", pairs)
        done = yield now, came
        wide = after(came, *done).astype(F32)
        term = joined(step)[:, None, None, None] * wide
        total = term if total is None else total + term
        if 2 * step < rows:
            now = (now.astype(F32) + linked(step)[:, None, None, None] * wide).astype(BF16)
        step = 2 * step
    return total


def finish(steps, done=()):
    try:
        steps.send(done)
        while True:
            steps.send(())
    except StopIteration as end:
        return end.value


def scatter8(parts, *kernels):
    steps = scatter_steps(parts)
    sent = next(steps)
    for i, kernel in enumerate(kernels):
        done = kernel(sent)
        if i == 1:
            return finish(steps, done)
        sent = steps.send(done)
    return finish(steps)


def params(mib=60):
    return pltpu.CompilerParams(dimension_semantics=("arbitrary",), vmem_limit_bytes=mib * 1024 * 1024)


def cost(flops, *arrays):
    return pl.CostEstimate(
        flops=int(flops),
        transcendentals=0,
        bytes_accessed=int(sum(math.prod(a.shape) * a.dtype.itemsize for a in arrays)),
    )


def slot_call(kernel, pieces, ins, outs, flops, deps=(), whole=()):
    n = len(pieces)
    width = pieces[0][0].shape[1]
    per = pieces[0][0].shape[0]

    def wrapped(*refs):
        rows = refs[:n]
        at = n + len(ins)
        rest = refs[n:at] + refs[at + len(deps) : at + len(deps) + len(outs) + len(whole)]
        buf, sem = refs[-2:]
        i = pl.program_id(0)

        @pl.when(i == 0)
        def _():
            for (a, slot, start), ref in zip(pieces, rows):
                pltpu.make_async_copy(ref, buf.at[slot, pl.ds(start, a.shape[0])], sem.at[slot]).start()

        pltpu.make_async_copy(buf.at[i], buf.at[i], sem.at[i]).wait()
        kernel(buf.at[i], *rest)

    def spec(a, by_slot):
        rest = len(a.shape) - 1
        if by_slot:
            return pl.BlockSpec((None,) + a.shape[1:], lambda i: (i,) + (0,) * rest)
        return pl.BlockSpec(a.shape, lambda i: (0,) * (rest + 1))

    return pl.pallas_call(
        wrapped,
        grid=(8,),
        in_specs=[pl.BlockSpec(memory_space=pltpu.HBM)] * n
        + [spec(a, k) for a, k in ins]
        + [pl.BlockSpec(memory_space=pl.ANY)] * len(deps),
        out_specs=[spec(a, True) for a in outs] + [spec(a, False) for a in whole],
        out_shape=list(outs) + list(whole),
        scratch_shapes=[pltpu.VMEM((8, per, width), BF16), pltpu.SemaphoreType.DMA((8,))],
        compiler_params=params(),
        cost_estimate=cost(flops, *[a for a, _, _ in pieces], *[a for a, _ in ins], *outs, *whole),
        name=kernel.__name__,
    )(*[a for a, _, _ in pieces], *[a for a, _ in ins], *deps)


def grad_call(kernel, pieces, tile, whole, ins, outs, flops, index=lambda i: i, steps=None, deps=()):
    n = len(pieces)
    width = pieces[0][0].shape[1]
    places = [(slot, start, a.shape[0]) for a, slot, start in pieces]

    def wrapped(*refs):
        at = n + len(whole) + len(ins)
        kernel(list(zip(refs[:n], places)), *refs[n:at], *refs[at + len(deps) :])

    def fixed(a):
        rest = len(a.shape)
        return pl.BlockSpec(a.shape, lambda i: (0,) * rest)

    return pl.pallas_call(
        wrapped,
        grid=(steps or width // tile,),
        in_specs=[pl.BlockSpec((a.shape[0], tile), lambda i: (0, index(i))) for a, _, _ in pieces]
        + [fixed(a) for a in whole]
        + [pl.BlockSpec(block, where) for _, block, where in ins]
        + [pl.BlockSpec(memory_space=pl.ANY)] * len(deps),
        out_specs=[pl.BlockSpec(block, where) for _, block, where in outs],
        out_shape=[a for a, _, _ in outs],
        compiler_params=params(),
        cost_estimate=cost(
            flops, *[a for a, _, _ in pieces], *whole, *[a for a, _, _ in ins], *[a for a, _, _ in outs]
        ),
        name=kernel.__name__,
    )(*[a for a, _, _ in pieces], *whole, *[a for a, _, _ in ins], *deps)


def summed(rows, right):
    total = None
    for ref, (slot, start, n) in rows:
        term = t_dot(ref[...], right[slot, start : start + n, :])
        total = term if total is None else total + term
    return total


def qkv_kernel(x_ref, given_ref, qkv_ref, inv_ref, w_ref):
    @pl.when(pl.program_id(0) == 0)
    def _():
        rows, groups, n, _ = given_ref.shape
        for g in range(groups):
            for r in range(rows):
                w_ref[pl.ds((g * rows + r) * n, n), :] = given_ref[r, g]

    x = x_ref[...]
    wide = x.astype(F32)
    inv = lax.rsqrt(jnp.sum(wide * wide, 1, keepdims=True) * (1.0 / x.shape[1]) + EPS)
    qkv_ref[...] = (dot(x, w_ref[...]) * inv).astype(BF16)
    inv_ref[...] = jnp.broadcast_to(inv, inv_ref.shape)


def ffn_in_kernel(a_ref, w_ref, gu_ref, h_ref, turned_ref):
    gu = dot(a_ref[...], w_ref[...])
    gu_ref[...] = gu.astype(BF16)
    m = (gu.shape[1] - 128) // 2
    g, u = gu[:, :m], gu[:, m : 2 * m]
    h_ref[:, :m] = (g * jax.nn.sigmoid(g) * u).astype(BF16)
    g = gu[:, 2 * m :]
    u = pltpu.roll(g, 64, 1)
    first = lax.broadcasted_iota(jnp.int32, g.shape, 1) < 64
    h_ref[:, m:] = jnp.where(first, g * jax.nn.sigmoid(g) * u, 0.0).astype(BF16)
    turned_ref[...] = jnp.transpose(h_ref[...])


def ffn_back_kernel(up_ref, w_ref, gu_ref, out_ref):
    up = up_ref[...]
    total = None
    for i in range(8):
        term = dot_t(up[:, i * 256 : (i + 1) * 256], w_ref[i])
        total = term if total is None else total + term
    m = total.shape[1] - 64

    def both(g, u, dh):
        s = jax.nn.sigmoid(g)
        return dh * u * (s * (1.0 + g * (1.0 - s))), dh * (g * s)

    gu = gu_ref[...].astype(F32)
    dg, du = both(gu[:, :m], gu[:, m : 2 * m], total[:, :m])
    out_ref[:, :m] = dg.astype(BF16)
    out_ref[:, m : 2 * m] = du.astype(BF16)
    mid = gu[:, 2 * m :]
    other = pltpu.roll(mid, 64, 1)
    first = lax.broadcasted_iota(jnp.int32, mid.shape, 1) < 64
    dh = jnp.concatenate([total[:, m:], total[:, m:]], 1)
    dg, du = both(jnp.where(first, mid, other), jnp.where(first, other, mid), dh)
    out_ref[:, 2 * m :] = jnp.where(first, dg, du).astype(BF16)


def down_grad_kernel(rows, h_ref, out_ref):
    total = None
    for ref, (slot, start, n) in rows:
        term = dot(h_ref[slot, : out_ref.shape[1], start : start + n], ref[...])
        total = term if total is None else total + term
    out_ref[0] = total.astype(BF16)


def gu_grad_kernel(rows, right_ref, w_ref, out_ref, gain_ref):
    total = summed(rows, right_ref)
    out_ref[...] = total.astype(BF16)
    gain_ref[...] = jnp.broadcast_to(
        jnp.sum(total * w_ref[...].astype(F32), 1, keepdims=True), gain_ref.shape
    )


def do_kernel(d_ref, w_ref, out_ref):
    out_ref[...] = dot_t(d_ref[...], w_ref[...]).astype(BF16)


def proj_grad_kernel(rows, o_ref, out_ref):
    total = None
    for ref, (slot, start, n) in rows:
        term = t_dot(o_ref[slot, start : start + n, :], ref[...])
        total = term if total is None else total + term
    out_ref[...] = total.astype(BF16)


def qkv_grad_kernel(rows, right_ref, gain_ref, out_ref):
    total = summed(rows, right_ref)
    lane = lax.broadcasted_iota(jnp.int32, (1, 128), 1)
    total = jnp.concatenate([total[:, :256], jnp.where(lane == 64, gain_ref[...], total[:, 256:])], 1)
    out_ref[...] = total.astype(BF16).reshape(out_ref.shape)


def row_sum(refs):
    own, other, first_x, last_y, last_x, first_y = [ref[...].astype(F32) for ref in refs]
    return own + other + jnp.concatenate([first_x + last_y, last_x + first_y], 0)


def scaled_rows(rows):
    inv = lax.rsqrt(jnp.sum(rows * rows, 1, keepdims=True) * (1.0 / rows.shape[1]) + EPS)
    return rows * inv, inv


def norm_back(normed, inv, grad):
    return inv * (grad - normed * (jnp.sum(grad * normed, 1, keepdims=True) * (1.0 / grad.shape[1])))


def residual_kernel(refs, x_ref, gain_ref, sum_ref, a_ref):
    rows = x_ref[...].astype(F32) + row_sum(refs)
    sum_ref[...] = rows
    a_ref[...] = (scaled_rows(rows)[0] * gain_ref[...]).astype(BF16)


def output_rows_kernel(refs, sum_ref, out_ref):
    out_ref[...] = (sum_ref[...] + row_sum(refs)).astype(BF16)


def residual_back_kernel(refs, up_ref, sum_ref, gain_ref, grad_ref, low_ref):
    normed, inv = scaled_rows(sum_ref[...])
    grad = up_ref[...].astype(F32) + norm_back(normed, inv, row_sum(refs) * gain_ref[...])
    grad_ref[...] = grad
    low_ref[...] = grad.astype(BF16)


def input_back_kernel(refs, x_ref, grad_ref, out_ref):
    normed, inv = scaled_rows(x_ref[...].astype(F32))
    out_ref[...] = grad_ref[...] + norm_back(normed, inv, row_sum(refs))


def row_call(kernel, pieces, ins, kinds, deps=()):
    shape = pieces[0].shape
    outs = [jax.ShapeDtypeStruct(shape, kind) for kind in kinds]

    def wrapped(*refs):
        at = 6 + len(ins)
        kernel(refs[:6], *refs[6:at], *refs[at + len(deps) :])

    return pl.pallas_call(
        wrapped,
        in_specs=[pl.BlockSpec(memory_space=pltpu.VMEM)] * (6 + len(ins))
        + [pl.BlockSpec(memory_space=pl.ANY)] * len(deps),
        out_specs=[pl.BlockSpec(memory_space=pltpu.VMEM)] * len(outs),
        out_shape=outs,
        compiler_params=pltpu.CompilerParams(vmem_limit_bytes=24 * 1024 * 1024),
        cost_estimate=cost(20 * math.prod(shape), *pieces, *ins, *outs),
        name=kernel.__name__,
    )(*pieces, *ins, *deps)


def parts_call(a, w, kind, deps=(), mib=60):
    slots, per, k = a.shape
    if kind == "blocks":
        tile, depth = w.shape[2], w.shape[1]
        width = w.shape[0] * tile
        w_spec = pl.BlockSpec((1, depth, tile), lambda i: (i, 0, 0))
    elif kind == "nn":
        tile, depth, width = 512, k, w.shape[1]
        w_spec = pl.BlockSpec((k, tile), lambda i: (0, i))
    else:
        tile, depth, width = 512, k, w.shape[0]
        w_spec = pl.BlockSpec((tile, k), lambda i: (i, 0))

    def kernel(a_ref, w_ref, *refs):
        right = w_ref[0] if kind == "blocks" else w_ref[...]
        for slot, out_ref in enumerate(refs[-slots:]):
            left = a_ref[slot, :, :depth]
            out_ref[...] = (dot_t if kind == "nt" else dot)(left, right).astype(BF16)

    out = jax.ShapeDtypeStruct((per, width), BF16)
    return pl.pallas_call(
        kernel,
        grid=(width // tile,),
        in_specs=[pl.BlockSpec(a.shape, lambda i: (0, 0, 0)), w_spec]
        + [pl.BlockSpec(memory_space=pl.ANY)] * len(deps),
        out_specs=[pl.BlockSpec((per, tile), lambda i: (0, i))] * slots,
        out_shape=[out] * slots,
        compiler_params=params(mib),
        cost_estimate=cost(2 * slots * per * depth * width, a, w, *[out] * slots),
        name="parts_" + kind,
    )(a, w, *deps)


def ordered(ref, me, lanes=slice(None)):
    return jnp.concatenate([ref[p ^ me, 0, :, lanes] for p in range(8)], 0)


def put_ordered(ref, me, value, lanes=slice(None)):
    sub = value.shape[0] // 8
    for p in range(8):
        ref[p ^ me, 0, :, lanes] = value[p * sub : (p + 1) * sub]


def phi(aligned, feat, rows):
    both = dot(aligned, feat) + rows[0:1, :]
    a, b = both[:, :FPAD], both[:, FPAD:]
    return a, b, a * b * rows[1:2, :FPAD]


def phi_back(a, b, grad, feat, rows):
    scaled = grad * rows[1:2, :FPAD]
    return dot_t((scaled * b).astype(BF16), feat[:, :FPAD]) + dot_t(
        (scaled * a).astype(BF16), feat[:, FPAD:]
    )


def put_state(ref, head, state, norm):
    ref[0, head] = state[:FROWS].astype(BF16)
    high = norm.astype(BF16)
    low = (norm - high.astype(F32)).astype(BF16)
    ref[0, head, FEAT : FEAT + 1, :] = high[:, :128]
    ref[0, head, FEAT + 1 : FEAT + 2, :] = low[:, :128]
    ref[0, head, FEAT + 2 : FEAT + 3, :] = high[:, 128:]
    ref[0, head, FEAT + 3 : FEAT + 4, :] = low[:, 128:]


def get_state(ref, head):
    whole = ref[0, head]
    state = jnp.concatenate([whole, jnp.zeros((FPAD - FROWS, 128), F32)], 0)
    norm = jnp.concatenate(
        [
            whole[FEAT : FEAT + 1] + whole[FEAT + 1 : FEAT + 2],
            whole[FEAT + 2 : FEAT + 3] + whole[FEAT + 3 : FEAT + 4],
        ],
        1,
    )
    return state.astype(BF16), norm


def align4(qk, align_ref):
    out = dot(qk, align_ref[...]).astype(BF16)
    return [out[:, i * 128 : (i + 1) * 128] for i in range(4)]


def column(seg_ref):
    row = seg_ref[0]
    return jnp.transpose(jnp.broadcast_to(row, (128, row.shape[1])))[:, 0:1]


def mask_of(seg_ref, meta_ref, which):
    at = 1 + which * pl.num_programs(0) + pl.program_id(0)
    return jnp.where(column(seg_ref) == meta_ref[at].astype(F32), 1.0, 0.0)


def visible(seg_ref):
    t = seg_ref.shape[2]
    causal = lax.broadcasted_iota(jnp.int32, (t, t), 0) >= lax.broadcasted_iota(jnp.int32, (t, t), 1)
    return causal & (column(seg_ref) == seg_ref[0])


def state_kernel(me_ref, qkv_ref, seg_ref, feat_ref, rows_ref, align_ref, out_ref):
    me = me_ref[0]
    qk = ordered(qkv_ref, me, slice(256, 384))
    v = ordered(qkv_ref, me, slice(0, 256))
    last = mask_of(seg_ref, me_ref, 1)
    parts = align4(qk, align_ref)
    for head in range(2):
        _, _, feat = phi(parts[2 + head], feat_ref[...], rows_ref[...])
        feat = feat * last
        state = t_dot(feat.astype(BF16), v[:, head * 128 : (head + 1) * 128])
        put_state(out_ref, head, state, jnp.sum(feat, 0, keepdims=True))


def intra_kernel(me_ref, qkv_ref, seg_ref, align_ref, num_ref, den_ref):
    me = me_ref[0]
    qk = ordered(qkv_ref, me, slice(256, 384))
    v = ordered(qkv_ref, me, slice(0, 256))
    see = visible(seg_ref)
    parts = align4(qk, align_ref)
    den_ref[0] = jnp.zeros(den_ref.shape[1:], F32)
    for head in range(2):
        z = dot_t(parts[head], parts[2 + head])
        w = jnp.where(see, 1.0 + z * (0.25 + 0.03125 * z), 0.0)
        num_ref[0, :, head * 128 : (head + 1) * 128] = dot(
            w.astype(BF16), v[:, head * 128 : (head + 1) * 128]
        )
        den_ref[0, :, head : head + 1] = jnp.sum(w, 1, keepdims=True)


def output_kernel(
    me_ref, qkv_ref, seg_ref, feat_ref, rows_ref, align_ref, num_ref, den_ref, state_ref, o_ref, all_ref
):
    me = me_ref[0]
    qk = ordered(qkv_ref, me, slice(256, 384))
    use = mask_of(seg_ref, me_ref, 0)
    parts = align4(qk, align_ref)
    all_ref[0] = jnp.zeros(all_ref.shape[1:], F32)
    for head in range(2):
        lanes = slice(head * 128, (head + 1) * 128)
        _, _, feat = phi(parts[head], feat_ref[...], rows_ref[...])
        state, norm = get_state(state_ref, head)
        num = num_ref[0, :, lanes] + use * dot(feat.astype(BF16), state)
        den = den_ref[0, :, head : head + 1] + use * jnp.sum(feat * norm, 1, keepdims=True)
        all_ref[0, :, head : head + 1] = den
        put_ordered(o_ref, me, (num / den).astype(BF16), lanes)


def back_parts(me, o_ref, do_ref, den_ref, head):
    lanes = slice(head * 128, (head + 1) * 128)
    inv = 1.0 / den_ref[0, :, head : head + 1]
    do = ordered(do_ref, me, lanes).astype(F32)
    o = ordered(o_ref, me, lanes).astype(F32)
    return (do * inv).astype(BF16), -jnp.sum(do * o, 1, keepdims=True) * inv


def back_state_kernel(
    me_ref, qkv_ref, seg_ref, feat_ref, rows_ref, align_ref, o_ref, do_ref, den_ref, out_ref
):
    me = me_ref[0]
    qk = ordered(qkv_ref, me, slice(256, 384))
    use = mask_of(seg_ref, me_ref, 0)
    parts = align4(qk, align_ref)
    for head in range(2):
        g, c = back_parts(me, o_ref, do_ref, den_ref, head)
        _, _, feat = phi(parts[head], feat_ref[...], rows_ref[...])
        feat = feat * use
        put_state(out_ref, head, t_dot(feat.astype(BF16), g), jnp.sum(feat * c, 0, keepdims=True))


def back_intra_kernel(
    me_ref, qkv_ref, seg_ref, feat_ref, rows_ref, align_ref, o_ref, do_ref, den_ref, state_ref,
    dq_ref, dk_ref, dv_ref,
):
    me = me_ref[0]
    qk = ordered(qkv_ref, me, slice(256, 384))
    v = ordered(qkv_ref, me, slice(0, 256))
    use = mask_of(seg_ref, me_ref, 0)
    see = visible(seg_ref)
    parts = align4(qk, align_ref)
    for head in range(2):
        lanes = slice(head * 128, (head + 1) * 128)
        g, c = back_parts(me, o_ref, do_ref, den_ref, head)
        z = dot_t(parts[head], parts[2 + head])
        w = jnp.where(see, 1.0 + z * (0.25 + 0.03125 * z), 0.0)
        dv_ref[0, :, lanes] = t_dot(w.astype(BF16), g)
        dw = dot_t(g, v[:, lanes]) + c
        dz = jnp.where(see, dw * (0.25 + 0.0625 * z), 0.0).astype(BF16)
        a, b, _ = phi(parts[head], feat_ref[...], rows_ref[...])
        state, norm = get_state(state_ref, head)
        grad = use * (dot_t(g, state) + c * norm)
        dq_ref[0, :, lanes] = dot(dz, parts[2 + head]) + phi_back(a, b, grad, feat_ref[...], rows_ref[...])
        dk_ref[0, :, lanes] = t_dot(dz, parts[head])


def back_output_kernel(
    me_ref, qkv_ref, seg_ref, feat_ref, rows_ref, align_ref, state_ref, dq_ref, dk_ref, dv_ref, inv_ref, out_ref, scaled_ref
):
    me = me_ref[0]
    qk = ordered(qkv_ref, me, slice(256, 384))
    v = ordered(qkv_ref, me, slice(0, 256))
    last = mask_of(seg_ref, me_ref, 1)
    parts = align4(qk, align_ref)
    inv = ordered(inv_ref, me)
    packed = None
    for head in range(2):
        lanes = slice(head * 128, (head + 1) * 128)
        a, b, feat = phi(parts[2 + head], feat_ref[...], rows_ref[...])
        state, norm = get_state(state_ref, head)
        grad = last * (dot_t(v[:, lanes], state) + norm)
        dk = dk_ref[0, :, lanes] + phi_back(a, b, grad, feat_ref[...], rows_ref[...])
        dv = dv_ref[0, :, lanes] + last * dot(feat.astype(BF16), state)
        put_ordered(out_ref, me, dv.astype(BF16), lanes)
        put_ordered(scaled_ref, me, (dv * inv).astype(BF16), lanes)
        place = align_ref[...]
        term = dot_t(dq_ref[0, :, lanes].astype(BF16), place[:, head * 128 : (head + 1) * 128]) + dot_t(
            dk.astype(BF16), place[:, (2 + head) * 128 : (3 + head) * 128]
        )
        packed = term if packed is None else packed + term
    put_ordered(out_ref, me, packed.astype(BF16), slice(256, 384))
    put_ordered(scaled_ref, me, (packed * inv).astype(BF16), slice(256, 384))


def attention_call(kernel, me, ins, kinds, outs, flops, deps=()):
    def spec(a, kind):
        if kind == "s":
            return pl.BlockSpec((8, 1) + a.shape[2:], lambda i, m: (0, i, 0, 0))
        rest = len(a.shape) - 1
        if kind == "q":
            return pl.BlockSpec((1,) + a.shape[1:], lambda i, m: (i,) + (0,) * rest)
        return pl.BlockSpec(a.shape, lambda i, m: (0,) * (rest + 1))

    seqs = ins[0].shape[1]
    n = 1 + len(ins)

    def wrapped(*refs):
        kernel(*refs[:n], *refs[n + len(deps) :])

    return pl.pallas_call(
        wrapped,
        out_shape=[jax.ShapeDtypeStruct(a.shape, a.dtype) for a, _ in outs],
        grid_spec=pltpu.PrefetchScalarGridSpec(
            num_scalar_prefetch=1,
            grid=(seqs,),
            in_specs=[spec(a, k) for a, k in zip(ins, kinds)] + [pl.BlockSpec(memory_space=pl.ANY)] * len(deps),
            out_specs=[spec(a, k) for a, k in outs],
        ),
        compiler_params=params(28),
        cost_estimate=cost(flops, *ins, *[a for a, _ in outs]),
        name=kernel.__name__,
    )(me, *ins, *deps)


def pick(cond, a, b):
    return jnp.where(cond, a, b)


def half_columns(gate, up, which, n_main, n_mid):
    mid = slice(n_main, n_main + 2 * n_mid)
    main = slice(0, n_main) if which == 0 else slice(n_main + 2 * n_mid, None)
    part = slice(0, n_mid) if which == 0 else slice(n_mid, None)
    return jnp.concatenate([gate[:, main], up[:, main], gate[:, mid][:, part], up[:, mid][:, part]], 1)


def body(inputs, segments, qw, kw, vw, pw, again, gw, uw, dw, fgain, upstream):
    hi, core, row, col = (lax.axis_index(a) for a in ("hi", "core", "row", "col"))
    rows = lax.axis_size("row")
    shards = 2 * rows
    seqs, sub = inputs.shape[0], inputs.shape[3]
    tokens = seqs * sub
    span = 8 * sub
    n_rows = qw.shape[0]
    is0 = col == 0
    ff = gw.shape[1]
    half_ff = ff // 2
    n_mid = 64
    n_main = half_ff - n_mid
    feat_c, rows_c, align_c = feature_constants()
    sds = jax.ShapeDtypeStruct
    x = inputs.reshape(tokens, D)

    shard_pairs = [(s, (s % rows) * 2 + s // rows) for s in range(shards)]
    moved = lax.ppermute(pw, ("row", "col"), shard_pairs)

    gain_one = again.astype(F32)[:, None]
    seg_own = segments.reshape(seqs, 4 * sub)

    def by_dest(w, scale):
        return (w.astype(F32) * scale).astype(BF16).reshape(n_rows, 8, -1)

    lane = lax.broadcasted_iota(jnp.int32, (n_rows, PAYLOAD - 320), 1)
    ends = jnp.pad(seg_own[:, -1], (0, n_rows - seqs)).astype(F32)[:, None]
    tens = jnp.floor(ends * (1.0 / 128.0))
    extra = jnp.where(
        lane == 0,
        fgain.astype(F32)[:, None],
        jnp.where(lane == 1, tens, jnp.where(lane == 2, ends - 128.0 * tens, 0.0)),
    ).astype(BF16)
    payload = jnp.concatenate(
        [
            by_dest(vw, gain_one),
            by_dest(qw, gain_one),
            by_dest(kw, gain_one),
            jnp.broadcast_to(extra[:, None], (n_rows, 8, PAYLOAD - 320)),
        ],
        2,
    ).transpose(1, 0, 2)
    payload = lax.all_to_all(payload, GROUP, split_axis=0, concat_axis=0, tiled=True)
    x_own = after(x, payload)
    xs = gather8(x_own)
    w_proj = lax.all_gather(moved, "row", axis=0, tiled=True)
    gathered = lax.all_gather(after(payload, moved), "row", axis=0, tiled=False)
    lasts = gathered[:, 1, :seqs, 321:323].astype(F32)
    lasts = (lasts[:, :, 0] * 128.0 + lasts[:, :, 1]).astype(jnp.int32)

    seg_other = swap(seg_own, "col")
    seg = jnp.concatenate([pick(is0, seg_own, seg_other), pick(is0, seg_other, seg_own)], 1)
    seg_row = seg.astype(F32)[:, None, :]
    before = jnp.where(row > 0, lasts[jnp.maximum(row - 1, 0)], -1)
    here = lasts[row]
    me3 = (4 * col + 2 * hi + core).astype(jnp.int32)
    meta = jnp.concatenate([me3[None], before, here])

    ends = jnp.concatenate([lasts, jnp.full((1, seqs), -1, jnp.int32)])

    def end_of(r):
        return ends[jnp.where((r >= 0) & (r < rows), r, rows)]

    def same(r, other):
        return ((end_of(r) == other) & (r >= 0) & (r < rows)).astype(F32)

    every = 8 * tokens
    qkv, inv, w_qkv = slot_call(
        qkv_kernel, xs, [(gathered.reshape(rows, 4, 2 * n_rows, PAYLOAD), False)],
        [sds((8, tokens, PAYLOAD), BF16), sds((8, tokens, 128), F32)], 2 * every * D * PAYLOAD,
        deps=[seg_row], whole=[sds((D, PAYLOAD), BF16)],
    )
    gain_two = w_qkv[:, 320].astype(F32)[None, :]
    inv = inv.reshape(8, seqs, sub, 128)
    ups = gather8(after(upstream.reshape(tokens, D), qkv))
    qkv = qkv.reshape(8, seqs, sub, PAYLOAD)
    st = sds((seqs, 2, FROWS, 128), BF16)
    near = 4 * seqs * span * span * 160
    far = 4 * seqs * span * FPAD * 300
    (state,) = attention_call(
        state_kernel, meta, [qkv, seg_row, feat_c, rows_c, align_c], "sqccc", [(st, "q")], far
    )
    mine = pick(is0, half_columns(gw, uw, 0, n_main, n_mid), half_columns(gw, uw, 1, n_main, n_mid))
    theirs = pick(is0, half_columns(gw, uw, 1, n_main, n_mid), half_columns(gw, uw, 0, n_main, n_mid))
    got = swap(after(theirs, xs[6][0], xs[7][0]), "col")
    got = after(got, state)
    gu_rows = jnp.concatenate([pick(is0, mine, got), pick(is0, got, mine)], 0)
    w_gu = lax.all_gather(gu_rows, "row", axis=0, tiled=True)
    down0 = dw[: n_main + n_mid]
    down1 = jnp.concatenate([dw[n_main + 2 * n_mid :], dw[n_main + n_mid : n_main + 2 * n_mid]], 0)
    d_mine, d_theirs = pick(is0, down0, down1), pick(is0, down1, down0)
    d_got = swap(after(d_theirs, got), "col")
    d_cols = jnp.stack([pick(is0, d_mine, d_got), pick(is0, d_got, d_mine)])
    w_down = lax.all_gather(d_cols, "row", axis=0, tiled=True)
    fold = shards // 8
    w_down = (
        w_down.reshape(8, fold, half_ff, D // shards).transpose(0, 2, 1, 3).reshape(8, half_ff, D // 8)
    )

    num, den_in = attention_call(
        intra_kernel, meta, [qkv, seg_row, align_c], "sqc",
        [(sds((seqs, span, 256), F32), "q"), (sds((seqs, span, 8), F32), "q")], near,
    )
    forth = walk_steps(state, lambda d: same(row - d, here), lambda d: same(row - d, before), True)
    next(forth)
    state_in = finish(forth, [num])
    o, den = attention_call(
        output_kernel, meta, [qkv, seg_row, feat_c, rows_c, align_c, num, den_in, state_in], "sqcccqqq",
        [(sds((8, seqs, sub, 256), BF16), "s"), (sds((seqs, span, 8), F32), "q")], far,
        [ups[6][0], ups[7][0], d_got],
    )
    o_rows = o.reshape(8, tokens, 256)
    residual, a2_own = row_call(
        residual_kernel, scatter8(parts_call(o_rows, w_proj, "nn", mib=28)), [x, gain_two], [F32, BF16]
    )

    a2 = gather8(a2_own)
    ff_flops = 2 * every * D * half_ff
    gu, h, h_turned = slot_call(
        ffn_in_kernel, a2, [(w_gu, False)],
        [
            sds((8, tokens, ff), BF16),
            sds((8, tokens, half_ff + n_mid), BF16),
            sds((8, half_ff + n_mid, tokens), BF16),
        ],
        2 * ff_flops,
    )
    (down_g,) = grad_call(
        down_grad_kernel, ups, 256, [h_turned], [],
        [(sds((8, half_ff, 256), BF16), (1, half_ff, 256), lambda i: (i, 0, 0))], ff_flops,
    )
    (dgu,) = slot_call(
        ffn_back_kernel, ups, [(w_down, False), (gu, True)], [sds((8, tokens, ff), BF16)], ff_flops, [down_g],
    )
    down_g = (
        down_g.reshape(8, half_ff, fold, D // shards).transpose(0, 2, 1, 3).reshape(shards * half_ff, -1)
    )
    down_g = lax.psum_scatter(down_g, "row", scatter_dimension=0, tiled=True)
    block = D // shards
    gu_gs, gains = [], []

    def gu_half(x_bit):
        def run(sent):
            one, gain = grad_call(
                gu_grad_kernel, a2, 256, [dgu], [(w_gu, (256, ff), lambda i: (2 * i + x_bit, 0))],
                [
                    (sds((D // 2, ff), BF16), (256, ff), lambda i: (i, 0)),
                    (sds((D // 2, 128), F32), (256, 128), lambda i: (i, 0)),
                ],
                ff_flops, lambda i: 2 * i + x_bit, 4, sent,
            )
            gu_gs.append(one)
            gains.append(gain)
            return [one]

        return run

    grad_r, datt_own = row_call(
        residual_back_kernel, scatter8(parts_call(dgu, w_gu, "nt"), gu_half(0), gu_half(1)),
        [upstream.reshape(tokens, D), residual, gain_two], [F32, BF16],
    )
    gain_part = jnp.stack([g.reshape(4, 256, 128) for g in gains], 1).reshape(D, 128)
    if fold > 1:
        natural = jnp.stack([g.reshape(4, 256, ff) for g in gu_gs], 1)
        by_col = natural.reshape(rows, 2, block, ff).transpose(1, 0, 2, 3)
        gu_gs = [by_col[0].reshape(D // 2, ff), by_col[1].reshape(D // 2, ff)]
    gu_r = [lax.psum_scatter(g, "row", scatter_dimension=0, tiled=True) for g in gu_gs]

    late = {}

    def down_side(own):
        late["out"] = parts_call(h, w_down, "blocks", [own])
        return late["out"][0]

    datt = gather8(datt_own, down_side)
    (do,) = slot_call(
        do_kernel, datt, [(w_proj, False)], [sds((8, tokens, 256), BF16)], 2 * every * D * 256,
        [down_g, late["out"][0]],
    )
    do = do.reshape(8, seqs, sub, 256)

    (dstate,) = attention_call(
        back_state_kernel, meta, [qkv, seg_row, feat_c, rows_c, align_c, o, do, den], "sqcccssq",
        [(st, "q")], far,
    )
    part = sds((seqs, span, 256), F32)

    back = walk_steps(
        dstate,
        lambda d: same(row + d - 1, before) * (row + d < rows),
        lambda d: same(row + d - 1, here) * (row + d < rows),
        False,
    )
    _, came = next(back)
    down_steps = scatter_steps(late["out"])
    dq, dk, dv = attention_call(
        back_intra_kernel, meta, [qkv, seg_row, feat_c, rows_c, align_c, o, do, den, state_in],
        "sqcccssqq", [(part, "q")] * 3, 3 * near + far, next(down_steps),
    )
    sent = down_steps.send([dq, came])
    now, _ = back.send([dq])
    (proj_g,) = grad_call(
        proj_grad_kernel, datt, 1024, [o_rows], [],
        [(sds((256, D), BF16), (256, 1024), lambda i: (0, i))], 2 * every * D * 256, deps=[*sent, now, gu_r[0]],
    )
    (outputs,) = row_call(output_rows_kernel, finish(down_steps, [proj_g]), [residual], [BF16])
    dstate_out = finish(back, [proj_g])
    proj_r = lax.psum_scatter(proj_g, "row", scatter_dimension=0, tiled=True)
    project_grad = lax.ppermute(proj_r, ("row", "col"), [(b, a) for a, b in shard_pairs]).astype(F32)
    row_out = sds((8, seqs, sub, PAYLOAD), BF16)
    dqkv, scaled = attention_call(
        back_output_kernel, meta, [qkv, seg_row, feat_c, rows_c, align_c, dstate_out, dq, dk, dv, inv],
        "sqcccqqqqs", [(row_out, "s")] * 2, 2 * far, [outputs, gu_r[1]],
    )
    down_g = down_g.reshape(2, half_ff, D // shards)
    d_keep, d_send = pick(is0, down_g[0], down_g[1]), pick(is0, down_g[1], down_g[0])
    d_got = swap(d_send, "col")
    d0, d1 = pick(is0, d_keep, d_got).astype(F32), pick(is0, d_got, d_keep).astype(F32)
    down_grad = jnp.concatenate([d0, d1[n_main:], d1[:n_main]], 0)
    g_keep = pick(is0, gu_r[0], gu_r[1])
    g_got = swap(pick(is0, gu_r[1], gu_r[0]), "col")
    g0, g1 = pick(is0, g_keep, g_got).astype(F32), pick(is0, g_got, g_keep).astype(F32)
    m = 2 * n_main
    gate_grad = jnp.concatenate(
        [g0[:, :n_main], g0[:, m : m + n_mid], g1[:, m : m + n_mid], g1[:, :n_main]], 1
    )
    up_grad = jnp.concatenate(
        [g0[:, n_main:m], g0[:, m + n_mid :], g1[:, m + n_mid :], g1[:, n_main:m]], 1
    )

    def qkv_side(sent):
        (late["qkv"],) = grad_call(
            qkv_grad_kernel, xs, 512, [scaled.reshape(8, tokens, PAYLOAD)],
            [(gain_part, (512, 128), lambda i: (i, 0))],
            [
                (
                    sds((rows, 4, 2 * n_rows, PAYLOAD), BF16),
                    (rows, 1, 2 * n_rows, PAYLOAD),
                    lambda i: (0, i, 0, 0),
                )
            ],
            2 * every * D * PAYLOAD, deps=sent,
        )
        return [late["qkv"]]

    f_parts = parts_call(dqkv.reshape(8, tokens, PAYLOAD), w_qkv, "nt", [gate_grad, up_grad, down_grad], 28)
    f_pieces = scatter8(f_parts, qkv_side)
    qkv_g = late["qkv"]
    (inputs_grad,) = row_call(input_back_kernel, f_pieces, [x, grad_r], [F32])
    qkv_g = lax.psum_scatter(qkv_g.reshape(D, PAYLOAD), "row", scatter_dimension=0, tiled=True)
    qkv_g = lax.all_to_all(
        qkv_g.reshape(8, n_rows, PAYLOAD), GROUP, split_axis=0, concat_axis=0, tiled=True
    ).astype(F32)
    per_row = qkv_g.transpose(1, 0, 2)
    v_g = per_row[:, :, :256].reshape(n_rows, -1)
    q_g = per_row[:, :, 256:288].reshape(n_rows, -1)
    k_g = per_row[:, :, 288:320].reshape(n_rows, -1)
    forward_grad = jnp.sum(per_row[:, :, 320], 1) / fgain.astype(F32)
    attend_grad = (
        jnp.sum(v_g * vw.astype(F32), 1) + jnp.sum(q_g * qw.astype(F32), 1) + jnp.sum(k_g * kw.astype(F32), 1)
    )

    return (
        outputs.reshape(inputs.shape),
        inputs_grad.reshape(inputs.shape),
        q_g * gain_one,
        k_g * gain_one,
        v_g * gain_one,
        project_grad,
        attend_grad,
        gate_grad,
        up_grad,
        down_grad,
        forward_grad,
    )


def solution(mesh):
    heads, shards = mesh.devices.shape
    fine = Mesh(mesh.devices.reshape(heads // 2, 2, shards // 2, 2), ("hi", "core", "row", "col"))
    h, s = ("hi", "core"), ("row", "col")
    every = P(h + s)
    tokens = P(None, s, h)
    return jax.shard_map(
        body,
        mesh=fine,
        in_specs=(
            tokens, P(None, s), every, every, every, every, every, P(s, h), P(s, h), P(h, s), every, tokens,
        ),
        out_specs=(
            tokens, tokens, every, every, every, every, every, P(s, h), P(s, h), P(h, s), every,
        ),
        check_vma=False,
    )
```

time: 837 us -> 688 us (0.82)
  Pallas kernels: 44 us -> 206 us
  matrix products: 135 us -> 0 us
  waiting for transfers between devices: 307 us -> 186 us
  local copies, waits for them, and re-layouts: 147 us -> 93.2 us
  blocking collectives: 11.2 us -> 0 us
  starting transfers between devices: 93.3 us -> 104 us
    pallas_call x6 -> x44, Pallas kernels: 44 us -> 206 us  [the longest x5 56.9 us: grad_call(): pl.pallas_call(wrapped, grid=(steps or width // tile,), in_specs=[pl.Bloc...]
    dot_general x12 -> x0, matrix products: 135 us -> none  [the longest x4 49.5 us: t_dot(): lax.dot_general(a, b, (((0,), (0,)), ((), ())), preferred_element_type=F32)]
    reduce_scatter x3 -> x5, waiting for transfers between devices: 77.3 us -> 16.9 us  [the longest x1 12.2 us: body(): lax.psum_scatter(qkv_g.reshape(D, PAYLOAD), 'row', scatter_dimension=0, t...]
    convert_element_type x18 -> x28, other arithmetic: 9.93 us -> 44.4 us  [the longest x4 9.4 us: scatter_steps(): far_x = (both(x, xc, half, n) + from_y.astype(F32)).astype(BF16)]
    ppermute x7 -> x5, waiting for transfers between devices: 56.5 us -> 28.5 us  [the longest x4 20.2 us: walk_steps(): came = lax.ppermute(now, 'row', pairs)]
    slice x26 -> x4, local copies, waits for them, and re-layouts: 28.4 us -> 2.72 us  [the longest x1 1 us: body(): g1[:, n_main:m]]
    add x9 -> x2, other arithmetic: 25.8 us -> 2.56 us  [walk_steps(): total = term if total is None else total + term]
    unnamed x9, waiting for transfers between devices: 20.8 us -> 0.15 us
  transfers between devices with their start and end apart: 94 -> 98, of which waited for: 30 -> 34; matrix products, arithmetic and copies ran while one was open for 31% -> 13% of each run, Pallas kernels for 5% -> 30%
where the time goes in v2:
time: 688 us; the launch traced here: 675 us
  Pallas kernels  206 us (30%)
  waiting for transfers between devices  186 us (27%)
  starting transfers between devices  104 us (15%)
  local copies, waits for them, and re-layouts  93.2 us (14%)
  other arithmetic  69.8 us (10%)
  between operations  15.9 us (2%)
    ppermute x81, waiting for transfers between devices, swap(): return lax.ppermute(value, axis, [(0, 1), (1, 0)])  134 us
    unnamed x304, local copies, waits for them, and re-layouts  63.8 us
    pallas_call x5, Pallas kernels, grad_call(): pl.pallas_call(wrapped, grid=(steps or width // tile,), in_specs=[pl.Bloc...  56.9 us
    ppermute x81, starting transfers between devices, swap(): return lax.ppermute(value, axis, [(0, 1), (1, 0)])  55.2 us
    pallas_call x4, Pallas kernels, slot_call(): pl.pallas_call(wrapped, grid=(8,), in_specs=[pl.BlockSpec(memory_space=pl...  52.8 us
    pallas_call x6, Pallas kernels, attention_call(): pl.pallas_call(wrapped, out_shape=[jax.ShapeDtypeStruct(a.shape, a.dtype)...  42.3 us
    pallas_call x4, Pallas kernels, parts_call(): pl.pallas_call(kernel, grid=(width // tile,), in_specs=[pl.BlockSpec(a.sh...  39.6 us
    ppermute x4, starting transfers between devices, walk_steps(): came = lax.ppermute(now, 'row', pairs)  33.1 us
  transfers between devices with their start and end apart: 98, of which 34 were waited for; matrix products, arithmetic and copies ran while one was open for 13% of the time, Pallas kernels for 30%

profile of v2, /device:TPU:16, one launch (start us, length us, event | category | flops | bytes accessed | tf_op | source)
XLA Modules:
  0.0 675.1 jit_solution(5893965821945269621)
XLA Ops:
  41.4 14.3 %collective-permute-done.4.refs_4_ = bf16[256,2048]{1,0:T(8,128)(2,1)} collective-permute-done((bf16[256,2048]{1,0:T(8,128)(2,1)}, bf16[256,2048]{1,0:T(8,128)(2,1)}, u32[]{:S(2)}, u32[]{:S(2)}) %collective-permute-start.4) | collective-permute-done | bytes 1048608 | tf_op jit(solution)/shard_map/ppermute | solution.py:70
  76.1 9.6 %qkv_kernel.1 = (bf16[8,256,384]{2,1,0:T(8,128)(2,1)}, f32[8,256,128]{2,1,0:T(8,128)}, bf16[2048,384]{1,0:T(8,128)(2,1)}) custom-call(bf16[256,2048]{1,0:T(8,128)(2,1)} %gate.22.refs_0_, bf16[256,2048]{1,0:T(8,128)(2,1)} %collective-permute-done.1.refs_1_, bf16[256,2048]{1,0:T(8,128)(2,1)} %collective-permute-done.2.refs_2_, ...), custom_call_target="tpu_custom_call" | custom-call | flops 3221225472 | bytes 14155776 | tf_op jit(solution)/shard_map/qkv_kernel/pallas_call | solution.py:218
  99.3 8.7 %collective-permute-start.11 = (bf16[4,2,160,128]{3,2,1,0:T(8,128)(2,1)S(1)}, bf16[4,2,160,128]{3,2,1,0:T(8,128)(2,1)}, u32[]{:S(2)}, u32[]{:S(2)}) collective-permute-start(bf16[4,2,160,128]{3,2,1,0:T(8,128)(2,1)S(1)} %copy-done.38), channel_id=1, source_target_pairs={{0,2},{2,4},{4,6},{1,3},{3,5},{5,7},{8,10},{10,12},{12,14},{9,11},... | collective-permute-start | bytes 983048 | tf_op jit(solution)/shard_map/ppermute | solution.py:149
  133.3 10.1 %collective-permute-done.12 = bf16[4,2,160,128]{3,2,1,0:T(8,128)(2,1)S(1)} collective-permute-done((bf16[4,2,160,128]{3,2,1,0:T(8,128)(2,1)}, bf16[4,2,160,128]{3,2,1,0:T(8,128)(2,1)S(1)}, u32[]{:S(2)}, u32[]{:S(2)}) %collective-permute-start.12) | collective-permute-done | bytes 327712 | tf_op jit(solution)/shard_map/ppermute | solution.py:149
  150.4 6.9 %output_kernel.1 = (bf16[8,4,64,256]{3,2,1,0:T(8,128)(2,1)S(1)}, f32[4,512,8]{2,1,0:T(8,128)S(1)}) custom-call(s32[9]{0:T(128)S(1)} %copy-done.72, bf16[8,4,64,384]{3,2,1,0:T(8,128)(2,1)S(1)} %bitcast.86, f32[4,1,512]{2,1,0:T(1,128)S(1)} %copy-done.66, bf16[128,512]{1,0:T(8,128)(2,1)S(1)} %copy-done.42, f32[8,512]{1,0:T(8,128)S(1)} %copy-done.64, ...), custom_call_target="tpu_custom_call" | custom-call | flops 629145600 | bytes 5791744 | tf_op jit(solution)/shard_map/output_kernel/pallas_call | solution.py:651
  176.1 10.6 %collective-permute-done.26 = bf16[128,2048]{1,0:T(8,128)(2,1)} collective-permute-done((bf16[128,2048]{1,0:T(8,128)(2,1)}, bf16[128,2048]{1,0:T(8,128)(2,1)}, u32[]{:S(2)}, u32[]{:S(2)}) %collective-permute-start.26) | collective-permute-done | bytes 524320 | tf_op jit(solution)/shard_map/ppermute | solution.py:70
  196.5 7.4 %collective-permute-done.27.refs_4_ = bf16[128,2048]{1,0:T(8,128)(2,1)S(1)} collective-permute-done((bf16[128,2048]{1,0:T(8,128)(2,1)S(1)}, bf16[128,2048]{1,0:T(8,128)(2,1)S(1)}, u32[]{:S(2)}, u32[]{:S(2)}) %collective-permute-start.27) | collective-permute-done | bytes 524320 | tf_op jit(solution)/shard_map/ppermute | solution.py:70
  203.9 9.5 %collective-permute-done.21.refs_2_ = bf16[128,2048]{1,0:T(8,128)(2,1)S(1)} collective-permute-done((bf16[128,2048]{1,0:T(8,128)(2,1)S(1)}, bf16[128,2048]{1,0:T(8,128)(2,1)S(1)}, u32[]{:S(2)}, u32[]{:S(2)}) %collective-permute-start.21) | collective-permute-done | bytes 524320 | tf_op jit(solution)/shard_map/ppermute | solution.py:70
  221.4 21.1 %collective-permute-done.32.refs_4_ = bf16[256,2048]{1,0:T(8,128)(2,1)S(1)} collective-permute-done((bf16[256,2048]{1,0:T(8,128)(2,1)S(1)}, bf16[256,2048]{1,0:T(8,128)(2,1)S(1)}, u32[]{:S(2)}, u32[]{:S(2)}) %collective-permute-start.32) | collective-permute-done | bytes 1048608 | tf_op jit(solution)/shard_map/ppermute | solution.py:70
  245.6 11.6 %collective-permute-done.35.refs_7_ = bf16[128,2048]{1,0:T(8,128)(2,1)S(1)} collective-permute-done((bf16[128,2048]{1,0:T(8,128)(2,1)S(1)}, bf16[128,2048]{1,0:T(8,128)(2,1)S(1)}, u32[]{:S(2)}, u32[]{:S(2)}) %collective-permute-start.35) | collective-permute-done | bytes 524320 | tf_op jit(solution)/shard_map/ppermute | solution.py:70
  262.2 20.9 %ffn_in_kernel.1 = (bf16[8,256,1408]{2,1,0:T(8,128)(2,1)}, bf16[8,256,768]{2,1,0:T(8,128)(2,1)}, bf16[8,768,256]{2,1,0:T(8,128)(2,1)}) custom-call(bf16[256,2048]{1,0:T(8,128)(2,1)} %copy-done.62, bf16[256,2048]{1,0:T(8,128)(2,1)} %copy-done.122, bf16[256,2048]{1,0:T(8,128)(2,1)} %copy-done.97, bf16[256,2048]{1,0:T(8,128)(2,1)} %copy-done.124, ...), custom_call_target="tpu_custom_call" | custom-call | flops 11811160064 | bytes 26214400 | tf_op jit(solution)/shard_map/ffn_in_kernel/pallas_call | solution.py:218
  283.2 13.1 %down_grad_kernel.1.refs_12_ = bf16[8,704,256]{2,1,0:T(8,128)(2,1)} custom-call(bf16[256,2048]{1,0:T(8,128)(2,1)} %gate.24.refs_0_, bf16[256,2048]{1,0:T(8,128)(2,1)} %collective-permute-done.38.refs_1_, bf16[256,2048]{1,0:T(8,128)(2,1)} %collective-permute-done.13.refs_2_, bf16[256,2048]{1,0:T(8,128)(2,1)} %collective-permute-done.39.refs_3_, ...), custom_call_target="tpu_custom_call" | custom-call | flops 5905580032 | bytes 14417920 | tf_op jit(solution)/shard_map/down_grad_kernel/pallas_call | solution.py:246
  296.5 14.8 %ffn_back_kernel.1.a_ref.refs_10_ = bf16[8,256,1408]{2,1,0:T(8,128)(2,1)} custom-call(bf16[256,2048]{1,0:T(8,128)(2,1)} %gate.24.refs_0_, bf16[256,2048]{1,0:T(8,128)(2,1)} %collective-permute-done.38.refs_1_, bf16[256,2048]{1,0:T(8,128)(2,1)} %collective-permute-done.13.refs_2_, bf16[256,2048]{1,0:T(8,128)(2,1)} %collective-permute-done.39.refs_3_, ...), custom_call_target="tpu_custom_call" | custom-call | flops 5905580032 | bytes 22806528 | tf_op jit(solution)/shard_map/ffn_back_kernel/pallas_call | solution.py:218
  311.3 17.9 %parts_nt.2 = (bf16[256,2048]{1,0:T(8,128)(2,1)}, bf16[256,2048]{1,0:T(8,128)(2,1)}, bf16[256,2048]{1,0:T(8,128)(2,1)}, bf16[256,2048]{1,0:T(8,128)(2,1)}, bf16[...) custom-call(bf16[8,256,1408]{2,1,0:T(8,128)(2,1)} %ffn_back_kernel.1.a_, ...), custom_call_target="tpu_custom_call" | custom-call | flops 11811160064 | bytes 19922944 | tf_op jit(solution)/shard_map/parts_nt/pallas_call | solution.py:434
  337.1 13.6 %gu_grad_kernel.2 = (bf16[1024,1408]{1,0:T(8,128)(2,1)}, f32[1024,128]{1,0:T(8,128)}) custom-call(bf16[256,2048]{1,0:T(8,128)(2,1)} %copy-done.62, bf16[256,2048]{1,0:T(8,128)(2,1)} %copy-done.122, bf16[256,2048]{1,0:T(8,128)(2,1)} %copy-done.97, bf16[256,2048]{1,0:T(8,128)(2,1)} %copy-done.124, bf16[256,2048]{1,0:T(8,128)(2,1)} %copy-done.96, ...), custom_call_target="tpu_custom_call" | custom-call | flops 5905580032 | bytes 23330816 | tf_op jit(solution)/shard_map/gu_grad_kernel/pallas_call | solution.py:246
  355.8 10.8 %collective-permute-done.48.refs_0_ = bf16[128,2048]{1,0:T(8,128)(2,1)} collective-permute-done((bf16[128,2048]{1,0:T(8,128)(2,1)S(1)}, bf16[128,2048]{1,0:T(8,128)(2,1)}, u32[]{:S(2)}, u32[]{:S(2)}) %collective-permute-start.48) | collective-permute-done | bytes 524320 | tf_op jit(solution)/shard_map/ppermute | solution.py:70
  373.7 13.5 %gu_grad_kernel.3 = (bf16[1024,1408]{1,0:T(8,128)(2,1)}, f32[1024,128]{1,0:T(8,128)}) custom-call(bf16[256,2048]{1,0:T(8,128)(2,1)} %copy-done.62, bf16[256,2048]{1,0:T(8,128)(2,1)} %copy-done.122, bf16[256,2048]{1,0:T(8,128)(2,1)} %copy-done.97, bf16[256,2048]{1,0:T(8,128)(2,1)} %copy-done.124, bf16[256,2048]{1,0:T(8,128)(2,1)} %copy-done.96, ...), custom_call_target="tpu_custom_call" | custom-call | flops 5905580032 | bytes 23330816 | tf_op jit(solution)/shard_map/gu_grad_kernel/pallas_call | solution.py:246
  403.3 11.1 %parts_blocks.1 = (bf16[256,2048]{1,0:T(8,128)(2,1)}, bf16[256,2048]{1,0:T(8,128)(2,1)}, bf16[256,2048]{1,0:T(8,128)(2,1)}, bf16[256,2048]{1,0:T(8,128)(2,1)}, b...) custom-call(bf16[8,256,768]{2,1,0:T(8,128)(2,1)} %get-tuple-element., ...), custom_call_target="tpu_custom_call" | custom-call | flops 5905580032 | bytes 14417920 | tf_op jit(solution)/shard_map/parts_blocks/pallas_call | solution.py:434
  415.0 11.5 %collective-permute-done.60.refs_0_ = bf16[256,2048]{1,0:T(8,128)(2,1)} collective-permute-done((bf16[256,2048]{1,0:T(8,128)(2,1)}, bf16[256,2048]{1,0:T(8,128)(2,1)}, u32[]{:S(2)}, u32[]{:S(2)}) %collective-permute-start.60) | collective-permute-done | bytes 1048608 | tf_op jit(solution)/shard_map/ppermute | solution.py:70
  437.1 5.1 collective-permute-done.65.refs_7_
  452.6 7.6 %do_kernel.1 = bf16[8,256,256]{2,1,0:T(8,128)(2,1)} custom-call(bf16[256,2048]{1,0:T(8,128)(2,1)} %get-tuple-element.94.refs_0_, bf16[256,2048]{1,0:T(8,128)(2,1)} %copy-done.91, bf16[256,2048]{1,0:T(8,128)(2,1)} %gate.32.refs_2_, bf16[256,2048]{1,0:T(8,128)(2,1)} %copy-done.92, bf16[256,2048]{1,0:T(8,128)(2,1)} %gate.33.refs_4_, ...), custom_call_target="tpu_custom_call" | custom-call | flops 2147483648 | bytes 10485760 | tf_op jit(solution)/shard_map/do_kernel/pallas_call | solution.py:218
  462.7 5.3 back_state_kernel.1
  467.9 21.5 %collective-permute-start.68 = (bf16[4,2,160,128]{3,2,1,0:T(8,128)(2,1)S(1)}, bf16[4,2,160,128]{3,2,1,0:T(8,128)(2,1)S(1)}, u32[]{:S(2)}, u32[]{:S(2)}) collective-permute-start(bf16[4,2,160,128]{3,2,1,0:T(8,128)(2,1)S(1)} %back_state_kernel.1), channel_id=1, source_target_pairs={{2,0},{4,2},{6,4},{3,1},{5,3},{7,5},{10,8},{12,10},{14,12},{11,9},... | collective-permute-start | bytes 983048 | tf_op jit(solution)/shard_map/ppermute | solution.py:149
  490.3 13.1 %back_intra_kernel.1 = (f32[4,512,256]{2,1,0:T(8,128)S(1)}, f32[4,512,256]{2,1,0:T(8,128)S(1)}, f32[4,512,256]{2,1,0:T(8,128)S(1)}) custom-call(s32[9]{0:T(128)S(1)} %copy-done.73, bf16[8,4,64,384]{3,2,1,0:T(8,128)(2,1)S(1)} %bitcast.88, f32[4,1,512]{2,1,0:T(1,128)S(1)} %copy-done.67, bf16[128,512]{1,0:T(8,128)(2,1)S(1)} %copy-done.42, ...), custom_call_target="tpu_custom_call" | custom-call | flops 2642411520 | bytes 10969088 | tf_op jit(solution)/shard_map/back_intra_kernel/pallas_call | solution.py:651
  522.0 5.1 collective-permute-done.73.refs_0_
  534.3 7.2 %proj_grad_kernel.1.refs_1_ = bf16[256,2048]{1,0:T(8,128)(2,1)} custom-call(bf16[256,2048]{1,0:T(8,128)(2,1)} %get-tuple-element.94.refs_0_, bf16[256,2048]{1,0:T(8,128)(2,1)} %copy-done.91, bf16[256,2048]{1,0:T(8,128)(2,1)} %gate.32.refs_2_, bf16[256,2048]{1,0:T(8,128)(2,1)} %copy-done.92, bf16[256,2048]{1,0:T(8,128)(2,1)} %gate.33.refs_4_, ...), custom_call_target="tpu_custom_call" | custom-call | flops 2147483648 | bytes 10485760 | tf_op jit(solution)/shard_map/proj_grad_kernel/pallas_call | solution.py:246
  550.8 7.3 %back_output_kernel.1 = (bf16[8,4,64,384]{3,2,1,0:T(8,128)(2,1)S(1)}, bf16[8,4,64,384]{3,2,1,0:T(8,128)(2,1)S(1)}) custom-call(s32[9]{0:T(128)S(1)} %copy-done.74, bf16[8,4,64,384]{3,2,1,0:T(8,128)(2,1)S(1)} %bitcast.89, f32[4,1,512]{2,1,0:T(1,128)S(1)} %copy-done.68, bf16[128,512]{1,0:T(8,128)(2,1)S(1)} %copy-done.42, f32[8,512]{1,0:T(8,128)S(1)} %copy-done.64, ...), custom_call_target="tpu_custom_call" | custom-call | flops 1258291200 | bytes 13000704 | tf_op jit(solution)/shard_map/back_output_kernel/pallas_call | solution.py:651
  571.9 6.4 parts_nt.3
  591.7 9.5 %qkv_grad_kernel.1.refs_1_ = bf16[4,4,128,384]{3,2,1,0:T(8,128)(2,1)} custom-call(bf16[256,2048]{1,0:T(8,128)(2,1)} %gate.22.refs_0_, bf16[256,2048]{1,0:T(8,128)(2,1)} %collective-permute-done.1.refs_1_, bf16[256,2048]{1,0:T(8,128)(2,1)} %collective-permute-done.2.refs_2_, bf16[256,2048]{1,0:T(8,128)(2,1)} %collective-permute-done.3.refs_3_, ...), custom_call_target="tpu_custom_call" | custom-call | flops 3221225472 | bytes 12582912 | tf_op jit(solution)/shard_map/qkv_grad_kernel/pallas_call | solution.py:246
  627.0 8.2 %collective-permute-done.86 = bf16[64,2048]{1,0:T(8,128)(2,1)S(1)} collective-permute-done((bf16[64,2048]{1,0:T(8,128)(2,1)}, bf16[64,2048]{1,0:T(8,128)(2,1)S(1)}, u32[]{:S(2)}, u32[]{:S(2)}) %collective-permute-start.86) | collective-permute-done | bytes 262176 | tf_op jit(solution)/shard_map/ppermute | solution.py:886
  636.9 12.2 %reduce-scatter.12.cloned.1.call-done = bf16[512,384]{1,0:T(8,128)(2,1)} async-done(((bf16[2048,384]{1,0:T(8,128)(2,1)}), bf16[512,384]{1,0:T(8,128)(2,1)}) %reduce-scatter.12.cloned.1.call-update) | async-done | bytes 393232 | tf_op jit(solution)/shard_map/reduce_scatter | solution.py:927
  649.1 5.6 all-to-all-start.1
  (616 shorter events, 308.1 us)
Async XLA Ops:
  27.3 45.6 %all-gather.12.cloned.1.call-start = ((), (), s32[]{:S(2)}) async-start(), calls=%async_computation.15 | async-start | bytes 1966080 | tf_op jit(solution)/shard_map/all_gather | solution.py:724
  30.0 130.0 %all-gather.6.cloned.1.call-start = ((), (), s32[]{:S(2)}) async-start(), calls=%async_computation.7 | async-start | bytes 1310720 | tf_op jit(solution)/shard_map/all_gather | solution.py:723
  30.0 25.7 %collective-permute-start.4 = (bf16[256,2048]{1,0:T(8,128)(2,1)}, bf16[256,2048]{1,0:T(8,128)(2,1)}, u32[]{:S(2)}, u32[]{:S(2)}) collective-permute-start(bf16[256,2048]{1,0:T(8,128)(2,1)} %gate.22.refs_0_), channel_id=1, source_target_pairs={{0,1},{1,0},{2,3},{3,2},{4,5},{5,4},{6,7},{7,6},{8,9},{9,8},{10,11... | collective-permute-start | bytes 3145736 | tf_op jit(solution)/shard_map/ppermute | solution.py:70
  33.7 25.4 %collective-permute-start.2 = (bf16[256,2048]{1,0:T(8,128)(2,1)}, bf16[256,2048]{1,0:T(8,128)(2,1)}, u32[]{:S(2)}, u32[]{:S(2)}) collective-permute-start(bf16[256,2048]{1,0:T(8,128)(2,1)} %gate.22.refs_0_), channel_id=1, source_target_pairs={{0,16},{16,0},{1,17},{17,1},{2,18},{18,2},{3,19},{19,3},{4,20},{20... | collective-permute-start | bytes 3145736 | tf_op jit(solution)/shard_map/ppermute | solution.py:70
  35.4 28.2 %collective-permute-start.10 = (s32[4,256]{1,0:T(4,128)}, s32[4,256]{1,0:T(4,128)S(1)}, u32[]{:S(2)}, u32[]{:S(2)}) collective-permute-start(s32[4,256]{1,0:T(4,128)} %reshape.291), channel_id=1, source_target_pairs={{0,1},{1,0},{2,3},{3,2},{4,5},{5,4},{6,7},{7,6},{8,9},{9,8},{10,11... | collective-permute-start | bytes 12296 | tf_op jit(solution)/shard_map/ppermute | solution.py:70
  41.4 32.5 %collective-permute-start.1 = (bf16[256,2048]{1,0:T(8,128)(2,1)S(1)}, bf16[256,2048]{1,0:T(8,128)(2,1)}, u32[]{:S(2)}, u32[]{:S(2)}) collective-permute-start(bf16[256,2048]{1,0:T(8,128)(2,1)S(1)} %copy-done.80), channel_id=1, source_target_pairs={{0,8},{8,0},{1,9},{9,1},{2,10},{10,2},{3,11},{11,3},{4,12},{12,4},... | collective-permute-start | bytes 3145736 | tf_op jit(solution)/shard_map/ppermute | solution.py:70
  65.5 196.8 %all-gather.8.cloned.1.call-start = ((), (), s32[]{:S(2)}) async-start(), calls=%async_computation.8 | async-start | bytes 7208960 | tf_op jit(solution)/shard_map/all_gather | solution.py:765
  96.5 200.0 %all-gather.10.cloned.1.call-start = ((), (), s32[]{:S(2)}) async-start(), calls=%async_computation.9 | async-start | bytes 3604480 | tf_op jit(solution)/shard_map/all_gather | solution.py:771
  97.9 28.8 %collective-permute-start.15 = (bf16[256,2048]{1,0:T(8,128)(2,1)}, bf16[256,2048]{1,0:T(8,128)(2,1)}, u32[]{:S(2)}, u32[]{:S(2)}) collective-permute-start(bf16[256,2048]{1,0:T(8,128)(2,1)} %gate.24.refs_0_), channel_id=1, source_target_pairs={{0,1},{1,0},{2,3},{3,2},{4,5},{5,4},{6,7},{7,6},{8,9},{9,8},{10,11... | collective-permute-start | bytes 3145736 | tf_op jit(solution)/shard_map/ppermute | solution.py:70
  98.5 30.0 %collective-permute-start.13 = (bf16[256,2048]{1,0:T(8,128)(2,1)}, bf16[256,2048]{1,0:T(8,128)(2,1)}, u32[]{:S(2)}, u32[]{:S(2)}) collective-permute-start(bf16[256,2048]{1,0:T(8,128)(2,1)} %gate.24.refs_0_), channel_id=1, source_target_pairs={{0,16},{16,0},{1,17},{17,1},{2,18},{18,2},{3,19},{19,3},{4,20},{20... | collective-permute-start | bytes 3145736 | tf_op jit(solution)/shard_map/ppermute | solution.py:70
  175.4 277.1 %reduce-scatter.6.cloned.1.call-start = ((), (), s32[]{:S(2)}) async-start(), calls=%async_computation.10 | async-start | bytes 3604480 | tf_op jit(solution)/shard_map/reduce_scatter | solution.py:815
  221.4 36.8 %collective-permute-start.29 = (bf16[256,2048]{1,0:T(8,128)(2,1)S(1)}, bf16[256,2048]{1,0:T(8,128)(2,1)S(1)}, u32[]{:S(2)}, u32[]{:S(2)}) collective-permute-start(bf16[256,2048]{1,0:T(8,128)(2,1)S(1)} %get-tuple-element.79.refs_0_), channel_id=1, source_target_pairs={{0,8},{8,0},{1,9},{9,1},{2,10},{10,2},{3,11},{11,3},{4,12},{12,4},... | collective-permute-start | bytes 3145736 | tf_op jit(solution)/shard_map/ppermute | solution.py:70
  296.3 232.2 %reduce-scatter.8.cloned.1.call-start = ((), (), s32[]{:S(2)}) async-start(), calls=%async_computation.11 | async-start | bytes 3604480 | tf_op jit(solution)/shard_map/reduce_scatter | solution.py:844
  350.8 177.7 %reduce-scatter.10.cloned.1.call-start = ((), (), s32[]{:S(2)}) async-start(), calls=%async_computation.12 | async-start | bytes 3604480 | tf_op jit(solution)/shard_map/reduce_scatter | solution.py:844
  354.1 36.1 %collective-permute-start.43 = (bf16[256,2048]{1,0:T(8,128)(2,1)}, bf16[256,2048]{1,0:T(8,128)(2,1)}, u32[]{:S(2)}, u32[]{:S(2)}) collective-permute-start(bf16[256,2048]{1,0:T(8,128)(2,1)} %get-tuple-element.84), channel_id=1, source_target_pairs={{0,8},{8,0},{1,9},{9,1},{2,10},{10,2},{3,11},{11,3},{4,12},{12,4},... | collective-permute-start | bytes 3145736 | tf_op jit(solution)/shard_map/ppermute | solution.py:70
  354.1 36.1 %collective-permute-start.45 = (bf16[128,2048]{1,0:T(8,128)(2,1)}, bf16[128,2048]{1,0:T(8,128)(2,1)}, u32[]{:S(2)}, u32[]{:S(2)}) collective-permute-start(bf16[128,2048]{1,0:T(8,128)(2,1)} %add_convert_fusion.17.refs_14_), channel_id=1, source_target_pairs={{0,1},{1,0},{2,3},{3,2},{4,5},{5,4},{6,7},{7,6},{8,9},{9,8},{10,11... | collective-permute-start | bytes 1572872 | tf_op jit(solution)/shard_map/ppermute | solution.py:70
  354.7 35.4 %collective-permute-start.52 = (bf16[128,2048]{1,0:T(8,128)(2,1)}, bf16[128,2048]{1,0:T(8,128)(2,1)}, u32[]{:S(2)}, u32[]{:S(2)}) collective-permute-start(bf16[128,2048]{1,0:T(8,128)(2,1)} %add_convert_fusion.14.refs_15_), channel_id=1, source_target_pairs={{0,16},{16,0},{1,17},{17,1},{2,18},{18,2},{3,19},{19,3},{4,20},{20... | collective-permute-start | bytes 1572872 | tf_op jit(solution)/shard_map/ppermute | solution.py:70
  387.3 221.4 %reduce-scatter.14.cloned.1.call-start = ((), (), s32[]{:S(2)}) async-start(), calls=%async_computation.14 | async-start | bytes 1310720 | tf_op jit(solution)/shard_map/reduce_scatter | solution.py:885
  401.8 26.6 %collective-permute-start.62 = (bf16[256,2048]{1,0:T(8,128)(2,1)}, bf16[256,2048]{1,0:T(8,128)(2,1)S(1)}, u32[]{:S(2)}, u32[]{:S(2)}) collective-permute-start(bf16[256,2048]{1,0:T(8,128)(2,1)} %get-tuple-element.94.refs_0_), channel_id=1, source_target_pairs={{0,1},{1,0},{2,3},{3,2},{4,5},{5,4},{6,7},{7,6},{8,9},{9,8},{10,11... | collective-permute-start | bytes 3145736 | tf_op jit(solution)/shard_map/ppermute | solution.py:70
  448.2 94.7 %collective-permute-start.53 = (bf16[256,2048]{1,0:T(8,128)(2,1)}, bf16[256,2048]{1,0:T(8,128)(2,1)}, u32[]{:S(2)}, u32[]{:S(2)}) collective-permute-start(bf16[256,2048]{1,0:T(8,128)(2,1)} %get-tuple-element.96), channel_id=1, source_target_pairs={{0,8},{8,0},{1,9},{9,1},{2,10},{10,2},{3,11},{11,3},{4,12},{12,4},... | collective-permute-start | bytes 3145736 | tf_op jit(solution)/shard_map/ppermute | solution.py:70
  448.7 94.3 %collective-permute-start.55 = (bf16[128,2048]{1,0:T(8,128)(2,1)}, bf16[128,2048]{1,0:T(8,128)(2,1)}, u32[]{:S(2)}, u32[]{:S(2)}) collective-permute-start(bf16[128,2048]{1,0:T(8,128)(2,1)} %add_convert_fusion.11.refs_12_), channel_id=1, source_target_pairs={{0,1},{1,0},{2,3},{3,2},{4,5},{5,4},{6,7},{7,6},{8,9},{9,8},{10,11... | collective-permute-start | bytes 1572872 | tf_op jit(solution)/shard_map/ppermute | solution.py:70
  450.0 57.4 %collective-permute-start.70 = (bf16[128,2048]{1,0:T(8,128)(2,1)}, bf16[128,2048]{1,0:T(8,128)(2,1)}, u32[]{:S(2)}, u32[]{:S(2)}) collective-permute-start(bf16[128,2048]{1,0:T(8,128)(2,1)} %get-tuple-element.186.refs_11_), channel_id=1, source_target_pairs={{0,16},{16,0},{1,17},{17,1},{2,18},{18,2},{3,19},{19,3},{4,20},{20... | collective-permute-start | bytes 1572872 | tf_op jit(solution)/shard_map/ppermute | solution.py:70
  452.1 58.6 %collective-permute-start.58 = (bf16[128,2048]{1,0:T(8,128)(2,1)}, bf16[128,2048]{1,0:T(8,128)(2,1)}, u32[]{:S(2)}, u32[]{:S(2)}) collective-permute-start(bf16[128,2048]{1,0:T(8,128)(2,1)} %get-tuple-element.187.refs_10_), channel_id=1, source_target_pairs={{0,1},{1,0},{2,3},{3,2},{4,5},{5,4},{6,7},{7,6},{8,9},{9,8},{10,11... | collective-permute-start | bytes 1572872 | tf_op jit(solution)/shard_map/ppermute | solution.py:70
  467.9 40.7 %collective-permute-start.68 = (bf16[4,2,160,128]{3,2,1,0:T(8,128)(2,1)S(1)}, bf16[4,2,160,128]{3,2,1,0:T(8,128)(2,1)S(1)}, u32[]{:S(2)}, u32[]{:S(2)}) collective-permute-start(bf16[4,2,160,128]{3,2,1,0:T(8,128)(2,1)S(1)} %back_state_kernel.1), channel_id=1, source_target_pairs={{2,0},{4,2},{6,4},{3,1},{5,3},{7,5},{10,8},{12,10},{14,12},{11,9},... | collective-permute-start | bytes 983048 | tf_op jit(solution)/shard_map/ppermute | solution.py:149
  507.4 35.6 %collective-permute-start.72 = (bf16[128,2048]{1,0:T(8,128)(2,1)}, bf16[128,2048]{1,0:T(8,128)(2,1)}, u32[]{:S(2)}, u32[]{:S(2)}) collective-permute-start(bf16[128,2048]{1,0:T(8,128)(2,1)} %add_convert_fusion.8.refs_13_), channel_id=1, source_target_pairs={{0,16},{16,0},{1,17},{17,1},{2,18},{18,2},{3,19},{19,3},{4,20},{20... | collective-permute-start | bytes 1572872 | tf_op jit(solution)/shard_map/ppermute | solution.py:70
  531.8 26.4 %collective-permute-start.74 = (bf16[256,1408]{1,0:T(8,128)(2,1)}, bf16[256,1408]{1,0:T(8,128)(2,1)}, u32[]{:S(2)}, u32[]{:S(2)}) collective-permute-start(bf16[256,1408]{1,0:T(8,128)(2,1)} %broadcast_select_fusion), channel_id=1, source_target_pairs={{0,1},{1,0},{2,3},{3,2},{4,5},{5,4},{6,7},{7,6},{8,9},{9,8},{10,11... | collective-permute-start | bytes 2162696 | tf_op jit(solution)/shard_map/ppermute | solution.py:70
  582.8 66.3 %reduce-scatter.12.cloned.1.call-start = ((), (), s32[]{:S(2)}) async-start(), calls=%async_computation.13 | async-start | bytes 1966080 | tf_op jit(solution)/shard_map/reduce_scatter | solution.py:927
  604.0 51.6 %collective-permute-start.76 = (bf16[256,2048]{1,0:T(8,128)(2,1)}, bf16[256,2048]{1,0:T(8,128)(2,1)}, u32[]{:S(2)}, u32[]{:S(2)}) collective-permute-start(bf16[256,2048]{1,0:T(8,128)(2,1)} %get-tuple-element.110), channel_id=1, source_target_pairs={{0,8},{8,0},{1,9},{9,1},{2,10},{10,2},{3,11},{11,3},{4,12},{12,4},... | collective-permute-start | bytes 3145736 | tf_op jit(solution)/shard_map/ppermute | solution.py:70
  608.7 26.6 %collective-permute-start.86 = (bf16[64,2048]{1,0:T(8,128)(2,1)}, bf16[64,2048]{1,0:T(8,128)(2,1)S(1)}, u32[]{:S(2)}, u32[]{:S(2)}) collective-permute-start(bf16[64,2048]{1,0:T(8,128)(2,1)} %reduce-scatter.14.cloned.1.call-done), channel_id=1, source_target_pairs={{0,0},{2,1},{4,2},{6,3},{1,4},{3,5},{5,6},{7,7},{8,8},{10,9},{12,1... | collective-permute-start | bytes 786440 | tf_op jit(solution)/shard_map/ppermute | solution.py:886
  610.6 45.0 %collective-permute-start.78 = (bf16[128,2048]{1,0:T(8,128)(2,1)}, bf16[128,2048]{1,0:T(8,128)(2,1)S(1)}, u32[]{:S(2)}, u32[]{:S(2)}) collective-permute-start(bf16[128,2048]{1,0:T(8,128)(2,1)} %add_convert_fusion.5.refs_14_), channel_id=1, source_target_pairs={{0,1},{1,0},{2,3},{3,2},{4,5},{5,4},{6,7},{7,6},{8,9},{9,8},{10,11... | collective-permute-start | bytes 1572872 | tf_op jit(solution)/shard_map/ppermute | solution.py:70
  616.3 39.3 %collective-permute-start.85 = (bf16[128,2048]{1,0:T(8,128)(2,1)}, bf16[128,2048]{1,0:T(8,128)(2,1)S(1)}, u32[]{:S(2)}, u32[]{:S(2)}) collective-permute-start(bf16[128,2048]{1,0:T(8,128)(2,1)} %add_convert_fusion.2.refs_15_), channel_id=1, source_target_pairs={{0,16},{16,0},{1,17},{17,1},{2,18},{18,2},{3,19},{19,3},{4,20},{20... | collective-permute-start | bytes 1572872 | tf_op jit(solution)/shard_map/ppermute | solution.py:70
  623.7 31.9 %collective-permute-start.84 = (bf16[128,2048]{1,0:T(8,128)(2,1)}, bf16[128,2048]{1,0:T(8,128)(2,1)}, u32[]{:S(2)}, u32[]{:S(2)}) collective-permute-start(bf16[128,2048]{1,0:T(8,128)(2,1)} %add_convert_fusion), channel_id=1, source_target_pairs={{0,1},{1,0},{2,3},{3,2},{4,5},{5,4},{6,7},{7,6},{8,9},{9,8},{10,11... | collective-permute-start | bytes 1572872 | tf_op jit(solution)/shard_map/ppermute | solution.py:70
  (214 other events, 1891.1 us)
Sparse Core Ops, SparseCore 0:
  30.2 40.7 all-gather.11
  72.6 27.3 all-gather.5
  102.2 109.0 all-gather.7
  212.7 67.9 all-gather.9
  296.4 76.4 reduce-scatter.5
  375.0 56.0 reduce-scatter.7
  433.4 56.0 reduce-scatter.9
  582.9 25.6 reduce-scatter.13
  611.6 37.4 reduce-scatter.11

commit v3 on v2

--- a/solution.py
+++ b/solution.py
@@ -88,28 +88,41 @@
     )(value, *others)
 
 
-def gather8(own, first=None):
+def meet(*values):
+    def gate(*refs):
+        pass
+
+    return pl.pallas_call(
+        gate,
+        in_specs=[pl.BlockSpec(memory_space=pl.ANY)] * len(values),
+        out_specs=[pl.BlockSpec(memory_space=pl.ANY)] * len(values),
+        out_shape=[jax.ShapeDtypeStruct(v.shape, v.dtype) for v in values],
+        input_output_aliases={i: i for i in range(len(values))},
+        cost_estimate=pl.CostEstimate(flops=0, transcendentals=0, bytes_accessed=0),
+        name="meet",
+    )(*values)
+
+
+def gather_steps(own):
     half = own.shape[0] // 2
     over_x = swap(own, "col")
     over_y = swap(own, "hi")
-    over_c = swap(own, "core")
-    if first is not None:
-        done = first(own)
-        over_x, over_y = after(over_x, done), after(over_y, done)
+    rows = [(own, 0, 0), (swap(own, "core"), 1, 0)]
+    done = yield rows
+    over_x, over_y = after(over_x, *done), after(over_y, *done)
     top = swap(over_y[:half], "col")
     low = swap(over_x[half:], "hi")
-    return [
-        (own, 0, 0),
-        (over_c, 1, 0),
-        (over_y, 2, 0),
-        (swap(over_y, "core"), 3, 0),
-        (over_x, 4, 0),
-        (swap(over_x, "core"), 5, 0),
-        (top, 6, 0),
-        (low, 6, half),
-        (swap(top, "core"), 7, 0),
-        (swap(low, "core"), 7, half),
-    ]
+    near = [(over_y, 2, 0), (swap(over_y, "core"), 3, 0), (over_x, 4, 0), (swap(over_x, "core"), 5, 0)]
+    done = yield near
+    top, low = after(top, *done), after(low, *done)
+    far = [(top, 6, 0), (low, 6, half), (swap(top, "core"), 7, 0), (swap(low, "core"), 7, half)]
+    return rows + near + far
+
+
+def gather8(own):
+    steps = gather_steps(own)
+    next(steps)
+    return finish(steps)
 
 
 def scatter_steps(parts):
@@ -147,8 +160,7 @@
     while step < rows:
         pairs = [(i, i + step) if up else (i + step, i) for i in range(rows - step)]
         came = lax.ppermute(now, "row", pairs)
-        done = yield now, came
-        wide = after(came, *done).astype(F32)
+        wide = (yield now, came).astype(F32)
         term = joined(step)[:, None, None, None] * wide
         total = term if total is None else total + term
         if 2 * step < rows:
@@ -159,11 +171,15 @@
 
 def finish(steps, done=()):
     try:
-        steps.send(done)
+        step = steps.send(done)
         while True:
-            steps.send(())
+            step = steps.send(step[1] if isinstance(step, tuple) else ())
     except StopIteration as end:
         return end.value
+
+
+def pair_sum(one, two, start, end):
+    return one[start:end].astype(F32) + two[start:end].astype(F32)
 
 
 def scatter8(parts, *kernels):
@@ -177,6 +193,15 @@
     return finish(steps)
 
 
+def far_in(values):
+    return [pltpu.with_memory_space_constraint(v, pltpu.HBM) if math.prod(v.shape) >= 65536 else v for v in values]
+
+
+def far_out(shapes):
+    return list(shapes)
+    return [pltpu.HBM(a.shape, a.dtype) if math.prod(a.shape) >= 65536 else a for a in shapes]
+
+
 def params(mib=60):
     return pltpu.CompilerParams(dimension_semantics=("arbitrary",), vmem_limit_bytes=mib * 1024 * 1024)
 
@@ -189,22 +214,25 @@
     )
 
 
-def slot_call(kernel, pieces, ins, outs, flops, deps=(), whole=()):
+def slot_call(kernel, pieces, ins, outs, flops, deps=(), whole=(), slots=(0, 8), into=(), mib=60):
+    first, count = slots[0], slots[1] - slots[0]
+    pieces = [p for p in pieces if slots[0] <= p[1] < slots[1]]
     n = len(pieces)
-    width = pieces[0][0].shape[1]
-    per = pieces[0][0].shape[0]
+    per, width = outs[0].shape[1], pieces[0][0].shape[1]
+    extra = list(deps) + list(into)
 
     def wrapped(*refs):
         rows = refs[:n]
         at = n + len(ins)
-        rest = refs[n:at] + refs[at + len(deps) : at + len(deps) + len(outs) + len(whole)]
+        rest = refs[n:at] + refs[at + len(extra) : at + len(extra) + len(outs) + len(whole)]
         buf, sem = refs[-2:]
         i = pl.program_id(0)
 
         @pl.when(i == 0)
         def _():
             for (a, slot, start), ref in zip(pieces, rows):
-                pltpu.make_async_copy(ref, buf.at[slot, pl.ds(start, a.shape[0])], sem.at[slot]).start()
+                there = buf.at[slot - first, pl.ds(start, a.shape[0])]
+                pltpu.make_async_copy(ref, there, sem.at[slot - first]).start()
 
         pltpu.make_async_copy(buf.at[i], buf.at[i], sem.at[i]).wait()
         kernel(buf.at[i], *rest)
@@ -212,25 +240,29 @@
     def spec(a, by_slot):
         rest = len(a.shape) - 1
         if by_slot:
-            return pl.BlockSpec((None,) + a.shape[1:], lambda i: (i,) + (0,) * rest)
+            return pl.BlockSpec((None,) + a.shape[1:], lambda i: (i + first,) + (0,) * rest)
         return pl.BlockSpec(a.shape, lambda i: (0,) * (rest + 1))
 
+    at = n + len(ins) + len(deps)
     return pl.pallas_call(
         wrapped,
-        grid=(8,),
+        grid=(count,),
         in_specs=[pl.BlockSpec(memory_space=pltpu.HBM)] * n
         + [spec(a, k) for a, k in ins]
-        + [pl.BlockSpec(memory_space=pl.ANY)] * len(deps),
+        + [pl.BlockSpec(memory_space=pl.ANY)] * len(extra),
         out_specs=[spec(a, True) for a in outs] + [spec(a, False) for a in whole],
-        out_shape=list(outs) + list(whole),
-        scratch_shapes=[pltpu.VMEM((8, per, width), BF16), pltpu.SemaphoreType.DMA((8,))],
-        compiler_params=params(),
-        cost_estimate=cost(flops, *[a for a, _, _ in pieces], *[a for a, _ in ins], *outs, *whole),
+        out_shape=far_out(list(outs) + list(whole)),
+        scratch_shapes=[pltpu.VMEM((count, per, width), BF16), pltpu.SemaphoreType.DMA((count,))],
+        input_output_aliases={at + i: i for i in range(len(into))},
+        compiler_params=params(mib),
+        cost_estimate=cost(
+            flops * count // 8, *[a for a, _, _ in pieces], *[a for a, k in ins if not k], *outs[:count // 4], *whole
+        ),
         name=kernel.__name__,
-    )(*[a for a, _, _ in pieces], *[a for a, _ in ins], *deps)
-
-
-def grad_call(kernel, pieces, tile, whole, ins, outs, flops, index=lambda i: i, steps=None, deps=()):
+    )(*[a for a, _, _ in pieces], *far_in([a for a, _ in ins]), *extra)
+
+
+def grad_call(kernel, pieces, tile, whole, ins, outs, flops, index=lambda i: i, steps=None, deps=(), mib=60):
     n = len(pieces)
     width = pieces[0][0].shape[1]
     places = [(slot, start, a.shape[0]) for a, slot, start in pieces]
@@ -251,13 +283,13 @@
         + [pl.BlockSpec(block, where) for _, block, where in ins]
         + [pl.BlockSpec(memory_space=pl.ANY)] * len(deps),
         out_specs=[pl.BlockSpec(block, where) for _, block, where in outs],
-        out_shape=[a for a, _, _ in outs],
-        compiler_params=params(),
+        out_shape=far_out([a for a, _, _ in outs]),
+        compiler_params=params(mib),
         cost_estimate=cost(
             flops, *[a for a, _, _ in pieces], *whole, *[a for a, _, _ in ins], *[a for a, _, _ in outs]
         ),
         name=kernel.__name__,
-    )(*[a for a, _, _ in pieces], *whole, *[a for a, _, _ in ins], *deps)
+    )(*far_in([*[a for a, _, _ in pieces], *whole, *[a for a, _, _ in ins]]), *deps)
 
 
 def summed(rows, right):
@@ -411,8 +443,9 @@
     )(*pieces, *ins, *deps)
 
 
-def parts_call(a, w, kind, deps=(), mib=60):
-    slots, per, k = a.shape
+def parts_call(a, w, kind, deps=(), mib=60, pairs=(0, 1, 2, 3)):
+    _, per, k = a.shape
+    n, slots = len(pairs), 2 * len(pairs)
     if kind == "blocks":
         tile, depth = w.shape[2], w.shape[1]
         width = w.shape[0] * tile
@@ -424,24 +457,26 @@
         tile, depth, width = 512, k, w.shape[0]
         w_spec = pl.BlockSpec((tile, k), lambda i: (i, 0))
 
-    def kernel(a_ref, w_ref, *refs):
+    def kernel(*refs):
+        w_ref = refs[n]
         right = w_ref[0] if kind == "blocks" else w_ref[...]
         for slot, out_ref in enumerate(refs[-slots:]):
-            left = a_ref[slot, :, :depth]
+            left = refs[slot // 2][slot % 2, :, :depth]
             out_ref[...] = (dot_t if kind == "nt" else dot)(left, right).astype(BF16)
 
     out = jax.ShapeDtypeStruct((per, width), BF16)
     return pl.pallas_call(
         kernel,
         grid=(width // tile,),
-        in_specs=[pl.BlockSpec(a.shape, lambda i: (0, 0, 0)), w_spec]
+        in_specs=[pl.BlockSpec((2, per, k), lambda i, p=p: (p, 0, 0)) for p in pairs]
+        + [w_spec]
         + [pl.BlockSpec(memory_space=pl.ANY)] * len(deps),
         out_specs=[pl.BlockSpec((per, tile), lambda i: (0, i))] * slots,
-        out_shape=[out] * slots,
+        out_shape=far_out([out] * slots),
         compiler_params=params(mib),
-        cost_estimate=cost(2 * slots * per * depth * width, a, w, *[out] * slots),
+        cost_estimate=cost(2 * slots * per * depth * width, w, *[out] * slots),
         name="parts_" + kind,
-    )(a, w, *deps)
+    )(*far_in([*[a] * n, w]), *deps)
 
 
 def ordered(ref, me, lanes=slice(None)):
@@ -650,7 +685,7 @@
 
     return pl.pallas_call(
         wrapped,
-        out_shape=[jax.ShapeDtypeStruct(a.shape, a.dtype) for a, _ in outs],
+        out_shape=far_out([a for a, _ in outs]),
         grid_spec=pltpu.PrefetchScalarGridSpec(
             num_scalar_prefetch=1,
             grid=(seqs,),
@@ -660,7 +695,7 @@
         compiler_params=params(28),
         cost_estimate=cost(flops, *ins, *[a for a, _ in outs]),
         name=kernel.__name__,
-    )(me, *ins, *deps)
+    )(me, *far_in(ins), *deps)
 
 
 def pick(cond, a, b):
@@ -779,8 +814,9 @@
         [(sds((seqs, span, 256), F32), "q"), (sds((seqs, span, 8), F32), "q")], near,
     )
     forth = walk_steps(state, lambda d: same(row - d, here), lambda d: same(row - d, before), True)
-    next(forth)
-    state_in = finish(forth, [num])
+    _, came = next(forth)
+    came, num, den_in = meet(came, num, den_in)
+    state_in = finish(forth, came)
     o, den = attention_call(
         output_kernel, meta, [qkv, seg_row, feat_c, rows_c, align_c, num, den_in, state_in], "sqcccqqq",
         [(sds((8, seqs, sub, 256), BF16), "s"), (sds((seqs, span, 8), F32), "q")], far,
@@ -791,24 +827,48 @@
         residual_kernel, scatter8(parts_call(o_rows, w_proj, "nn", mib=28)), [x, gain_two], [F32, BF16]
     )
 
-    a2 = gather8(a2_own)
     ff_flops = 2 * every * D * half_ff
+    steps = gather_steps(a2_own)
+    wide = [
+        sds((8, tokens, ff), BF16),
+        sds((8, tokens, half_ff + n_mid), BF16),
+        sds((8, half_ff + n_mid, tokens), BF16),
+    ]
+    hidden = slot_call(ffn_in_kernel, next(steps), [(w_gu, False)], wide, 2 * ff_flops, slots=(0, 2))
+    hidden = slot_call(
+        ffn_in_kernel, steps.send(hidden[:1]), [(w_gu, False)], wide, 2 * ff_flops, slots=(2, 6), into=hidden
+    )
+    a2 = finish(steps, hidden[:1])
     gu, h, h_turned = slot_call(
-        ffn_in_kernel, a2, [(w_gu, False)],
-        [
-            sds((8, tokens, ff), BF16),
-            sds((8, tokens, half_ff + n_mid), BF16),
-            sds((8, half_ff + n_mid, tokens), BF16),
-        ],
-        2 * ff_flops,
+        ffn_in_kernel, a2, [(w_gu, False)], wide, 2 * ff_flops, slots=(6, 8), into=hidden
     )
     (down_g,) = grad_call(
         down_grad_kernel, ups, 256, [h_turned], [],
         [(sds((8, half_ff, 256), BF16), (1, half_ff, 256), lambda i: (i, 0, 0))], ff_flops,
     )
-    (dgu,) = slot_call(
-        ffn_back_kernel, ups, [(w_down, False), (gu, True)], [sds((8, tokens, ff), BF16)], ff_flops, [down_g],
-    )
+    late = {}
+
+    def ffn_back(slots, into, deps=()):
+        return slot_call(
+            ffn_back_kernel, ups, [(w_down, False), (gu, True)], [sds((8, tokens, ff), BF16)], ff_flops, deps,
+            slots=slots, into=into,
+        )[0]
+
+    half = tokens // 2
+    dgu = ffn_back((6, 8), (), [down_g])
+    xy, xyc = parts_call(dgu, w_gu, "nt", pairs=(3,))
+    xyc, dgu = meet(swap(xyc, "core"), ffn_back((2, 6), [dgu], [xy]))
+    to_x = pair_sum(xy, xyc, 0, half).astype(BF16)
+    to_y = pair_sum(xy, xyc, half, tokens).astype(BF16)
+    from_x, from_y, y, yc, x_, xc = meet(
+        swap(to_x, "col"), swap(to_y, "hi"), *parts_call(dgu, w_gu, "nt", [to_x, to_y], pairs=(1, 2))
+    )
+    xc, yc, dgu = meet(swap(xc, "core"), swap(yc, "core"), ffn_back((0, 2), [dgu], [x_]))
+    near_x = pair_sum(x_, xc, 0, half).astype(BF16)
+    near_y = pair_sum(y, yc, half, tokens).astype(BF16)
+    far_x = (pair_sum(x_, xc, half, tokens) + from_y.astype(F32)).astype(BF16)
+    far_y = (pair_sum(y, yc, 0, half) + from_x.astype(F32)).astype(BF16)
+    own, other = parts_call(dgu, w_gu, "nt", [near_x, near_y, far_x, far_y], pairs=(0,))
     down_g = (
         down_g.reshape(8, half_ff, fold, D // shards).transpose(0, 2, 1, 3).reshape(shards * half_ff, -1)
     )
@@ -832,9 +892,29 @@
 
         return run
 
+    gu_half(0)([own])
+    first_x, first_y, last_x, last_y, other, gu_gs[0] = meet(
+        swap(near_x, "col"), swap(near_y, "hi"), swap(far_x, "col"), swap(far_y, "hi"), swap(other, "core"), gu_gs[0]
+    )
     grad_r, datt_own = row_call(
-        residual_back_kernel, scatter8(parts_call(dgu, w_gu, "nt"), gu_half(0), gu_half(1)),
+        residual_back_kernel, [own, other, first_x, last_y, last_x, first_y],
         [upstream.reshape(tokens, D), residual, gain_two], [F32, BF16],
+    )
+    gu_half(1)([datt_own])
+    over_x, over_y, over_c, gu_gs[1] = meet(
+        swap(datt_own, "col"), swap(datt_own, "hi"), swap(datt_own, "core"), gu_gs[1]
+    )
+    to_x, to_y = over_y[:half], over_x[half:]
+    down_parts = parts_call(h, w_down, "blocks", [to_x, to_y])
+    top, low, over_yc, over_xc, *down_parts = meet(
+        swap(to_x, "col"), swap(to_y, "hi"), swap(over_y, "core"), swap(over_x, "core"), *down_parts
+    )
+    datt = [
+        (datt_own, 0, 0), (over_c, 1, 0), (over_y, 2, 0), (over_yc, 3, 0), (over_x, 4, 0), (over_xc, 5, 0),
+        (top, 6, 0), (low, 6, half), (swap(top, "core"), 7, 0), (swap(low, "core"), 7, half),
+    ]
+    (do,) = slot_call(
+        do_kernel, datt, [(w_proj, False)], [sds((8, tokens, 256), BF16)], 2 * every * D * 256, [down_g]
     )
     gain_part = jnp.stack([g.reshape(4, 256, 128) for g in gains], 1).reshape(D, 128)
     if fold > 1:
@@ -843,17 +923,6 @@
         gu_gs = [by_col[0].reshape(D // 2, ff), by_col[1].reshape(D // 2, ff)]
     gu_r = [lax.psum_scatter(g, "row", scatter_dimension=0, tiled=True) for g in gu_gs]
 
-    late = {}
-
-    def down_side(own):
-        late["out"] = parts_call(h, w_down, "blocks", [own])
-        return late["out"][0]
-
-    datt = gather8(datt_own, down_side)
-    (do,) = slot_call(
-        do_kernel, datt, [(w_proj, False)], [sds((8, tokens, 256), BF16)], 2 * every * D * 256,
-        [down_g, late["out"][0]],
-    )
     do = do.reshape(8, seqs, sub, 256)
 
     (dstate,) = attention_call(
@@ -869,40 +938,46 @@
         False,
     )
     _, came = next(back)
-    down_steps = scatter_steps(late["out"])
-    dq, dk, dv = attention_call(
+    own, other, y, yc, x_, xc, xy, xyc = down_parts
+    other, yc, xc, xyc = (swap(part, "core") for part in (other, yc, xc, xyc))
+    to_x = pair_sum(xy, xyc, 0, half).astype(BF16)
+    to_y = pair_sum(xy, xyc, half, tokens).astype(BF16)
+    near_x = pair_sum(x_, xc, 0, half).astype(BF16)
+    near_y = pair_sum(y, yc, half, tokens).astype(BF16)
+    intra = attention_call(
         back_intra_kernel, meta, [qkv, seg_row, feat_c, rows_c, align_c, o, do, den, state_in],
-        "sqcccssqq", [(part, "q")] * 3, 3 * near + far, next(down_steps),
-    )
-    sent = down_steps.send([dq, came])
-    now, _ = back.send([dq])
+        "sqcccssqq", [(part, "q")] * 3, 3 * near + far, [dstate, to_x, to_y, near_x, near_y, gu_r[0]],
+    )
+    dq, dk, dv = intra
+    came, from_x, from_y, first_x, first_y, dq = meet(
+        came, swap(to_x, "col"), swap(to_y, "hi"), swap(near_x, "col"), swap(near_y, "hi"), dq
+    )
+    far_x = (pair_sum(x_, xc, half, tokens) + from_y.astype(F32)).astype(BF16)
+    far_y = (pair_sum(y, yc, 0, half) + from_x.astype(F32)).astype(BF16)
+    step = back.send(came)
+    now = None
+    if step is not None:
+        now, came = step
     (proj_g,) = grad_call(
         proj_grad_kernel, datt, 1024, [o_rows], [],
-        [(sds((256, D), BF16), (256, 1024), lambda i: (0, i))], 2 * every * D * 256, deps=[*sent, now, gu_r[0]],
-    )
-    (outputs,) = row_call(output_rows_kernel, finish(down_steps, [proj_g]), [residual], [BF16])
-    dstate_out = finish(back, [proj_g])
+        [(sds((256, D), BF16), (256, 1024), lambda i: (0, i))], 2 * every * D * 256, deps=[far_x, far_y, now], mib=24,
+    )
+    down_r = down_g.reshape(2, half_ff, D // shards)
+    d_keep, d_send = pick(is0, down_r[0], down_r[1]), pick(is0, down_r[1], down_r[0])
+    g_keep = pick(is0, gu_r[0], gu_r[1])
+    g_send = pick(is0, gu_r[1], gu_r[0])
+    came, last_x, last_y, d_got, proj_g = meet(
+        came, swap(far_x, "col"), swap(far_y, "hi"), swap(d_send, "col"), proj_g
+    )
+    (outputs,) = row_call(
+        output_rows_kernel, [own, other, first_x, last_y, last_x, first_y], [residual], [BF16]
+    )
+    dstate_out = finish(back, came)
     proj_r = lax.psum_scatter(proj_g, "row", scatter_dimension=0, tiled=True)
-    project_grad = lax.ppermute(proj_r, ("row", "col"), [(b, a) for a, b in shard_pairs]).astype(F32)
     row_out = sds((8, seqs, sub, PAYLOAD), BF16)
     dqkv, scaled = attention_call(
         back_output_kernel, meta, [qkv, seg_row, feat_c, rows_c, align_c, dstate_out, dq, dk, dv, inv],
         "sqcccqqqqs", [(row_out, "s")] * 2, 2 * far, [outputs, gu_r[1]],
-    )
-    down_g = down_g.reshape(2, half_ff, D // shards)
-    d_keep, d_send = pick(is0, down_g[0], down_g[1]), pick(is0, down_g[1], down_g[0])
-    d_got = swap(d_send, "col")
-    d0, d1 = pick(is0, d_keep, d_got).astype(F32), pick(is0, d_got, d_keep).astype(F32)
-    down_grad = jnp.concatenate([d0, d1[n_main:], d1[:n_main]], 0)
-    g_keep = pick(is0, gu_r[0], gu_r[1])
-    g_got = swap(pick(is0, gu_r[1], gu_r[0]), "col")
-    g0, g1 = pick(is0, g_keep, g_got).astype(F32), pick(is0, g_got, g_keep).astype(F32)
-    m = 2 * n_main
-    gate_grad = jnp.concatenate(
-        [g0[:, :n_main], g0[:, m : m + n_mid], g1[:, m : m + n_mid], g1[:, :n_main]], 1
-    )
-    up_grad = jnp.concatenate(
-        [g0[:, n_main:m], g0[:, m + n_mid :], g1[:, m + n_mid :], g1[:, n_main:m]], 1
     )
 
     def qkv_side(sent):
@@ -916,15 +991,31 @@
                     lambda i: (0, i, 0, 0),
                 )
             ],
-            2 * every * D * PAYLOAD, deps=sent,
+            2 * every * D * PAYLOAD, deps=sent, mib=24,
         )
         return [late["qkv"]]
 
-    f_parts = parts_call(dqkv.reshape(8, tokens, PAYLOAD), w_qkv, "nt", [gate_grad, up_grad, down_grad], 28)
-    f_pieces = scatter8(f_parts, qkv_side)
-    qkv_g = late["qkv"]
+    own, other, y, yc, x_, xc, xy, xyc = parts_call(
+        dqkv.reshape(8, tokens, PAYLOAD), w_qkv, "nt", [proj_r], 28
+    )
+    qkv_side([own])
+    other, yc, xc, xyc, qkv_g = meet(*(swap(part, "core") for part in (other, yc, xc, xyc)), late["qkv"])
+    to_x = pair_sum(xy, xyc, 0, half).astype(BF16)
+    to_y = pair_sum(xy, xyc, half, tokens).astype(BF16)
+    near_x = pair_sum(x_, xc, 0, half).astype(BF16)
+    near_y = pair_sum(y, yc, half, tokens).astype(BF16)
+    from_x, from_y, first_x, first_y = (
+        swap(to_x, "col"), swap(to_y, "hi"), swap(near_x, "col"), swap(near_y, "hi")
+    )
+    far_x = (pair_sum(x_, xc, half, tokens) + from_y.astype(F32)).astype(BF16)
+    far_y = (pair_sum(y, yc, 0, half) + from_x.astype(F32)).astype(BF16)
+    g_got = swap(after(g_send, far_x), "col")
+    f_pieces = [own, other, first_x, swap(far_y, "hi"), swap(far_x, "col"), first_y]
     (inputs_grad,) = row_call(input_back_kernel, f_pieces, [x, grad_r], [F32])
     qkv_g = lax.psum_scatter(qkv_g.reshape(D, PAYLOAD), "row", scatter_dimension=0, tiled=True)
+    project_grad = lax.ppermute(
+        after(proj_r, qkv_g), ("row", "col"), [(b, a) for a, b in shard_pairs]
+    ).astype(F32)
     qkv_g = lax.all_to_all(
         qkv_g.reshape(8, n_rows, PAYLOAD), GROUP, split_axis=0, concat_axis=0, tiled=True
     ).astype(F32)
@@ -932,6 +1023,16 @@
     v_g = per_row[:, :, :256].reshape(n_rows, -1)
     q_g = per_row[:, :, 256:288].reshape(n_rows, -1)
     k_g = per_row[:, :, 288:320].reshape(n_rows, -1)
+    d0, d1 = pick(is0, d_keep, d_got).astype(F32), pick(is0, d_got, d_keep).astype(F32)
+    down_grad = jnp.concatenate([d0, d1[n_main:], d1[:n_main]], 0)
+    g0, g1 = pick(is0, g_keep, g_got).astype(F32), pick(is0, g_got, g_keep).astype(F32)
+    m = 2 * n_main
+    gate_grad = jnp.concatenate(
+        [g0[:, :n_main], g0[:, m : m + n_mid], g1[:, m : m + n_mid], g1[:, :n_main]], 1
+    )
+    up_grad = jnp.concatenate(
+        [g0[:, n_main:m], g0[:, m + n_mid :], g1[:, m + n_mid :], g1[:, n_main:m]], 1
+    )
     forward_grad = jnp.sum(per_row[:, :, 320], 1) / fgain.astype(F32)
     attend_grad = (
         jnp.sum(v_g * vw.astype(F32), 1) + jnp.sum(q_g * qw.astype(F32), 1) + jnp.sum(k_g * kw.astype(F32), 1)

time: 688 us -> 668 us (0.971)
  Pallas kernels: 206 us -> 237 us
  local copies, waits for them, and re-layouts: 93.2 us -> 64.7 us
  other arithmetic: 69.8 us -> 57.2 us
    pallas_call x14 -> x30, Pallas kernels: 135 us -> 167 us  [the longest x8 70.3 us: slot_call(): pl.pallas_call(wrapped, grid=(count,), in_specs=[pl.BlockSpec(memory_spac...]
    unnamed x304 -> x180, local copies, waits for them, and re-layouts: 63.8 us -> 36.1 us
    convert_element_type x7 -> x12, other arithmetic: 14.7 us -> 27.9 us  [the longest x3 8.71 us: body(): to_y = pair_sum(xy, xyc, half, tokens).astype(BF16)]
    reduce_scatter x1, waiting for transfers between devices: 12.2 us -> 0.02 us  [body(): lax.psum_scatter(qkv_g.reshape(D, PAYLOAD), 'row', scatter_dimension=0, t...]
    convert_element_type x4 -> x1, other arithmetic: 9.4 us -> 0.49 us  [scatter_steps(): far_x = (both(x, xc, half, n) + from_y.astype(F32)).astype(BF16)]
  transfers between devices with their start and end apart: 98 -> 98, of which waited for: 34 -> 42; matrix products, arithmetic and copies ran while one was open for 13% -> 12% of each run, Pallas kernels for 30% -> 35%
where the time goes in v3:
time: 668 us; the launch traced here: 657 us
  Pallas kernels  237 us (35%)
  waiting for transfers between devices  181 us (27%)
  starting transfers between devices  102 us (15%)
  local copies, waits for them, and re-layouts  64.7 us (10%)
  other arithmetic  57.2 us (9%)
  between operations  15.6 us (2%)
    ppermute x81, waiting for transfers between devices, swap(): return lax.ppermute(value, axis, [(0, 1), (1, 0)])  138 us
    pallas_call x8, Pallas kernels, slot_call(): pl.pallas_call(wrapped, grid=(count,), in_specs=[pl.BlockSpec(memory_spac...  70.3 us
    ppermute x81, starting transfers between devices, swap(): return lax.ppermute(value, axis, [(0, 1), (1, 0)])  57.8 us
    pallas_call x5, Pallas kernels, grad_call(): pl.pallas_call(wrapped, grid=(steps or width // tile,), in_specs=[pl.Bloc...  55 us
    pallas_call x6, Pallas kernels, attention_call(): pl.pallas_call(wrapped, out_shape=far_out([a for a, _ in outs]), grid_spe...  49.1 us
    pallas_call x6, Pallas kernels, parts_call(): pl.pallas_call(kernel, grid=(width // tile,), in_specs=[pl.BlockSpec((2,...  48 us
    unnamed x180, local copies, waits for them, and re-layouts  36.1 us
    ppermute x4, starting transfers between devices, walk_steps(): came = lax.ppermute(now, 'row', pairs)  29.9 us
  transfers between devices with their start and end apart: 98, of which 42 were waited for; matrix products, arithmetic and copies ran while one was open for 12% of the time, Pallas kernels for 35%

profile of v3, /device:TPU:16, one launch (start us, length us, event | category | flops | bytes accessed | tf_op | source)
XLA Modules:
  0.0 657.3 jit_solution(16532758943694451389)
XLA Ops:
  40.5 13.6 %collective-permute-done.1.refs_2_ = bf16[256,2048]{1,0:T(8,128)(2,1)} collective-permute-done((bf16[256,2048]{1,0:T(8,128)(2,1)}, bf16[256,2048]{1,0:T(8,128)(2,1)}, u32[]{:S(2)}, u32[]{:S(2)}) %collective-permute-start.1) | collective-permute-done | bytes 1048608 | tf_op jit(solution)/shard_map/ppermute | solution.py:70
  74.1 9.5 %qkv_kernel.1 = (bf16[8,256,384]{2,1,0:T(8,128)(2,1)}, f32[8,256,128]{2,1,0:T(8,128)}, bf16[2048,384]{1,0:T(8,128)(2,1)}) custom-call(bf16[256,2048]{1,0:T(8,128)(2,1)} %gate.12.refs_0_, bf16[256,2048]{1,0:T(8,128)(2,1)} %collective-permute-done.refs_1_, bf16[256,2048]{1,0:T(8,128)(2,1)} %collective-permute-done.1.refs_2_, ...), custom_call_target="tpu_custom_call" | custom-call | flops 3221225472 | bytes 14155776 | tf_op jit(solution)/shard_map/qkv_kernel/pallas_call | solution.py:247
  97.0 8.2 %collective-permute-start.19 = (bf16[4,2,160,128]{3,2,1,0:T(8,128)(2,1)S(1)}, bf16[4,2,160,128]{3,2,1,0:T(8,128)(2,1)S(1)}, u32[]{:S(2)}, u32[]{:S(2)}) collective-permute-start(bf16[4,2,160,128]{3,2,1,0:T(8,128)(2,1)S(1)} %copy-done.28), channel_id=1, source_target_pairs={{0,2},{2,4},{4,6},{1,3},{3,5},{5,7},{8,10},{10,12},{12,14},{9,11},... | collective-permute-start | bytes 983048 | tf_op jit(solution)/shard_map/ppermute | solution.py:162
  127.1 11.5 %collective-permute-done.20 = bf16[4,2,160,128]{3,2,1,0:T(8,128)(2,1)} collective-permute-done((bf16[4,2,160,128]{3,2,1,0:T(8,128)(2,1)}, bf16[4,2,160,128]{3,2,1,0:T(8,128)(2,1)}, u32[]{:S(2)}, u32[]{:S(2)}) %collective-permute-start.20) | collective-permute-done | bytes 327712 | tf_op jit(solution)/shard_map/ppermute | solution.py:162
  141.9 8.1 %output_kernel.1 = (bf16[8,4,64,256]{3,2,1,0:T(8,128)(2,1)S(1)}, f32[4,512,8]{2,1,0:T(8,128)S(1)}) custom-call(s32[9]{0:T(128)S(1)} %pad_add_fusion.refs_0_, bf16[8,4,64,384]{3,2,1,0:T(8,128)(2,1)} %bitcast.105, f32[4,1,512]{2,1,0:T(1,128)S(1)} %copy-done.38, bf16[128,512]{1,0:T(8,128)(2,1)} %constant.57.clone.refs_3_, f32[8,512]{1,0:T(8,128)S(1)} %copy-done.37, ...), custom_call_target="tpu_custom_call" | custom-call | flops 629145600 | bytes 5791744 | tf_op jit(solution)/shard_map/output_kernel/pallas_call | solution.py:686
  162.9 11.0 %collective-permute-done.28 = bf16[128,2048]{1,0:T(8,128)(2,1)S(1)} collective-permute-done((bf16[128,2048]{1,0:T(8,128)(2,1)S(1)}, bf16[128,2048]{1,0:T(8,128)(2,1)S(1)}, u32[]{:S(2)}, u32[]{:S(2)}) %collective-permute-start.28) | collective-permute-done | bytes 524320 | tf_op jit(solution)/shard_map/ppermute | solution.py:70
  180.6 8.7 %collective-permute-done.23.refs_2_ = bf16[128,2048]{1,0:T(8,128)(2,1)S(1)} collective-permute-done((bf16[128,2048]{1,0:T(8,128)(2,1)S(1)}, bf16[128,2048]{1,0:T(8,128)(2,1)S(1)}, u32[]{:S(2)}, u32[]{:S(2)}) %collective-permute-start.23) | collective-permute-done | bytes 524320 | tf_op jit(solution)/shard_map/ppermute | solution.py:70
  191.7 7.3 %collective-permute-done.29.refs_4_ = bf16[128,2048]{1,0:T(8,128)(2,1)S(1)} collective-permute-done((bf16[128,2048]{1,0:T(8,128)(2,1)S(1)}, bf16[128,2048]{1,0:T(8,128)(2,1)S(1)}, u32[]{:S(2)}, u32[]{:S(2)}) %collective-permute-start.29) | collective-permute-done | bytes 524320 | tf_op jit(solution)/shard_map/ppermute | solution.py:70
  209.1 8.8 %ffn_in_kernel.3 = (bf16[8,256,1408]{2,1,0:T(8,128)(2,1)}, bf16[8,256,768]{2,1,0:T(8,128)(2,1)}, bf16[8,768,256]{2,1,0:T(8,128)(2,1)}) custom-call(bf16[256,2048]{1,0:T(8,128)(2,1)} %get-tuple-element.140.refs_0_, bf16[256,2048]{1,0:T(8,128)(2,1)} %collective-permute-done.32.refs_1_, ...), custom_call_target="tpu_custom_call" | custom-call | flops 2952790016 | bytes 7864320 | tf_op jit(solution)/shard_map/ffn_in_kernel/pallas_call | solution.py:247
  217.9 13.0 %collective-permute-done.31.refs_0_ = bf16[256,2048]{1,0:T(8,128)(2,1)} collective-permute-done((bf16[256,2048]{1,0:T(8,128)(2,1)}, bf16[256,2048]{1,0:T(8,128)(2,1)}, u32[]{:S(2)}, u32[]{:S(2)}) %collective-permute-start.31) | collective-permute-done | bytes 1048608 | tf_op jit(solution)/shard_map/ppermute | solution.py:70
  236.6 12.9 %ffn_in_kernel.4 = (bf16[8,256,1408]{2,1,0:T(8,128)(2,1)}, bf16[8,256,768]{2,1,0:T(8,128)(2,1)}, bf16[8,768,256]{2,1,0:T(8,128)(2,1)}) custom-call(bf16[256,2048]{1,0:T(8,128)(2,1)} %gate.18.refs_0_.refs_2_, bf16[256,2048]{1,0:T(8,128)(2,1)} %collective-permute-done.34.refs_1_.refs_3_, ...), custom_call_target="tpu_custom_call", output_to_operand_aliasing={{0}: (5, {}), {1}: (6, {}), {2}: (7, {})} | custom-call | flops 5905580032 | bytes 15728640 | tf_op jit(solution)/shard_map/ffn_in_kernel/pallas_call | solution.py:247
  254.0 8.8 %ffn_in_kernel.5 = (bf16[8,256,1408]{2,1,0:T(8,128)(2,1)}, bf16[8,256,768]{2,1,0:T(8,128)(2,1)}, bf16[8,768,256]{2,1,0:T(8,128)(2,1)}) custom-call(bf16[128,2048]{1,0:T(8,128)(2,1)} %gate.20.refs_0_.refs_6_, bf16[128,2048]{1,0:T(8,128)(2,1)} %gate.21.refs_1_.refs_7_, ...), custom_call_target="tpu_custom_call", output_to_operand_aliasing={{0}: (5, {}), {1}: (6, {}), {2}: (7, {})} | custom-call | flops 2952790016 | bytes 7864320 | tf_op jit(solution)/shard_map/ffn_in_kernel/pallas_call | solution.py:247
  262.9 13.1 %down_grad_kernel.1.refs_6_ = bf16[8,704,256]{2,1,0:T(8,128)(2,1)} custom-call(bf16[256,2048]{1,0:T(8,128)(2,1)} %gate.14.refs_0_, bf16[256,2048]{1,0:T(8,128)(2,1)} %collective-permute-done.40.refs_1_, bf16[256,2048]{1,0:T(8,128)(2,1)} %copy-done.58, bf16[256,2048]{1,0:T(8,128)(2,1)} %collective-permute-done.41.refs_3_.refs_1_, ...), custom_call_target="tpu_custom_call" | custom-call | flops 5905580032 | bytes 14417920 | tf_op jit(solution)/shard_map/down_grad_kernel/pallas_call | solution.py:278
  285.9 7.2 %parts_nt.4 = (bf16[256,2048]{1,0:T(8,128)(2,1)}, bf16[256,2048]{1,0:T(8,128)(2,1)}) custom-call(bf16[8,256,1408]{2,1,0:T(8,128)(2,1)} %ffn_back_kernel.3.refs_0_.refs_7_, bf16[2048,1408]{1,0:T(8,128)(2,1)} %all-gather.10.cloned.1.call-done.refs_2_.refs_4_.refs_1_.refs_11_), custom_call_target="tpu_custom_call" | custom-call | flops 2952790016 | bytes 7864320 | tf_op jit(solution)/shard_map/parts_nt/pallas_call | solution.py:468
  293.1 9.4 %ffn_back_kernel.4.refs_1_ = bf16[8,256,1408]{2,1,0:T(8,128)(2,1)} custom-call(bf16[256,2048]{1,0:T(8,128)(2,1)} %copy-done.58, bf16[256,2048]{1,0:T(8,128)(2,1)} %collective-permute-done.41.refs_3_.refs_1_, bf16[256,2048]{1,0:T(8,128)(2,1)} %collective-permute-done.13.refs_4_.refs_2_, ...), custom_call_target="tpu_custom_call", output_to_operand_aliasing={{}: (7, {})} | custom-call | flops 2952790016 | bytes 12845056 | tf_op jit(solution)/shard_map/ffn_back_kernel/pallas_call | solution.py:247
  308.2 10.4 %parts_nt.5 = (bf16[256,2048]{1,0:T(8,128)(2,1)}, bf16[256,2048]{1,0:T(8,128)(2,1)}, bf16[256,2048]{1,0:T(8,128)(2,1)}, bf16[256,2048]{1,0:T(8,128)(2,1)}) custom-call(bf16[8,256,1408]{2,1,0:T(8,128)(2,1)} %get-tuple-element.152.refs_0_.refs_1_.refs_5_, bf16[8,256,1408]{2,1,0:T(8,128)(2,1)} %get-tuple-element.152.refs_0_.refs_1_.refs_5_, ...), custom_call_target="tpu_custom_call" | custom-call | flops 5905580032 | bytes 9961472 | tf_op jit(solution)/shard_map/parts_nt/pallas_call | solution.py:468
  334.2 7.2 %parts_nt.6 = (bf16[256,2048]{1,0:T(8,128)(2,1)}, bf16[256,2048]{1,0:T(8,128)(2,1)}) custom-call(bf16[8,256,1408]{2,1,0:T(8,128)(2,1)} %get-tuple-element.160.refs_0_.refs_10_, bf16[2048,1408]{1,0:T(8,128)(2,1)} %all-gather.10.cloned.1.call-done.refs_2_.refs_4_.refs_1_.refs_11_, bf16[128,2048]{1,0:T(8,128)(2,1)} %get-tuple-element.300.refs_2_, ...), custom_call_target="tpu_custom_call" | custom-call | flops 2952790016 | bytes 7864320 | tf_op jit(solution)/shard_map/parts_nt/pallas_call | solution.py:468
  345.4 13.5 %gu_grad_kernel.2 = (bf16[1024,1408]{1,0:T(8,128)(2,1)}, f32[1024,128]{1,0:T(8,128)}) custom-call(bf16[256,2048]{1,0:T(8,128)(2,1)} %get-tuple-element.140.refs_0_, bf16[256,2048]{1,0:T(8,128)(2,1)} %collective-permute-done.32.refs_1_, bf16[256,2048]{1,0:T(8,128)(2,1)} %gate.18.refs_0_.refs_2_, bf16[256,2048]{1,0:T(8,128)(2,1)} %collective-permute-done.34.refs_1_.refs_3_, ...), custom_call_target="tpu_custom_call" | custom-call | flops 5905580032 | bytes 23330816 | tf_op jit(solution)/shard_map/gu_grad_kernel/pallas_call | solution.py:278
  358.9 8.3 %collective-permute-done.50.refs_2_ = bf16[128,2048]{1,0:T(8,128)(2,1)} collective-permute-done((bf16[128,2048]{1,0:T(8,128)(2,1)S(1)}, bf16[128,2048]{1,0:T(8,128)(2,1)}, u32[]{:S(2)}, u32[]{:S(2)}) %collective-permute-start.50) | collective-permute-done | bytes 524320 | tf_op jit(solution)/shard_map/ppermute | solution.py:70
  379.2 13.5 %gu_grad_kernel.3 = (bf16[1024,1408]{1,0:T(8,128)(2,1)}, f32[1024,128]{1,0:T(8,128)}) custom-call(bf16[256,2048]{1,0:T(8,128)(2,1)} %get-tuple-element.140.refs_0_, bf16[256,2048]{1,0:T(8,128)(2,1)} %collective-permute-done.32.refs_1_, bf16[256,2048]{1,0:T(8,128)(2,1)} %gate.18.refs_0_.refs_2_, bf16[256,2048]{1,0:T(8,128)(2,1)} %collective-permute-done.34.refs_1_.refs_3_, ...), custom_call_target="tpu_custom_call" | custom-call | flops 5905580032 | bytes 23330816 | tf_op jit(solution)/shard_map/gu_grad_kernel/pallas_call | solution.py:278
  392.8 8.4 %collective-permute-done.53.refs_0_ = bf16[256,2048]{1,0:T(8,128)(2,1)} collective-permute-done((bf16[256,2048]{1,0:T(8,128)(2,1)}, bf16[256,2048]{1,0:T(8,128)(2,1)}, u32[]{:S(2)}, u32[]{:S(2)}) %collective-permute-start.53) | collective-permute-done | bytes 1048608 | tf_op jit(solution)/shard_map/ppermute | solution.py:70
  408.1 11.0 %parts_blocks.1 = (bf16[256,2048]{1,0:T(8,128)(2,1)}, bf16[256,2048]{1,0:T(8,128)(2,1)}, bf16[256,2048]{1,0:T(8,128)(2,1)}, bf16[256,2048]{1,0:T(8,128)(2,1)}, b...) custom-call(bf16[8,256,768]{2,1,0:T(8,128)(2,1)} %get-tuple-element., ...), custom_call_target="tpu_custom_call" | custom-call | flops 5905580032 | bytes 11272192 | tf_op jit(solution)/shard_map/parts_blocks/pallas_call | solution.py:468
  424.9 7.6 %do_kernel.1 = bf16[8,256,256]{2,1,0:T(8,128)(2,1)} custom-call(bf16[256,2048]{1,0:T(8,128)(2,1)} %get-tuple-element.175.refs_12_.refs_0_, bf16[256,2048]{1,0:T(8,128)(2,1)} %get-tuple-element.190.refs_1_, bf16[256,2048]{1,0:T(8,128)(2,1)} %get-tuple-element.177.refs_2_, bf16[256,2048]{1,0:T(8,128)(2,1)} %get-tuple-element.191.refs_3_, ...), custom_call_target="tpu_custom_call" | custom-call | flops 2147483648 | bytes 10485760 | tf_op jit(solution)/shard_map/do_kernel/pallas_call | solution.py:247
  450.0 16.0 %collective-permute-start.63 = (bf16[4,2,160,128]{3,2,1,0:T(8,128)(2,1)S(1)}, bf16[4,2,160,128]{3,2,1,0:T(8,128)(2,1)}, u32[]{:S(2)}, u32[]{:S(2)}) collective-permute-start(bf16[4,2,160,128]{3,2,1,0:T(8,128)(2,1)S(1)} %back_state_kernel.1.refs_10_), channel_id=1, source_target_pairs={{2,0},{4,2},{6,4},{3,1},{5,3},{7,5},{10,8},{12,10},{14,12},{11,9},... | collective-permute-start | bytes 983048 | tf_op jit(solution)/shard_map/ppermute | solution.py:162
  469.2 14.0 %back_intra_kernel.1 = (f32[4,512,256]{2,1,0:T(8,128)S(1)}, f32[4,512,256]{2,1,0:T(8,128)S(1)}, f32[4,512,256]{2,1,0:T(8,128)S(1)}) custom-call(s32[9]{0:T(128)S(1)} %pad_add_fusion.refs_0_, bf16[8,4,64,384]{3,2,1,0:T(8,128)(2,1)} %bitcast.107, f32[4,1,512]{2,1,0:T(1,128)S(1)} %copy-done.38, bf16[128,512]{1,0:T(8,128)(2,1)} %constant.57.clone.refs_3_, ...), custom_call_target="tpu_custom_call" | custom-call | flops 2642411520 | bytes 10969088 | tf_op jit(solution)/shard_map/back_intra_kernel/pallas_call | solution.py:686
  506.0 8.0 %collective-permute-done.71.refs_0_ = bf16[4,2,160,128]{3,2,1,0:T(8,128)(2,1)S(1)} collective-permute-done((bf16[4,2,160,128]{3,2,1,0:T(8,128)(2,1)S(1)}, bf16[4,2,160,128]{3,2,1,0:T(8,128)(2,1)S(1)}, u32[]{:S(2)}, u32[]{:S(2)}) %collective-permute-start.71) | collective-permute-done | bytes 327712 | tf_op jit(solution)/shard_map/ppermute | solution.py:162
  526.9 8.9 %back_output_kernel.1 = (bf16[8,4,64,384]{3,2,1,0:T(8,128)(2,1)S(1)}, bf16[8,4,64,384]{3,2,1,0:T(8,128)(2,1)S(1)}) custom-call(s32[9]{0:T(128)S(1)} %pad_add_fusion.refs_0_, bf16[8,4,64,384]{3,2,1,0:T(8,128)(2,1)} %bitcast.108, f32[4,1,512]{2,1,0:T(1,128)S(1)} %copy-done.38, bf16[128,512]{1,0:T(8,128)(2,1)} %constant.57.clone.refs_3_, ...), custom_call_target="tpu_custom_call" | custom-call | flops 1258291200 | bytes 13000704 | tf_op jit(solution)/shard_map/back_output_kernel/pallas_call | solution.py:686
  542.7 7.4 %parts_nt.7 = (bf16[256,2048]{1,0:T(8,128)(2,1)S(1)}, bf16[256,2048]{1,0:T(8,128)(2,1)S(1)}, bf16[256,2048]{1,0:T(8,128)(2,1)S(1)}, bf16[256,2048]{1,0:T(8,128)(...) custom-call(bf16[8,256,384]{2,1,0:T(8,128)(2,1)} %bitcast.99, ...), custom_call_target="tpu_custom_call" | custom-call | flops 3221225472 | bytes 9961472 | tf_op jit(solution)/shard_map/parts_nt/pallas_call | solution.py:468
  552.2 8.6 %qkv_grad_kernel.1.refs_4_ = bf16[4,4,128,384]{3,2,1,0:T(8,128)(2,1)S(1)} custom-call(bf16[256,2048]{1,0:T(8,128)(2,1)} %gate.12.refs_0_, bf16[256,2048]{1,0:T(8,128)(2,1)} %collective-permute-done.refs_1_, bf16[256,2048]{1,0:T(8,128)(2,1)} %collective-permute-done.1.refs_2_, bf16[256,2048]{1,0:T(8,128)(2,1)} %collective-permute-done.2.refs_3_, ...), custom_call_target="tpu_custom_call" | custom-call | flops 3221225472 | bytes 12582912 | tf_op jit(solution)/shard_map/qkv_grad_kernel/pallas_call | solution.py:278
  570.9 10.3 %collective-permute-done.82 = bf16[128,2048]{1,0:T(8,128)(2,1)} collective-permute-done((bf16[128,2048]{1,0:T(8,128)(2,1)}, bf16[128,2048]{1,0:T(8,128)(2,1)}, u32[]{:S(2)}, u32[]{:S(2)}) %collective-permute-start.82) | collective-permute-done | bytes 524320 | tf_op jit(solution)/shard_map/ppermute | solution.py:70
  616.8 6.8 %collective-permute-done.86 = bf16[256,1408]{1,0:T(8,128)(2,1)S(1)} collective-permute-done((bf16[256,1408]{1,0:T(8,128)(2,1)}, bf16[256,1408]{1,0:T(8,128)(2,1)S(1)}, u32[]{:S(2)}, u32[]{:S(2)}) %collective-permute-start.86) | collective-permute-done | bytes 720928 | tf_op jit(solution)/shard_map/ppermute | solution.py:70
  636.3 7.7 %collective-permute-done.85 = bf16[64,2048]{1,0:T(8,128)(2,1)} collective-permute-done((bf16[64,2048]{1,0:T(8,128)(2,1)}, bf16[64,2048]{1,0:T(8,128)(2,1)}, u32[]{:S(2)}, u32[]{:S(2)}) %collective-permute-start.85) | collective-permute-done | bytes 262176 | tf_op jit(solution)/shard_map/ppermute | solution.py:1016
  (495 shorter events, 322.9 us)
Async XLA Ops:
  26.2 45.2 %all-gather.12.cloned.1.call-start = ((), (), s32[]{:S(2)}) async-start(), calls=%async_computation.15 | async-start | bytes 1966080 | tf_op jit(solution)/shard_map/all_gather | solution.py:759
  28.9 123.0 %all-gather.8.cloned.1.call-start = ((), (), s32[]{:S(2)}) async-start(), calls=%async_computation.8 | async-start | bytes 1310720 | tf_op jit(solution)/shard_map/all_gather | solution.py:758
  28.9 25.2 %collective-permute-start.1 = (bf16[256,2048]{1,0:T(8,128)(2,1)}, bf16[256,2048]{1,0:T(8,128)(2,1)}, u32[]{:S(2)}, u32[]{:S(2)}) collective-permute-start(bf16[256,2048]{1,0:T(8,128)(2,1)} %gate.12.refs_0_), channel_id=1, source_target_pairs={{0,16},{16,0},{1,17},{17,1},{2,18},{18,2},{3,19},{19,3},{4,20},{20... | collective-permute-start | bytes 3145736 | tf_op jit(solution)/shard_map/ppermute | solution.py:70
  31.9 26.3 %collective-permute-start.3 = (bf16[256,2048]{1,0:T(8,128)(2,1)}, bf16[256,2048]{1,0:T(8,128)(2,1)}, u32[]{:S(2)}, u32[]{:S(2)}) collective-permute-start(bf16[256,2048]{1,0:T(8,128)(2,1)} %gate.12.refs_0_), channel_id=1, source_target_pairs={{0,1},{1,0},{2,3},{3,2},{4,5},{5,4},{6,7},{7,6},{8,9},{9,8},{10,11... | collective-permute-start | bytes 3145736 | tf_op jit(solution)/shard_map/ppermute | solution.py:70
  34.3 28.2 %collective-permute-start.10 = (s32[4,256]{1,0:T(4,128)S(1)}, s32[4,256]{1,0:T(4,128)S(1)}, u32[]{:S(2)}, u32[]{:S(2)}) collective-permute-start(s32[4,256]{1,0:T(4,128)S(1)} %reshape.293), channel_id=1, source_target_pairs={{0,1},{1,0},{2,3},{3,2},{4,5},{5,4},{6,7},{7,6},{8,9},{9,8},{10,11... | collective-permute-start | bytes 12296 | tf_op jit(solution)/shard_map/ppermute | solution.py:70
  40.5 31.9 %collective-permute-start = (bf16[256,2048]{1,0:T(8,128)(2,1)S(1)}, bf16[256,2048]{1,0:T(8,128)(2,1)}, u32[]{:S(2)}, u32[]{:S(2)}) collective-permute-start(bf16[256,2048]{1,0:T(8,128)(2,1)S(1)} %copy-done.40), channel_id=1, source_target_pairs={{0,8},{8,0},{1,9},{9,1},{2,10},{10,2},{3,11},{11,3},{4,12},{12,4},... | collective-permute-start | bytes 3145736 | tf_op jit(solution)/shard_map/ppermute | solution.py:70
  63.7 145.4 %all-gather.10.cloned.1.call-start = ((), (), s32[]{:S(2)}) async-start(), calls=%async_computation.9 | async-start | bytes 7208960 | tf_op jit(solution)/shard_map/all_gather | solution.py:800
  93.8 185.5 %all-gather.6.cloned.1.call-start = ((), (), s32[]{:S(2)}) async-start(), calls=%async_computation.7 | async-start | bytes 3604480 | tf_op jit(solution)/shard_map/all_gather | solution.py:806
  95.2 25.1 %collective-permute-start.11 = (bf16[256,2048]{1,0:T(8,128)(2,1)}, bf16[256,2048]{1,0:T(8,128)(2,1)S(1)}, u32[]{:S(2)}, u32[]{:S(2)}) collective-permute-start(bf16[256,2048]{1,0:T(8,128)(2,1)} %gate.14.refs_0_), channel_id=1, source_target_pairs={{0,16},{16,0},{1,17},{17,1},{2,18},{18,2},{3,19},{19,3},{4,20},{20... | collective-permute-start | bytes 3145736 | tf_op jit(solution)/shard_map/ppermute | solution.py:70
  96.4 25.8 %collective-permute-start.13 = (bf16[256,2048]{1,0:T(8,128)(2,1)}, bf16[256,2048]{1,0:T(8,128)(2,1)}, u32[]{:S(2)}, u32[]{:S(2)}) collective-permute-start(bf16[256,2048]{1,0:T(8,128)(2,1)} %gate.14.refs_0_), channel_id=1, source_target_pairs={{0,1},{1,0},{2,3},{3,2},{4,5},{5,4},{6,7},{7,6},{8,9},{9,8},{10,11... | collective-permute-start | bytes 3145736 | tf_op jit(solution)/shard_map/ppermute | solution.py:70
  178.3 22.7 %collective-permute-start.30 = (bf16[128,2048]{1,0:T(8,128)(2,1)S(1)}, bf16[128,2048]{1,0:T(8,128)(2,1)S(1)}, u32[]{:S(2)}, u32[]{:S(2)}) collective-permute-start(bf16[128,2048]{1,0:T(8,128)(2,1)S(1)} %get-tuple-element.303), channel_id=1, source_target_pairs={{0,16},{16,0},{1,17},{17,1},{2,18},{18,2},{3,19},{19,3},{4,20},{20... | collective-permute-start | bytes 1572872 | tf_op jit(solution)/shard_map/ppermute | solution.py:70
  204.5 217.1 %reduce-scatter.6.cloned.1.call-start = ((), (), s32[]{:S(2)}) async-start(), calls=%async_computation.10 | async-start | bytes 3604480 | tf_op jit(solution)/shard_map/reduce_scatter | solution.py:875
  205.0 25.9 %collective-permute-start.31 = (bf16[256,2048]{1,0:T(8,128)(2,1)}, bf16[256,2048]{1,0:T(8,128)(2,1)}, u32[]{:S(2)}, u32[]{:S(2)}) collective-permute-start(bf16[256,2048]{1,0:T(8,128)(2,1)} %get-tuple-element.140.refs_0_), channel_id=1, source_target_pairs={{0,16},{16,0},{1,17},{17,1},{2,18},{18,2},{3,19},{19,3},{4,20},{20... | collective-permute-start | bytes 3145736 | tf_op jit(solution)/shard_map/ppermute | solution.py:70
  206.3 25.6 %collective-permute-start.35 = (bf16[256,2048]{1,0:T(8,128)(2,1)}, bf16[256,2048]{1,0:T(8,128)(2,1)}, u32[]{:S(2)}, u32[]{:S(2)}) collective-permute-start(bf16[256,2048]{1,0:T(8,128)(2,1)} %get-tuple-element.140.refs_0_), channel_id=1, source_target_pairs={{0,1},{1,0},{2,3},{3,2},{4,5},{5,4},{6,7},{7,6},{8,9},{9,8},{10,11... | collective-permute-start | bytes 3145736 | tf_op jit(solution)/shard_map/ppermute | solution.py:70
  231.9 31.0 %collective-permute-start.40 = (bf16[256,2048]{1,0:T(8,128)(2,1)}, bf16[256,2048]{1,0:T(8,128)(2,1)}, u32[]{:S(2)}, u32[]{:S(2)}) collective-permute-start(bf16[256,2048]{1,0:T(8,128)(2,1)} %gate.14.refs_0_), channel_id=1, source_target_pairs={{0,8},{8,0},{1,9},{9,1},{2,10},{10,2},{3,11},{11,3},{4,12},{12,4},... | collective-permute-start | bytes 3145736 | tf_op jit(solution)/shard_map/ppermute | solution.py:70
  276.0 190.9 %reduce-scatter.8.cloned.1.call-start = ((), (), s32[]{:S(2)}) async-start(), calls=%async_computation.11 | async-start | bytes 3604480 | tf_op jit(solution)/shard_map/reduce_scatter | solution.py:924
  341.3 26.3 %collective-permute-start.52 = (bf16[256,2048]{1,0:T(8,128)(2,1)}, bf16[256,2048]{1,0:T(8,128)(2,1)}, u32[]{:S(2)}, u32[]{:S(2)}) collective-permute-start(bf16[256,2048]{1,0:T(8,128)(2,1)} %get-tuple-element.167), channel_id=1, source_target_pairs={{0,8},{8,0},{1,9},{9,1},{2,10},{10,2},{3,11},{11,3},{4,12},{12,4},... | collective-permute-start | bytes 3145736 | tf_op jit(solution)/shard_map/ppermute | solution.py:70
  343.5 23.8 %collective-permute-start.50 = (bf16[128,2048]{1,0:T(8,128)(2,1)S(1)}, bf16[128,2048]{1,0:T(8,128)(2,1)}, u32[]{:S(2)}, u32[]{:S(2)}) collective-permute-start(bf16[128,2048]{1,0:T(8,128)(2,1)S(1)} %copy-done.59), channel_id=1, source_target_pairs={{0,1},{1,0},{2,3},{3,2},{4,5},{5,4},{6,7},{7,6},{8,9},{9,8},{10,11... | collective-permute-start | bytes 1572872 | tf_op jit(solution)/shard_map/ppermute | solution.py:70
  367.6 156.9 %reduce-scatter.10.cloned.1.call-start = ((), (), s32[]{:S(2)}) async-start(), calls=%async_computation.12 | async-start | bytes 3604480 | tf_op jit(solution)/shard_map/reduce_scatter | solution.py:924
  376.4 24.8 %collective-permute-start.53 = (bf16[256,2048]{1,0:T(8,128)(2,1)}, bf16[256,2048]{1,0:T(8,128)(2,1)}, u32[]{:S(2)}, u32[]{:S(2)}) collective-permute-start(bf16[256,2048]{1,0:T(8,128)(2,1)} %get-tuple-element.175.refs_12_.refs_0_), channel_id=1, source_target_pairs={{0,1},{1,0},{2,3},{3,2},{4,5},{5,4},{6,7},{7,6},{8,9},{9,8},{10,11... | collective-permute-start | bytes 3145736 | tf_op jit(solution)/shard_map/ppermute | solution.py:70
  377.7 24.5 %collective-permute-start.54 = (bf16[256,2048]{1,0:T(8,128)(2,1)}, bf16[256,2048]{1,0:T(8,128)(2,1)}, u32[]{:S(2)}, u32[]{:S(2)}) collective-permute-start(bf16[256,2048]{1,0:T(8,128)(2,1)} %get-tuple-element.175.refs_12_.refs_0_), channel_id=1, source_target_pairs={{0,16},{16,0},{1,17},{17,1},{2,18},{18,2},{3,19},{19,3},{4,20},{20... | collective-permute-start | bytes 3145736 | tf_op jit(solution)/shard_map/ppermute | solution.py:70
  379.2 23.0 %collective-permute-start.55 = (bf16[256,2048]{1,0:T(8,128)(2,1)}, bf16[256,2048]{1,0:T(8,128)(2,1)}, u32[]{:S(2)}, u32[]{:S(2)}) collective-permute-start(bf16[256,2048]{1,0:T(8,128)(2,1)} %get-tuple-element.175.refs_12_.refs_0_), channel_id=1, source_target_pairs={{0,8},{8,0},{1,9},{9,1},{2,10},{10,2},{3,11},{11,3},{4,12},{12,4},... | collective-permute-start | bytes 3145736 | tf_op jit(solution)/shard_map/ppermute | solution.py:70
  402.3 139.5 %reduce-scatter.12.cloned.1.call-start = ((), (), s32[]{:S(2)}) async-start(), calls=%async_computation.13 | async-start | bytes 1310720 | tf_op jit(solution)/shard_map/reduce_scatter | solution.py:976
  435.5 53.0 %collective-permute-start.65 = (bf16[128,2048]{1,0:T(8,128)(2,1)}, bf16[128,2048]{1,0:T(8,128)(2,1)}, u32[]{:S(2)}, u32[]{:S(2)}) collective-permute-start(bf16[128,2048]{1,0:T(8,128)(2,1)} %get-tuple-element.296.refs_11_), channel_id=1, source_target_pairs={{0,1},{1,0},{2,3},{3,2},{4,5},{5,4},{6,7},{7,6},{8,9},{9,8},{10,11... | collective-permute-start | bytes 1572872 | tf_op jit(solution)/shard_map/ppermute | solution.py:70
  436.9 51.6 %collective-permute-start.66 = (bf16[128,2048]{1,0:T(8,128)(2,1)}, bf16[128,2048]{1,0:T(8,128)(2,1)}, u32[]{:S(2)}, u32[]{:S(2)}) collective-permute-start(bf16[128,2048]{1,0:T(8,128)(2,1)} %get-tuple-element.295.refs_12_), channel_id=1, source_target_pairs={{0,16},{16,0},{1,17},{17,1},{2,18},{18,2},{3,19},{19,3},{4,20},{20... | collective-permute-start | bytes 1572872 | tf_op jit(solution)/shard_map/ppermute | solution.py:70
  440.4 48.1 %collective-permute-start.68 = (bf16[128,2048]{1,0:T(8,128)(2,1)}, bf16[128,2048]{1,0:T(8,128)(2,1)}, u32[]{:S(2)}, u32[]{:S(2)}) collective-permute-start(bf16[128,2048]{1,0:T(8,128)(2,1)} %add_convert_fusion.9.refs_13_), channel_id=1, source_target_pairs={{0,1},{1,0},{2,3},{3,2},{4,5},{5,4},{6,7},{7,6},{8,9},{9,8},{10,11... | collective-permute-start | bytes 1572872 | tf_op jit(solution)/shard_map/ppermute | solution.py:70
  443.0 45.5 %collective-permute-start.70 = (bf16[128,2048]{1,0:T(8,128)(2,1)}, bf16[128,2048]{1,0:T(8,128)(2,1)}, u32[]{:S(2)}, u32[]{:S(2)}) collective-permute-start(bf16[128,2048]{1,0:T(8,128)(2,1)} %add_convert_fusion.8.refs_14_), channel_id=1, source_target_pairs={{0,16},{16,0},{1,17},{17,1},{2,18},{18,2},{3,19},{19,3},{4,20},{20... | collective-permute-start | bytes 1572872 | tf_op jit(solution)/shard_map/ppermute | solution.py:70
  450.0 38.1 %collective-permute-start.63 = (bf16[4,2,160,128]{3,2,1,0:T(8,128)(2,1)S(1)}, bf16[4,2,160,128]{3,2,1,0:T(8,128)(2,1)}, u32[]{:S(2)}, u32[]{:S(2)}) collective-permute-start(bf16[4,2,160,128]{3,2,1,0:T(8,128)(2,1)S(1)} %back_state_kernel.1.refs_10_), channel_id=1, source_target_pairs={{2,0},{4,2},{6,4},{3,1},{5,3},{7,5},{10,8},{12,10},{14,12},{11,9},... | collective-permute-start | bytes 983048 | tf_op jit(solution)/shard_map/ppermute | solution.py:162
  490.2 23.8 %collective-permute-start.72 = (bf16[128,2048]{1,0:T(8,128)(2,1)S(1)}, bf16[128,2048]{1,0:T(8,128)(2,1)}, u32[]{:S(2)}, u32[]{:S(2)}) collective-permute-start(bf16[128,2048]{1,0:T(8,128)(2,1)S(1)} %add_convert_fusion.7.refs_11_), channel_id=1, source_target_pairs={{0,1},{1,0},{2,3},{3,2},{4,5},{5,4},{6,7},{7,6},{8,9},{9,8},{10,11... | collective-permute-start | bytes 1572872 | tf_op jit(solution)/shard_map/ppermute | solution.py:70
  514.8 110.4 %reduce-scatter.14.cloned.1.call-start = ((), (), s32[]{:S(2)}) async-start(), calls=%async_computation.14 | async-start | bytes 1966080 | tf_op jit(solution)/shard_map/reduce_scatter | solution.py:1015
  585.1 25.0 %collective-permute-start.83 = (bf16[128,2048]{1,0:T(8,128)(2,1)}, bf16[128,2048]{1,0:T(8,128)(2,1)}, u32[]{:S(2)}, u32[]{:S(2)}) collective-permute-start(bf16[128,2048]{1,0:T(8,128)(2,1)} %get-tuple-element.291.refs_1_), channel_id=1, source_target_pairs={{0,1},{1,0},{2,3},{3,2},{4,5},{5,4},{6,7},{7,6},{8,9},{9,8},{10,11... | collective-permute-start | bytes 1572872 | tf_op jit(solution)/shard_map/ppermute | solution.py:70
  585.7 37.9 %collective-permute-start.86 = (bf16[256,1408]{1,0:T(8,128)(2,1)}, bf16[256,1408]{1,0:T(8,128)(2,1)S(1)}, u32[]{:S(2)}, u32[]{:S(2)}) collective-permute-start(bf16[256,1408]{1,0:T(8,128)(2,1)} %gate.23), channel_id=1, source_target_pairs={{0,1},{1,0},{2,3},{3,2},{4,5},{5,4},{6,7},{7,6},{8,9},{9,8},{10,11... | collective-permute-start | bytes 2162696 | tf_op jit(solution)/shard_map/ppermute | solution.py:70
  (152 other events, 1368.2 us)
Sparse Core Ops, SparseCore 0:
  29.1 40.7 all-gather.11
  71.5 27.4 all-gather.7
  101.1 107.9 all-gather.9
  210.5 68.7 all-gather.5
  281.4 67.9 reduce-scatter.5
  367.7 70.4 reduce-scatter.7
  440.5 65.3 reduce-scatter.9
  514.9 26.7 reduce-scatter.11
  570.1 32.4 reduce-scatter.13

commit v4 on v3

--- a/solution.py
+++ b/solution.py
@@ -197,8 +197,9 @@
     return [pltpu.with_memory_space_constraint(v, pltpu.HBM) if math.prod(v.shape) >= 65536 else v for v in values]
 
 
-def far_out(shapes):
-    return list(shapes)
+def far_out(shapes, far=False):
+    if not far:
+        return list(shapes)
     return [pltpu.HBM(a.shape, a.dtype) if math.prod(a.shape) >= 65536 else a for a in shapes]
 
 
@@ -421,6 +422,42 @@
 def input_back_kernel(refs, x_ref, grad_ref, out_ref):
     normed, inv = scaled_rows(x_ref[...].astype(F32))
     out_ref[...] = grad_ref[...] + norm_back(normed, inv, row_sum(refs))
+
+
+def weights_kernel(got_ref, place_ref, vw_ref, qw_ref, kw_ref, gain_ref, v_ref, q_ref, k_ref, gains_ref):
+    gain = gain_ref[:, 0:1]
+    attend = jnp.zeros(gain.shape, F32)
+    forward = jnp.zeros(gain.shape, F32)
+    heads = None
+    lane = lax.broadcasted_iota(jnp.int32, (1, 128), 1)
+    for d in range(8):
+        lanes = slice(256 * d, 256 * (d + 1))
+        part = got_ref[d, :, :256].astype(F32)
+        attend = attend + jnp.sum(part * vw_ref[:, lanes].astype(F32), 1, keepdims=True)
+        v_ref[:, lanes] = part * gain
+        tail = got_ref[d, :, 256:]
+        forward = forward + jnp.sum(jnp.where(lane == 64, tail.astype(F32), 0.0), 1, keepdims=True)
+        term = dot(tail, place_ref[d])
+        heads = term if heads is None else heads + term
+    q, k = heads[:, :256], heads[:, 256:]
+    attend = attend + jnp.sum(q * qw_ref[...].astype(F32) + k * kw_ref[...].astype(F32), 1, keepdims=True)
+    q_ref[...] = q * gain
+    k_ref[...] = k * gain
+    gains_ref[...] = jnp.where(lane == 0, attend, forward / gain_ref[:, 1:2])
+
+
+def weights_call(got, vw, qw, kw, gains):
+    place = np.zeros((8, 128, 512), np.float32)
+    for d in range(8):
+        for i in range(32):
+            place[d, i, 32 * d + i] = 1.0
+            place[d, 32 + i, 256 + 32 * d + i] = 1.0
+    n = got.shape[1]
+    outs = [jax.ShapeDtypeStruct((n, c), F32) for c in (vw.shape[1], qw.shape[1], kw.shape[1], 128)]
+    return pl.pallas_call(
+        weights_kernel, out_shape=outs, compiler_params=pltpu.CompilerParams(vmem_limit_bytes=16 * 1024 * 1024),
+        name="weights_kernel",
+    )(got, jnp.asarray(place, BF16), vw, qw, kw, gains)
 
 
 def row_call(kernel, pieces, ins, kinds, deps=()):
@@ -685,7 +722,7 @@
 
     return pl.pallas_call(
         wrapped,
-        out_shape=far_out([a for a, _ in outs]),
+        out_shape=far_out([a for a, _ in outs], kernel is back_intra_kernel),
         grid_spec=pltpu.PrefetchScalarGridSpec(
             num_scalar_prefetch=1,
             grid=(seqs,),
@@ -855,20 +892,13 @@
         )[0]
 
     half = tokens // 2
-    dgu = ffn_back((6, 8), (), [down_g])
-    xy, xyc = parts_call(dgu, w_gu, "nt", pairs=(3,))
-    xyc, dgu = meet(swap(xyc, "core"), ffn_back((2, 6), [dgu], [xy]))
+    dgu = ffn_back((0, 8), (), [down_g])
+    own, other, y, yc, x_, xc, xy, xyc = parts_call(dgu, w_gu, "nt")
+    other, yc, xc, xyc = (swap(part, "core") for part in (other, yc, xc, xyc))
     to_x = pair_sum(xy, xyc, 0, half).astype(BF16)
     to_y = pair_sum(xy, xyc, half, tokens).astype(BF16)
-    from_x, from_y, y, yc, x_, xc = meet(
-        swap(to_x, "col"), swap(to_y, "hi"), *parts_call(dgu, w_gu, "nt", [to_x, to_y], pairs=(1, 2))
-    )
-    xc, yc, dgu = meet(swap(xc, "core"), swap(yc, "core"), ffn_back((0, 2), [dgu], [x_]))
     near_x = pair_sum(x_, xc, 0, half).astype(BF16)
     near_y = pair_sum(y, yc, half, tokens).astype(BF16)
-    far_x = (pair_sum(x_, xc, half, tokens) + from_y.astype(F32)).astype(BF16)
-    far_y = (pair_sum(y, yc, 0, half) + from_x.astype(F32)).astype(BF16)
-    own, other = parts_call(dgu, w_gu, "nt", [near_x, near_y, far_x, far_y], pairs=(0,))
     down_g = (
         down_g.reshape(8, half_ff, fold, D // shards).transpose(0, 2, 1, 3).reshape(shards * half_ff, -1)
     )
@@ -892,30 +922,31 @@
 
         return run
 
-    gu_half(0)([own])
-    first_x, first_y, last_x, last_y, other, gu_gs[0] = meet(
-        swap(near_x, "col"), swap(near_y, "hi"), swap(far_x, "col"), swap(far_y, "hi"), swap(other, "core"), gu_gs[0]
-    )
+    gu_half(0)([to_x, to_y, near_x, near_y])
+    from_x, from_y, first_x, first_y, gu_gs[0] = meet(
+        swap(to_x, "col"), swap(to_y, "hi"), swap(near_x, "col"), swap(near_y, "hi"), gu_gs[0]
+    )
+    far_x = (pair_sum(x_, xc, half, tokens) + from_y.astype(F32)).astype(BF16)
+    far_y = (pair_sum(y, yc, 0, half) + from_x.astype(F32)).astype(BF16)
+    gu_half(1)([far_x, far_y, gu_gs[0]])
+    last_x, last_y, gu_gs[1] = meet(swap(far_x, "col"), swap(far_y, "hi"), gu_gs[1])
     grad_r, datt_own = row_call(
         residual_back_kernel, [own, other, first_x, last_y, last_x, first_y],
         [upstream.reshape(tokens, D), residual, gain_two], [F32, BF16],
     )
-    gu_half(1)([datt_own])
-    over_x, over_y, over_c, gu_gs[1] = meet(
-        swap(datt_own, "col"), swap(datt_own, "hi"), swap(datt_own, "core"), gu_gs[1]
+    over_x, over_y, over_c, *down_parts = meet(
+        swap(datt_own, "col"), swap(datt_own, "hi"), swap(datt_own, "core"),
+        *parts_call(h, w_down, "blocks", [datt_own]),
     )
     to_x, to_y = over_y[:half], over_x[half:]
-    down_parts = parts_call(h, w_down, "blocks", [to_x, to_y])
-    top, low, over_yc, over_xc, *down_parts = meet(
-        swap(to_x, "col"), swap(to_y, "hi"), swap(over_y, "core"), swap(over_x, "core"), *down_parts
-    )
-    datt = [
-        (datt_own, 0, 0), (over_c, 1, 0), (over_y, 2, 0), (over_yc, 3, 0), (over_x, 4, 0), (over_xc, 5, 0),
-        (top, 6, 0), (low, 6, half), (swap(top, "core"), 7, 0), (swap(low, "core"), 7, half),
-    ]
-    (do,) = slot_call(
-        do_kernel, datt, [(w_proj, False)], [sds((8, tokens, 256), BF16)], 2 * every * D * 256, [down_g]
-    )
+    over_yc, over_xc = swap(over_y, "core"), swap(over_x, "core")
+    datt = [(datt_own, 0, 0), (over_c, 1, 0), (over_y, 2, 0), (over_yc, 3, 0), (over_x, 4, 0), (over_xc, 5, 0)]
+    do_out = [sds((8, tokens, 256), BF16)]
+    do_flops = 2 * every * D * 256
+    (do,) = slot_call(do_kernel, datt, [(w_proj, False)], do_out, do_flops, [to_x, to_y], slots=(0, 6))
+    top, low, do = meet(swap(to_x, "col"), swap(to_y, "hi"), do)
+    datt += [(top, 6, 0), (low, 6, half), (swap(top, "core"), 7, 0), (swap(low, "core"), 7, half)]
+    (do,) = slot_call(do_kernel, datt, [(w_proj, False)], do_out, do_flops, [down_g], slots=(6, 8), into=[do])
     gain_part = jnp.stack([g.reshape(4, 256, 128) for g in gains], 1).reshape(D, 128)
     if fold > 1:
         natural = jnp.stack([g.reshape(4, 256, ff) for g in gu_gs], 1)
@@ -939,7 +970,7 @@
     )
     _, came = next(back)
     own, other, y, yc, x_, xc, xy, xyc = down_parts
-    other, yc, xc, xyc = (swap(part, "core") for part in (other, yc, xc, xyc))
+    other, yc, xc, xyc = (after(swap(part, "core"), dstate) for part in (other, yc, xc, xyc))
     to_x = pair_sum(xy, xyc, 0, half).astype(BF16)
     to_y = pair_sum(xy, xyc, half, tokens).astype(BF16)
     near_x = pair_sum(x_, xc, 0, half).astype(BF16)
@@ -995,11 +1026,11 @@
         )
         return [late["qkv"]]
 
+    qkv_g = qkv_side([proj_r])[0]
     own, other, y, yc, x_, xc, xy, xyc = parts_call(
-        dqkv.reshape(8, tokens, PAYLOAD), w_qkv, "nt", [proj_r], 28
-    )
-    qkv_side([own])
-    other, yc, xc, xyc, qkv_g = meet(*(swap(part, "core") for part in (other, yc, xc, xyc)), late["qkv"])
+        dqkv.reshape(8, tokens, PAYLOAD), w_qkv, "nt", [qkv_g], 28
+    )
+    other, yc, xc, xyc = (swap(part, "core") for part in (other, yc, xc, xyc))
     to_x = pair_sum(xy, xyc, 0, half).astype(BF16)
     to_y = pair_sum(xy, xyc, half, tokens).astype(BF16)
     near_x = pair_sum(x_, xc, 0, half).astype(BF16)
@@ -1011,18 +1042,18 @@
     far_y = (pair_sum(y, yc, 0, half) + from_x.astype(F32)).astype(BF16)
     g_got = swap(after(g_send, far_x), "col")
     f_pieces = [own, other, first_x, swap(far_y, "hi"), swap(far_x, "col"), first_y]
-    (inputs_grad,) = row_call(input_back_kernel, f_pieces, [x, grad_r], [F32])
     qkv_g = lax.psum_scatter(qkv_g.reshape(D, PAYLOAD), "row", scatter_dimension=0, tiled=True)
     project_grad = lax.ppermute(
         after(proj_r, qkv_g), ("row", "col"), [(b, a) for a, b in shard_pairs]
     ).astype(F32)
     qkv_g = lax.all_to_all(
         qkv_g.reshape(8, n_rows, PAYLOAD), GROUP, split_axis=0, concat_axis=0, tiled=True
-    ).astype(F32)
-    per_row = qkv_g.transpose(1, 0, 2)
-    v_g = per_row[:, :, :256].reshape(n_rows, -1)
-    q_g = per_row[:, :, 256:288].reshape(n_rows, -1)
-    k_g = per_row[:, :, 288:320].reshape(n_rows, -1)
+    )
+    (inputs_grad,) = row_call(input_back_kernel, f_pieces, [x, grad_r], [F32], [qkv_g])
+    v_g, q_g, k_g, both_gains = weights_call(
+        qkv_g, vw, qw, kw, jnp.stack([again.astype(F32), fgain.astype(F32)], 1)
+    )
+    attend_grad, forward_grad = both_gains[:, 0], both_gains[:, 1]
     d0, d1 = pick(is0, d_keep, d_got).astype(F32), pick(is0, d_got, d_keep).astype(F32)
     down_grad = jnp.concatenate([d0, d1[n_main:], d1[:n_main]], 0)
     g0, g1 = pick(is0, g_keep, g_got).astype(F32), pick(is0, g_got, g_keep).astype(F32)
@@ -1033,17 +1064,12 @@
     up_grad = jnp.concatenate(
         [g0[:, n_main:m], g0[:, m + n_mid :], g1[:, m + n_mid :], g1[:, n_main:m]], 1
     )
-    forward_grad = jnp.sum(per_row[:, :, 320], 1) / fgain.astype(F32)
-    attend_grad = (
-        jnp.sum(v_g * vw.astype(F32), 1) + jnp.sum(q_g * qw.astype(F32), 1) + jnp.sum(k_g * kw.astype(F32), 1)
-    )
-
     return (
         outputs.reshape(inputs.shape),
         inputs_grad.reshape(inputs.shape),
-        q_g * gain_one,
-        k_g * gain_one,
-        v_g * gain_one,
+        q_g,
+        k_g,
+        v_g,
         project_grad,
         attend_grad,
         gate_grad,

time: 668 us -> 648 us (0.970)
  waiting for transfers between devices: 181 us -> 159 us
  local copies, waits for them, and re-layouts: 64.7 us -> 73 us
  Pallas kernels: 237 us -> 229 us
    ppermute x81, waiting for transfers between devices: 138 us -> 124 us  [swap(): return lax.ppermute(value, axis, [(0, 1), (1, 0)])]
    pallas_call x6 -> x4, Pallas kernels: 48 us -> 41.9 us  [parts_call(): pl.pallas_call(kernel, grid=(width // tile,), in_specs=[pl.BlockSpec((2,...]
    pallas_call x8 -> x7, Pallas kernels: 70.3 us -> 65.2 us  [slot_call(): pl.pallas_call(wrapped, grid=(count,), in_specs=[pl.BlockSpec(memory_spac...]
    pallas_call x6 -> x7, Pallas kernels: 49.1 us -> 51.1 us  [the longest x6 50 us: attention_call(): pl.pallas_call(wrapped, out_shape=far_out([a for a, _ in outs], kernel is...]
    unnamed x180 -> x161, local copies, waits for them, and re-layouts: 36.1 us -> 38.1 us
  transfers between devices with their start and end apart: 98 -> 98, of which waited for: 42 -> 36; matrix products, arithmetic and copies ran while one was open for 12% -> 14% of each run, Pallas kernels for 35% -> 32%
where the time goes in v4:
time: 648 us; the launch traced here: 640 us
  Pallas kernels  229 us (35%)
  waiting for transfers between devices  159 us (25%)
  starting transfers between devices  103 us (16%)
  local copies, waits for them, and re-layouts  73 us (11%)
  other arithmetic  60.4 us (9%)
  between operations  15.4 us (2%)
    ppermute x81, waiting for transfers between devices, swap(): return lax.ppermute(value, axis, [(0, 1), (1, 0)])  124 us
    pallas_call x7, Pallas kernels, slot_call(): pl.pallas_call(wrapped, grid=(count,), in_specs=[pl.BlockSpec(memory_spac...  65.2 us
    ppermute x81, starting transfers between devices, swap(): return lax.ppermute(value, axis, [(0, 1), (1, 0)])  60.7 us
    pallas_call x5, Pallas kernels, grad_call(): pl.pallas_call(wrapped, grid=(steps or width // tile,), in_specs=[pl.Bloc...  55.9 us
    pallas_call x6, Pallas kernels, attention_call(): pl.pallas_call(wrapped, out_shape=far_out([a for a, _ in outs], kernel is...  50 us
    pallas_call x4, Pallas kernels, parts_call(): pl.pallas_call(kernel, grid=(width // tile,), in_specs=[pl.BlockSpec((2,...  41.9 us
    unnamed x161, local copies, waits for them, and re-layouts  38.1 us
    ppermute x4, starting transfers between devices, walk_steps(): came = lax.ppermute(now, 'row', pairs)  27.3 us
  transfers between devices with their start and end apart: 98, of which 36 were waited for; matrix products, arithmetic and copies ran while one was open for 14% of the time, Pallas kernels for 32%

profile of v4, /device:TPU:16, one launch (start us, length us, event | category | flops | bytes accessed | tf_op | source)
XLA Modules:
  0.0 639.5 jit_solution(7974077554749396964)
XLA Ops:
  41.0 13.6 %collective-permute-done.1.refs_2_ = bf16[256,2048]{1,0:T(8,128)(2,1)} collective-permute-done((bf16[256,2048]{1,0:T(8,128)(2,1)}, bf16[256,2048]{1,0:T(8,128)(2,1)}, u32[]{:S(2)}, u32[]{:S(2)}) %collective-permute-start.1) | collective-permute-done | bytes 1048608 | tf_op jit(solution)/shard_map/ppermute | solution.py:70
  74.5 9.5 %qkv_kernel.1 = (bf16[8,256,384]{2,1,0:T(8,128)(2,1)}, f32[8,256,128]{2,1,0:T(8,128)}, bf16[2048,384]{1,0:T(8,128)(2,1)}) custom-call(bf16[256,2048]{1,0:T(8,128)(2,1)} %gate.16.refs_0_, bf16[256,2048]{1,0:T(8,128)(2,1)} %collective-permute-done.refs_1_, bf16[256,2048]{1,0:T(8,128)(2,1)} %collective-permute-done.1.refs_2_, ...), custom_call_target="tpu_custom_call" | custom-call | flops 3221225472 | bytes 14155776 | tf_op jit(solution)/shard_map/qkv_kernel/pallas_call | solution.py:248
  84.1 5.8 state_kernel.1.refs_1_
  97.5 8.2 %collective-permute-start.22 = (bf16[4,2,160,128]{3,2,1,0:T(8,128)(2,1)S(1)}, bf16[4,2,160,128]{3,2,1,0:T(8,128)(2,1)S(1)}, u32[]{:S(2)}, u32[]{:S(2)}) collective-permute-start(bf16[4,2,160,128]{3,2,1,0:T(8,128)(2,1)S(1)} %copy-done.22), channel_id=1, source_target_pairs={{0,2},{2,4},{4,6},{1,3},{3,5},{5,7},{8,10},{10,12},{12,14},{9,11},... | collective-permute-start | bytes 983048 | tf_op jit(solution)/shard_map/ppermute | solution.py:162
  107.6 5.9 intra_kernel.1
  127.5 11.6 %collective-permute-done.23 = bf16[4,2,160,128]{3,2,1,0:T(8,128)(2,1)} collective-permute-done((bf16[4,2,160,128]{3,2,1,0:T(8,128)(2,1)}, bf16[4,2,160,128]{3,2,1,0:T(8,128)(2,1)}, u32[]{:S(2)}, u32[]{:S(2)}) %collective-permute-start.23) | collective-permute-done | bytes 327712 | tf_op jit(solution)/shard_map/ppermute | solution.py:162
  142.3 8.1 %output_kernel.1 = (bf16[8,4,64,256]{3,2,1,0:T(8,128)(2,1)S(1)}, f32[4,512,8]{2,1,0:T(8,128)S(1)}) custom-call(s32[9]{0:T(128)S(1)} %pad_add_fusion.refs_0_, bf16[8,4,64,384]{3,2,1,0:T(8,128)(2,1)} %bitcast.97, f32[4,1,512]{2,1,0:T(1,128)S(1)} %copy-done.39, bf16[128,512]{1,0:T(8,128)(2,1)} %constant.59.clone.refs_3_, f32[8,512]{1,0:T(8,128)S(1)} %copy-done.35, ...), custom_call_target="tpu_custom_call" | custom-call | flops 629145600 | bytes 5791744 | tf_op jit(solution)/shard_map/output_kernel/pallas_call | solution.py:723
  163.4 11.0 %collective-permute-done.29 = bf16[128,2048]{1,0:T(8,128)(2,1)S(1)} collective-permute-done((bf16[128,2048]{1,0:T(8,128)(2,1)S(1)}, bf16[128,2048]{1,0:T(8,128)(2,1)S(1)}, u32[]{:S(2)}, u32[]{:S(2)}) %collective-permute-start.29) | collective-permute-done | bytes 524320 | tf_op jit(solution)/shard_map/ppermute | solution.py:70
  181.1 8.8 %collective-permute-done.30.refs_3_ = bf16[128,2048]{1,0:T(8,128)(2,1)S(1)} collective-permute-done((bf16[128,2048]{1,0:T(8,128)(2,1)S(1)}, bf16[128,2048]{1,0:T(8,128)(2,1)S(1)}, u32[]{:S(2)}, u32[]{:S(2)}) %collective-permute-start.30) | collective-permute-done | bytes 524320 | tf_op jit(solution)/shard_map/ppermute | solution.py:70
  189.9 9.6 %collective-permute-done.33.refs_5_ = bf16[128,2048]{1,0:T(8,128)(2,1)S(1)} collective-permute-done((bf16[128,2048]{1,0:T(8,128)(2,1)S(1)}, bf16[128,2048]{1,0:T(8,128)(2,1)S(1)}, u32[]{:S(2)}, u32[]{:S(2)}) %collective-permute-start.33) | collective-permute-done | bytes 524320 | tf_op jit(solution)/shard_map/ppermute | solution.py:70
  209.5 8.8 %ffn_in_kernel.3 = (bf16[8,256,1408]{2,1,0:T(8,128)(2,1)}, bf16[8,256,768]{2,1,0:T(8,128)(2,1)}, bf16[8,768,256]{2,1,0:T(8,128)(2,1)}) custom-call(bf16[256,2048]{1,0:T(8,128)(2,1)} %get-tuple-element.128.refs_0_, bf16[256,2048]{1,0:T(8,128)(2,1)} %collective-permute-done.35.refs_1_, bf16[2048,1408]{1,0:T(8,128)(2,1)} %all-gather.10.cloned.1.call-done.refs_2_.refs_4_.refs_11_), custom_call_target="tpu_custom_call" | custom-call | flops 2952790016 | bytes 7864320 | tf_op jit(solution)/shard_map/ffn_in_kernel/pallas_call | solution.py:248
  218.3 13.2 %collective-permute-done.38.refs_0_ = bf16[256,2048]{1,0:T(8,128)(2,1)} collective-permute-done((bf16[256,2048]{1,0:T(8,128)(2,1)}, bf16[256,2048]{1,0:T(8,128)(2,1)}, u32[]{:S(2)}, u32[]{:S(2)}) %collective-permute-start.38) | collective-permute-done | bytes 1048608 | tf_op jit(solution)/shard_map/ppermute | solution.py:70
  238.0 12.9 %ffn_in_kernel.4 = (bf16[8,256,1408]{2,1,0:T(8,128)(2,1)}, bf16[8,256,768]{2,1,0:T(8,128)(2,1)}, bf16[8,768,256]{2,1,0:T(8,128)(2,1)}) custom-call(bf16[256,2048]{1,0:T(8,128)(2,1)} %gate.22.refs_0_.refs_2_, bf16[256,2048]{1,0:T(8,128)(2,1)} %collective-permute-done.37.refs_1_.refs_3_, ...), custom_call_target="tpu_custom_call", output_to_operand_aliasing={{0}: (5, {}), {1}: (6, {}), {2}: (7, {})} | custom-call | flops 5905580032 | bytes 15728640 | tf_op jit(solution)/shard_map/ffn_in_kernel/pallas_call | solution.py:248
  255.5 8.8 %ffn_in_kernel.5 = (bf16[8,256,1408]{2,1,0:T(8,128)(2,1)}, bf16[8,256,768]{2,1,0:T(8,128)(2,1)}, bf16[8,768,256]{2,1,0:T(8,128)(2,1)}) custom-call(bf16[128,2048]{1,0:T(8,128)(2,1)} %gate.24.refs_0_.refs_6_, bf16[128,2048]{1,0:T(8,128)(2,1)} %gate.25.refs_1_.refs_7_, ...), custom_call_target="tpu_custom_call", output_to_operand_aliasing={{0}: (5, {}), {1}: (6, {}), {2}: (7, {})} | custom-call | flops 2952790016 | bytes 7864320 | tf_op jit(solution)/shard_map/ffn_in_kernel/pallas_call | solution.py:248
  264.3 13.1 %down_grad_kernel.1.refs_12_ = bf16[8,704,256]{2,1,0:T(8,128)(2,1)} custom-call(bf16[256,2048]{1,0:T(8,128)(2,1)} %gate.18.refs_0_, bf16[256,2048]{1,0:T(8,128)(2,1)} %collective-permute-done.11.refs_1_, bf16[256,2048]{1,0:T(8,128)(2,1)} %copy-done.54, bf16[256,2048]{1,0:T(8,128)(2,1)} %collective-permute-done.13.refs_3_, ...), custom_call_target="tpu_custom_call" | custom-call | flops 5905580032 | bytes 14417920 | tf_op jit(solution)/shard_map/down_grad_kernel/pallas_call | solution.py:279
  280.6 14.8 %ffn_back_kernel.1.refs_0_.refs_1_.refs_2_.refs_3_.refs_10_ = bf16[8,256,1408]{2,1,0:T(8,128)(2,1)} custom-call(bf16[256,2048]{1,0:T(8,128)(2,1)} %gate.18.refs_0_, bf16[256,2048]{1,0:T(8,128)(2,1)} %collective-permute-done.11.refs_1_, bf16[256,2048]{1,0:T(8,128)(2,1)} %copy-done.54, bf16[256,2048]{1,0:T(8,128)(2,1)} %collective-permute-done.13.refs_3_, ...), custom_call_target="tpu_custom_call" | custom-call | flops 5905580032 | bytes 17039360 | tf_op jit(solution)/shard_map/ffn_back_kernel/pallas_call | solution.py:248
  295.3 18.1 %parts_nt.2 = (bf16[256,2048]{1,0:T(8,128)(2,1)}, bf16[256,2048]{1,0:T(8,128)(2,1)}, bf16[256,2048]{1,0:T(8,128)(2,1)}, bf16[256,2048]{1,0:T(8,128)(2,1)}, bf16[...) custom-call(bf16[8,256,1408]{2,1,0:T(8,128)(2,1)} %ffn_back_kernel.1.re, ...), custom_call_target="tpu_custom_call" | custom-call | flops 11811160064 | bytes 14155776 | tf_op jit(solution)/shard_map/parts_nt/pallas_call | solution.py:505
  325.9 13.5 %gu_grad_kernel.2 = (bf16[1024,1408]{1,0:T(8,128)(2,1)}, f32[1024,128]{1,0:T(8,128)}) custom-call(bf16[256,2048]{1,0:T(8,128)(2,1)} %get-tuple-element.128.refs_0_, bf16[256,2048]{1,0:T(8,128)(2,1)} %collective-permute-done.35.refs_1_, bf16[256,2048]{1,0:T(8,128)(2,1)} %gate.22.refs_0_.refs_2_, bf16[256,2048]{1,0:T(8,128)(2,1)} %collective-permute-done.37.refs_1_.refs_3_, ...), custom_call_target="tpu_custom_call" | custom-call | flops 5905580032 | bytes 23330816 | tf_op jit(solution)/shard_map/gu_grad_kernel/pallas_call | solution.py:279
  339.4 7.7 %collective-permute-done.45.refs_0_ = bf16[128,2048]{1,0:T(8,128)(2,1)} collective-permute-done((bf16[128,2048]{1,0:T(8,128)(2,1)}, bf16[128,2048]{1,0:T(8,128)(2,1)}, u32[]{:S(2)}, u32[]{:S(2)}) %collective-permute-start.45) | collective-permute-done | bytes 524320 | tf_op jit(solution)/shard_map/ppermute | solution.py:70
  353.2 13.5 %gu_grad_kernel.3 = (bf16[1024,1408]{1,0:T(8,128)(2,1)}, f32[1024,128]{1,0:T(8,128)}) custom-call(bf16[256,2048]{1,0:T(8,128)(2,1)} %get-tuple-element.128.refs_0_, bf16[256,2048]{1,0:T(8,128)(2,1)} %collective-permute-done.35.refs_1_, bf16[256,2048]{1,0:T(8,128)(2,1)} %gate.22.refs_0_.refs_2_, bf16[256,2048]{1,0:T(8,128)(2,1)} %collective-permute-done.37.refs_1_.refs_3_, ...), custom_call_target="tpu_custom_call" | custom-call | flops 5905580032 | bytes 23330816 | tf_op jit(solution)/shard_map/gu_grad_kernel/pallas_call | solution.py:279
  377.9 11.0 %parts_blocks.1 = (bf16[256,2048]{1,0:T(8,128)(2,1)}, bf16[256,2048]{1,0:T(8,128)(2,1)}, bf16[256,2048]{1,0:T(8,128)(2,1)}, bf16[256,2048]{1,0:T(8,128)(2,1)}, b...) custom-call(bf16[8,256,768]{2,1,0:T(8,128)(2,1)} %get-tuple-element., ...), custom_call_target="tpu_custom_call" | custom-call | flops 5905580032 | bytes 11272192 | tf_op jit(solution)/shard_map/parts_blocks/pallas_call | solution.py:505
  388.9 11.8 %collective-permute-done.53.refs_0_ = bf16[256,2048]{1,0:T(8,128)(2,1)} collective-permute-done((bf16[256,2048]{1,0:T(8,128)(2,1)}, bf16[256,2048]{1,0:T(8,128)(2,1)}, u32[]{:S(2)}, u32[]{:S(2)}) %collective-permute-start.53) | collective-permute-done | bytes 1048608 | tf_op jit(solution)/shard_map/ppermute | solution.py:70
  407.5 6.4 %do_kernel.2.refs_2_ = bf16[8,256,256]{2,1,0:T(8,128)(2,1)} custom-call(bf16[256,2048]{1,0:T(8,128)(2,1)} %get-tuple-element.155.refs_5_.refs_0_, bf16[256,2048]{1,0:T(8,128)(2,1)} %get-tuple-element.169.refs_1_, bf16[256,2048]{1,0:T(8,128)(2,1)} %get-tuple-element.167.refs_2_, bf16[256,2048]{1,0:T(8,128)(2,1)} %collective-permute-done.59.refs_3_, ...), custom_call_target="tpu_custom_call" | custom-call | flops 1610612736 | bytes 8388608 | tf_op jit(solution)/shard_map/do_kernel/pallas_call | solution.py:248
  428.0 6.3 back_state_kernel.1.refs_1_.refs_10_
  446.3 15.5 %collective-permute-start.63 = (bf16[4,2,160,128]{3,2,1,0:T(8,128)(2,1)S(1)}, bf16[4,2,160,128]{3,2,1,0:T(8,128)(2,1)}, u32[]{:S(2)}, u32[]{:S(2)}) collective-permute-start(bf16[4,2,160,128]{3,2,1,0:T(8,128)(2,1)S(1)} %copy-done.1), channel_id=1, source_target_pairs={{2,0},{4,2},{6,4},{3,1},{5,3},{7,5},{10,8},{12,10},{14,12},{11,9},... | collective-permute-start | bytes 983048 | tf_op jit(solution)/shard_map/ppermute | solution.py:162
  465.0 15.1 %back_intra_kernel.1 = (f32[4,512,256]{2,1,0:T(8,128)}, f32[4,512,256]{2,1,0:T(8,128)}, f32[4,512,256]{2,1,0:T(8,128)}) custom-call(s32[9]{0:T(128)S(1)} %pad_add_fusion.refs_0_, bf16[8,4,64,384]{3,2,1,0:T(8,128)(2,1)} %bitcast.99, f32[4,1,512]{2,1,0:T(1,128)S(1)} %copy-done.39, bf16[128,512]{1,0:T(8,128)(2,1)} %constant.59.clone.refs_3_, ...), custom_call_target="tpu_custom_call" | custom-call | flops 2642411520 | bytes 10969088 | tf_op jit(solution)/shard_map/back_intra_kernel/pallas_call | solution.py:723
  489.5 6.3 proj_grad_kernel.1.refs_4_
  515.5 8.9 %back_output_kernel.1 = (bf16[8,4,64,384]{3,2,1,0:T(8,128)(2,1)S(1)}, bf16[8,4,64,384]{3,2,1,0:T(8,128)(2,1)S(1)}) custom-call(s32[9]{0:T(128)S(1)} %pad_add_fusion.refs_0_, bf16[8,4,64,384]{3,2,1,0:T(8,128)(2,1)} %bitcast.100, f32[4,1,512]{2,1,0:T(1,128)S(1)} %copy-done.39, bf16[128,512]{1,0:T(8,128)(2,1)} %constant.59.clone.refs_3_, ...), custom_call_target="tpu_custom_call" | custom-call | flops 1258291200 | bytes 13000704 | tf_op jit(solution)/shard_map/back_output_kernel/pallas_call | solution.py:723
  530.4 9.5 %qkv_grad_kernel.1.refs_5_ = bf16[4,4,128,384]{3,2,1,0:T(8,128)(2,1)} custom-call(bf16[256,2048]{1,0:T(8,128)(2,1)} %gate.16.refs_0_, bf16[256,2048]{1,0:T(8,128)(2,1)} %collective-permute-done.refs_1_, bf16[256,2048]{1,0:T(8,128)(2,1)} %collective-permute-done.1.refs_2_, bf16[256,2048]{1,0:T(8,128)(2,1)} %collective-permute-done.2.refs_3_, ...), custom_call_target="tpu_custom_call" | custom-call | flops 3221225472 | bytes 12582912 | tf_op jit(solution)/shard_map/qkv_grad_kernel/pallas_call | solution.py:279
  539.9 7.9 %parts_nt.3 = (bf16[256,2048]{1,0:T(8,128)(2,1)S(1)}, bf16[256,2048]{1,0:T(8,128)(2,1)}, bf16[256,2048]{1,0:T(8,128)(2,1)S(1)}, bf16[256,2048]{1,0:T(8,128)(2,1)...) custom-call(bf16[8,256,384]{2,1,0:T(8,128)(2,1)} %bitcast.91, ...), custom_call_target="tpu_custom_call" | custom-call | flops 3221225472 | bytes 9961472 | tf_op jit(solution)/shard_map/parts_nt/pallas_call | solution.py:505
  563.9 6.5 %collective-permute-done.82 = bf16[128,2048]{1,0:T(8,128)(2,1)S(1)} collective-permute-done((bf16[128,2048]{1,0:T(8,128)(2,1)S(1)}, bf16[128,2048]{1,0:T(8,128)(2,1)S(1)}, u32[]{:S(2)}, u32[]{:S(2)}) %collective-permute-start.82) | collective-permute-done | bytes 524320 | tf_op jit(solution)/shard_map/ppermute | solution.py:70
  582.5 10.4 %collective-permute-done.86 = bf16[256,1408]{1,0:T(8,128)(2,1)S(1)} collective-permute-done((bf16[256,1408]{1,0:T(8,128)(2,1)}, bf16[256,1408]{1,0:T(8,128)(2,1)S(1)}, u32[]{:S(2)}, u32[]{:S(2)}) %collective-permute-start.86) | collective-permute-done | bytes 720928 | tf_op jit(solution)/shard_map/ppermute | solution.py:70
  (470 shorter events, 292.2 us)
Async XLA Ops:
  26.6 45.2 %all-gather.12.cloned.1.call-start = ((), (), s32[]{:S(2)}) async-start(), calls=%async_computation.15 | async-start | bytes 1966080 | tf_op jit(solution)/shard_map/all_gather | solution.py:796
  29.3 123.1 %all-gather.8.cloned.1.call-start = ((), (), s32[]{:S(2)}) async-start(), calls=%async_computation.8 | async-start | bytes 1310720 | tf_op jit(solution)/shard_map/all_gather | solution.py:795
  29.4 25.2 %collective-permute-start.1 = (bf16[256,2048]{1,0:T(8,128)(2,1)}, bf16[256,2048]{1,0:T(8,128)(2,1)}, u32[]{:S(2)}, u32[]{:S(2)}) collective-permute-start(bf16[256,2048]{1,0:T(8,128)(2,1)} %gate.16.refs_0_), channel_id=1, source_target_pairs={{0,16},{16,0},{1,17},{17,1},{2,18},{18,2},{3,19},{19,3},{4,20},{20... | collective-permute-start | bytes 3145736 | tf_op jit(solution)/shard_map/ppermute | solution.py:70
  32.4 26.3 %collective-permute-start.3 = (bf16[256,2048]{1,0:T(8,128)(2,1)}, bf16[256,2048]{1,0:T(8,128)(2,1)}, u32[]{:S(2)}, u32[]{:S(2)}) collective-permute-start(bf16[256,2048]{1,0:T(8,128)(2,1)} %gate.16.refs_0_), channel_id=1, source_target_pairs={{0,1},{1,0},{2,3},{3,2},{4,5},{5,4},{6,7},{7,6},{8,9},{9,8},{10,11... | collective-permute-start | bytes 3145736 | tf_op jit(solution)/shard_map/ppermute | solution.py:70
  34.7 28.2 %collective-permute-start.10 = (s32[4,256]{1,0:T(4,128)S(1)}, s32[4,256]{1,0:T(4,128)S(1)}, u32[]{:S(2)}, u32[]{:S(2)}) collective-permute-start(s32[4,256]{1,0:T(4,128)S(1)} %reshape.284), channel_id=1, source_target_pairs={{0,1},{1,0},{2,3},{3,2},{4,5},{5,4},{6,7},{7,6},{8,9},{9,8},{10,11... | collective-permute-start | bytes 12296 | tf_op jit(solution)/shard_map/ppermute | solution.py:70
  40.9 31.9 %collective-permute-start = (bf16[256,2048]{1,0:T(8,128)(2,1)S(1)}, bf16[256,2048]{1,0:T(8,128)(2,1)}, u32[]{:S(2)}, u32[]{:S(2)}) collective-permute-start(bf16[256,2048]{1,0:T(8,128)(2,1)S(1)} %copy-done.41), channel_id=1, source_target_pairs={{0,8},{8,0},{1,9},{9,1},{2,10},{10,2},{3,11},{11,3},{4,12},{12,4},... | collective-permute-start | bytes 3145736 | tf_op jit(solution)/shard_map/ppermute | solution.py:70
  64.1 145.4 %all-gather.10.cloned.1.call-start = ((), (), s32[]{:S(2)}) async-start(), calls=%async_computation.9 | async-start | bytes 7208960 | tf_op jit(solution)/shard_map/all_gather | solution.py:837
  94.2 186.4 %all-gather.6.cloned.1.call-start = ((), (), s32[]{:S(2)}) async-start(), calls=%async_computation.7 | async-start | bytes 3604480 | tf_op jit(solution)/shard_map/all_gather | solution.py:843
  95.6 25.1 %collective-permute-start.12 = (bf16[256,2048]{1,0:T(8,128)(2,1)}, bf16[256,2048]{1,0:T(8,128)(2,1)S(1)}, u32[]{:S(2)}, u32[]{:S(2)}) collective-permute-start(bf16[256,2048]{1,0:T(8,128)(2,1)} %gate.18.refs_0_), channel_id=1, source_target_pairs={{0,16},{16,0},{1,17},{17,1},{2,18},{18,2},{3,19},{19,3},{4,20},{20... | collective-permute-start | bytes 3145736 | tf_op jit(solution)/shard_map/ppermute | solution.py:70
  96.9 25.8 %collective-permute-start.14 = (bf16[256,2048]{1,0:T(8,128)(2,1)}, bf16[256,2048]{1,0:T(8,128)(2,1)}, u32[]{:S(2)}, u32[]{:S(2)}) collective-permute-start(bf16[256,2048]{1,0:T(8,128)(2,1)} %gate.18.refs_0_), channel_id=1, source_target_pairs={{0,1},{1,0},{2,3},{3,2},{4,5},{5,4},{6,7},{7,6},{8,9},{9,8},{10,11... | collective-permute-start | bytes 3145736 | tf_op jit(solution)/shard_map/ppermute | solution.py:70
  176.2 23.3 %collective-permute-start.33 = (bf16[128,2048]{1,0:T(8,128)(2,1)S(1)}, bf16[128,2048]{1,0:T(8,128)(2,1)S(1)}, u32[]{:S(2)}, u32[]{:S(2)}) collective-permute-start(bf16[128,2048]{1,0:T(8,128)(2,1)S(1)} %get-tuple-element.266), channel_id=1, source_target_pairs={{0,16},{16,0},{1,17},{17,1},{2,18},{18,2},{3,19},{19,3},{4,20},{20... | collective-permute-start | bytes 1572872 | tf_op jit(solution)/shard_map/ppermute | solution.py:70
  205.0 217.7 %reduce-scatter.6.cloned.1.call-start = ((), (), s32[]{:S(2)}) async-start(), calls=%async_computation.10 | async-start | bytes 3604480 | tf_op jit(solution)/shard_map/reduce_scatter | solution.py:905
  205.6 25.9 %collective-permute-start.38 = (bf16[256,2048]{1,0:T(8,128)(2,1)}, bf16[256,2048]{1,0:T(8,128)(2,1)}, u32[]{:S(2)}, u32[]{:S(2)}) collective-permute-start(bf16[256,2048]{1,0:T(8,128)(2,1)} %get-tuple-element.128.refs_0_), channel_id=1, source_target_pairs={{0,1},{1,0},{2,3},{3,2},{4,5},{5,4},{6,7},{7,6},{8,9},{9,8},{10,11... | collective-permute-start | bytes 3145736 | tf_op jit(solution)/shard_map/ppermute | solution.py:70
  207.4 25.6 %collective-permute-start.34 = (bf16[256,2048]{1,0:T(8,128)(2,1)}, bf16[256,2048]{1,0:T(8,128)(2,1)}, u32[]{:S(2)}, u32[]{:S(2)}) collective-permute-start(bf16[256,2048]{1,0:T(8,128)(2,1)} %get-tuple-element.128.refs_0_), channel_id=1, source_target_pairs={{0,16},{16,0},{1,17},{17,1},{2,18},{18,2},{3,19},{19,3},{4,20},{20... | collective-permute-start | bytes 3145736 | tf_op jit(solution)/shard_map/ppermute | solution.py:70
  233.0 31.2 %collective-permute-start.11 = (bf16[256,2048]{1,0:T(8,128)(2,1)}, bf16[256,2048]{1,0:T(8,128)(2,1)}, u32[]{:S(2)}, u32[]{:S(2)}) collective-permute-start(bf16[256,2048]{1,0:T(8,128)(2,1)} %gate.18.refs_0_), channel_id=1, source_target_pairs={{0,8},{8,0},{1,9},{9,1},{2,10},{10,2},{3,11},{11,3},{4,12},{12,4},... | collective-permute-start | bytes 3145736 | tf_op jit(solution)/shard_map/ppermute | solution.py:70
  277.4 185.3 %reduce-scatter.8.cloned.1.call-start = ((), (), s32[]{:S(2)}) async-start(), calls=%async_computation.11 | async-start | bytes 3604480 | tf_op jit(solution)/shard_map/reduce_scatter | solution.py:955
  347.1 166.0 %reduce-scatter.10.cloned.1.call-start = ((), (), s32[]{:S(2)}) async-start(), calls=%async_computation.12 | async-start | bytes 3604480 | tf_op jit(solution)/shard_map/reduce_scatter | solution.py:955
  375.6 25.1 %collective-permute-start.53 = (bf16[256,2048]{1,0:T(8,128)(2,1)}, bf16[256,2048]{1,0:T(8,128)(2,1)}, u32[]{:S(2)}, u32[]{:S(2)}) collective-permute-start(bf16[256,2048]{1,0:T(8,128)(2,1)} %get-tuple-element.155.refs_5_.refs_0_), channel_id=1, source_target_pairs={{0,1},{1,0},{2,3},{3,2},{4,5},{5,4},{6,7},{7,6},{8,9},{9,8},{10,11... | collective-permute-start | bytes 3145736 | tf_op jit(solution)/shard_map/ppermute | solution.py:70
  376.1 24.9 %collective-permute-start.54 = (bf16[256,2048]{1,0:T(8,128)(2,1)}, bf16[256,2048]{1,0:T(8,128)(2,1)}, u32[]{:S(2)}, u32[]{:S(2)}) collective-permute-start(bf16[256,2048]{1,0:T(8,128)(2,1)} %get-tuple-element.155.refs_5_.refs_0_), channel_id=1, source_target_pairs={{0,16},{16,0},{1,17},{17,1},{2,18},{18,2},{3,19},{19,3},{4,20},{20... | collective-permute-start | bytes 3145736 | tf_op jit(solution)/shard_map/ppermute | solution.py:70
  377.6 23.4 %collective-permute-start.55 = (bf16[256,2048]{1,0:T(8,128)(2,1)}, bf16[256,2048]{1,0:T(8,128)(2,1)}, u32[]{:S(2)}, u32[]{:S(2)}) collective-permute-start(bf16[256,2048]{1,0:T(8,128)(2,1)} %get-tuple-element.155.refs_5_.refs_0_), channel_id=1, source_target_pairs={{0,8},{8,0},{1,9},{9,1},{2,10},{10,2},{3,11},{11,3},{4,12},{12,4},... | collective-permute-start | bytes 3145736 | tf_op jit(solution)/shard_map/ppermute | solution.py:70
  377.6 151.8 %reduce-scatter.12.cloned.1.call-start = ((), (), s32[]{:S(2)}) async-start(), calls=%async_computation.13 | async-start | bytes 1310720 | tf_op jit(solution)/shard_map/reduce_scatter | solution.py:1007
  407.5 27.6 %collective-permute-start.69 = (bf16[256,2048]{1,0:T(8,128)(2,1)}, bf16[256,2048]{1,0:T(8,128)(2,1)}, u32[]{:S(2)}, u32[]{:S(2)}) collective-permute-start(bf16[256,2048]{1,0:T(8,128)(2,1)} %get-tuple-element.179), channel_id=1, source_target_pairs={{0,8},{8,0},{1,9},{9,1},{2,10},{10,2},{3,11},{11,3},{4,12},{12,4},... | collective-permute-start | bytes 3145736 | tf_op jit(solution)/shard_map/ppermute | solution.py:70
  437.1 43.6 %collective-permute-start.70 = (bf16[128,2048]{1,0:T(8,128)(2,1)}, bf16[128,2048]{1,0:T(8,128)(2,1)}, u32[]{:S(2)}, u32[]{:S(2)}) collective-permute-start(bf16[128,2048]{1,0:T(8,128)(2,1)} %add_convert_fusion.8.refs_14_), channel_id=1, source_target_pairs={{0,16},{16,0},{1,17},{17,1},{2,18},{18,2},{3,19},{19,3},{4,20},{20... | collective-permute-start | bytes 1572872 | tf_op jit(solution)/shard_map/ppermute | solution.py:70
  440.8 40.0 %collective-permute-start.68 = (bf16[128,2048]{1,0:T(8,128)(2,1)}, bf16[128,2048]{1,0:T(8,128)(2,1)}, u32[]{:S(2)}, u32[]{:S(2)}) collective-permute-start(bf16[128,2048]{1,0:T(8,128)(2,1)} %add_convert_fusion.9.refs_13_), channel_id=1, source_target_pairs={{0,1},{1,0},{2,3},{3,2},{4,5},{5,4},{6,7},{7,6},{8,9},{9,8},{10,11... | collective-permute-start | bytes 1572872 | tf_op jit(solution)/shard_map/ppermute | solution.py:70
  444.3 36.4 %collective-permute-start.65 = (bf16[128,2048]{1,0:T(8,128)(2,1)}, bf16[128,2048]{1,0:T(8,128)(2,1)}, u32[]{:S(2)}, u32[]{:S(2)}) collective-permute-start(bf16[128,2048]{1,0:T(8,128)(2,1)} %get-tuple-element.263.refs_11_), channel_id=1, source_target_pairs={{0,1},{1,0},{2,3},{3,2},{4,5},{5,4},{6,7},{7,6},{8,9},{9,8},{10,11... | collective-permute-start | bytes 1572872 | tf_op jit(solution)/shard_map/ppermute | solution.py:70
  445.8 35.0 %collective-permute-start.66 = (bf16[128,2048]{1,0:T(8,128)(2,1)}, bf16[128,2048]{1,0:T(8,128)(2,1)}, u32[]{:S(2)}, u32[]{:S(2)}) collective-permute-start(bf16[128,2048]{1,0:T(8,128)(2,1)} %get-tuple-element.262.refs_12_), channel_id=1, source_target_pairs={{0,16},{16,0},{1,17},{17,1},{2,18},{18,2},{3,19},{19,3},{4,20},{20... | collective-permute-start | bytes 1572872 | tf_op jit(solution)/shard_map/ppermute | solution.py:70
  446.3 33.8 %collective-permute-start.63 = (bf16[4,2,160,128]{3,2,1,0:T(8,128)(2,1)S(1)}, bf16[4,2,160,128]{3,2,1,0:T(8,128)(2,1)}, u32[]{:S(2)}, u32[]{:S(2)}) collective-permute-start(bf16[4,2,160,128]{3,2,1,0:T(8,128)(2,1)S(1)} %copy-done.1), channel_id=1, source_target_pairs={{2,0},{4,2},{6,4},{3,1},{5,3},{7,5},{10,8},{12,10},{14,12},{11,9},... | collective-permute-start | bytes 983048 | tf_op jit(solution)/shard_map/ppermute | solution.py:162
  503.1 93.0 %reduce-scatter.14.cloned.1.call-start = ((), (), s32[]{:S(2)}) async-start(), calls=%async_computation.14 | async-start | bytes 1966080 | tf_op jit(solution)/shard_map/reduce_scatter | solution.py:1045
  577.0 50.6 %collective-permute-start.75 = (bf16[256,2048]{1,0:T(8,128)(2,1)}, bf16[256,2048]{1,0:T(8,128)(2,1)}, u32[]{:S(2)}, u32[]{:S(2)}) collective-permute-start(bf16[256,2048]{1,0:T(8,128)(2,1)} %get-tuple-element.200), channel_id=1, source_target_pairs={{0,8},{8,0},{1,9},{9,1},{2,10},{10,2},{3,11},{11,3},{4,12},{12,4},... | collective-permute-start | bytes 3145736 | tf_op jit(solution)/shard_map/ppermute | solution.py:70
  577.0 50.6 %collective-permute-start.83 = (bf16[128,2048]{1,0:T(8,128)(2,1)}, bf16[128,2048]{1,0:T(8,128)(2,1)}, u32[]{:S(2)}, u32[]{:S(2)}) collective-permute-start(bf16[128,2048]{1,0:T(8,128)(2,1)} %get-tuple-element.258.refs_1_), channel_id=1, source_target_pairs={{0,1},{1,0},{2,3},{3,2},{4,5},{5,4},{6,7},{7,6},{8,9},{9,8},{10,11... | collective-permute-start | bytes 1572872 | tf_op jit(solution)/shard_map/ppermute | solution.py:70
  580.4 47.2 %collective-permute-start.81 = (bf16[128,2048]{1,0:T(8,128)(2,1)}, bf16[128,2048]{1,0:T(8,128)(2,1)}, u32[]{:S(2)}, u32[]{:S(2)}) collective-permute-start(bf16[128,2048]{1,0:T(8,128)(2,1)} %get-tuple-element.257), channel_id=1, source_target_pairs={{0,16},{16,0},{1,17},{17,1},{2,18},{18,2},{3,19},{19,3},{4,20},{20... | collective-permute-start | bytes 1572872 | tf_op jit(solution)/shard_map/ppermute | solution.py:70
  581.9 45.7 %collective-permute-start.84 = (bf16[128,2048]{1,0:T(8,128)(2,1)}, bf16[128,2048]{1,0:T(8,128)(2,1)}, u32[]{:S(2)}, u32[]{:S(2)}) collective-permute-start(bf16[128,2048]{1,0:T(8,128)(2,1)} %get-tuple-element.256), channel_id=1, source_target_pairs={{0,16},{16,0},{1,17},{17,1},{2,18},{18,2},{3,19},{19,3},{4,20},{20... | collective-permute-start | bytes 1572872 | tf_op jit(solution)/shard_map/ppermute | solution.py:70
  (144 other events, 1273.1 us)
Sparse Core Ops, SparseCore 0:
  29.6 40.7 all-gather.11
  71.9 27.4 all-gather.7
  101.6 107.9 all-gather.9
  211.0 69.5 all-gather.5
  282.7 67.8 reduce-scatter.5
  352.8 64.2 reduce-scatter.7
  419.4 62.9 reduce-scatter.9
  503.2 26.1 reduce-scatter.11
  552.1 34.2 reduce-scatter.13

commit v5 on v4

--- a/solution.py
+++ b/solution.py
@@ -1010,6 +1010,7 @@
         back_output_kernel, meta, [qkv, seg_row, feat_c, rows_c, align_c, dstate_out, dq, dk, dv, inv],
         "sqcccqqqqs", [(row_out, "s")] * 2, 2 * far, [outputs, gu_r[1]],
     )
+    g_got, dqkv, scaled = meet(swap(g_send, "col"), dqkv, scaled)
 
     def qkv_side(sent):
         (late["qkv"],) = grad_call(
@@ -1040,16 +1041,15 @@
     )
     far_x = (pair_sum(x_, xc, half, tokens) + from_y.astype(F32)).astype(BF16)
     far_y = (pair_sum(y, yc, 0, half) + from_x.astype(F32)).astype(BF16)
-    g_got = swap(after(g_send, far_x), "col")
     f_pieces = [own, other, first_x, swap(far_y, "hi"), swap(far_x, "col"), first_y]
     qkv_g = lax.psum_scatter(qkv_g.reshape(D, PAYLOAD), "row", scatter_dimension=0, tiled=True)
     project_grad = lax.ppermute(
-        after(proj_r, qkv_g), ("row", "col"), [(b, a) for a, b in shard_pairs]
+        after(proj_r, f_pieces[5]), ("row", "col"), [(b, a) for a, b in shard_pairs]
     ).astype(F32)
     qkv_g = lax.all_to_all(
         qkv_g.reshape(8, n_rows, PAYLOAD), GROUP, split_axis=0, concat_axis=0, tiled=True
     )
-    (inputs_grad,) = row_call(input_back_kernel, f_pieces, [x, grad_r], [F32], [qkv_g])
+    (inputs_grad,) = row_call(input_back_kernel, f_pieces, [x, grad_r], [F32])
     v_g, q_g, k_g, both_gains = weights_call(
         qkv_g, vw, qw, kw, jnp.stack([again.astype(F32), fgain.astype(F32)], 1)
     )

time: 648 us -> 640 us (0.988)
    reduce_scatter x1, waiting for transfers between devices: 0.01 us -> 7.27 us  [body(): lax.psum_scatter(qkv_g.reshape(D, PAYLOAD), 'row', scatter_dimension=0, t...]
    unnamed x161 -> x183, local copies, waits for them, and re-layouts: 38.1 us -> 39.8 us
  transfers between devices with their start and end apart: 98 -> 98, of which waited for: 36 -> 35; matrix products, arithmetic and copies ran while one was open for 14% -> 14% of each run, Pallas kernels for 32% -> 33%
where the time goes in v5:
time: 640 us; the launch traced here: 629 us
  Pallas kernels  229 us (36%)
  waiting for transfers between devices  153 us (24%)
  starting transfers between devices  101 us (16%)
  local copies, waits for them, and re-layouts  74.5 us (12%)
  other arithmetic  55.5 us (9%)
  between operations  15.5 us (2%)
    ppermute x81, waiting for transfers between devices, swap(): return lax.ppermute(value, axis, [(0, 1), (1, 0)])  118 us
    pallas_call x7, Pallas kernels, slot_call(): pl.pallas_call(wrapped, grid=(count,), in_specs=[pl.BlockSpec(memory_spac...  65.2 us
    ppermute x81, starting transfers between devices, swap(): return lax.ppermute(value, axis, [(0, 1), (1, 0)])  58.7 us
    pallas_call x5, Pallas kernels, grad_call(): pl.pallas_call(wrapped, grid=(steps or width // tile,), in_specs=[pl.Bloc...  55.9 us
    pallas_call x6, Pallas kernels, attention_call(): pl.pallas_call(wrapped, out_shape=far_out([a for a, _ in outs], kernel is...  50 us
    pallas_call x4, Pallas kernels, parts_call(): pl.pallas_call(kernel, grid=(width // tile,), in_specs=[pl.BlockSpec((2,...  41.9 us
    unnamed x183, local copies, waits for them, and re-layouts  39.8 us
    ppermute x4, starting transfers between devices, walk_steps(): came = lax.ppermute(now, 'row', pairs)  27.3 us
  transfers between devices with their start and end apart: 98, of which 35 were waited for; matrix products, arithmetic and copies ran while one was open for 14% of the time, Pallas kernels for 33%

profile of v5, /device:TPU:16, one launch (start us, length us, event | category | flops | bytes accessed | tf_op | source)
XLA Modules:
  0.0 629.0 jit_solution(7711722681453857555)
XLA Ops:
  41.0 13.6 %collective-permute-done.1.refs_2_ = bf16[256,2048]{1,0:T(8,128)(2,1)} collective-permute-done((bf16[256,2048]{1,0:T(8,128)(2,1)}, bf16[256,2048]{1,0:T(8,128)(2,1)}, u32[]{:S(2)}, u32[]{:S(2)}) %collective-permute-start.1) | collective-permute-done | bytes 1048608 | tf_op jit(solution)/shard_map/ppermute | solution.py:70
  74.5 9.5 %qkv_kernel.1 = (bf16[8,256,384]{2,1,0:T(8,128)(2,1)}, f32[8,256,128]{2,1,0:T(8,128)}, bf16[2048,384]{1,0:T(8,128)(2,1)}) custom-call(bf16[256,2048]{1,0:T(8,128)(2,1)} %gate.15.refs_0_, bf16[256,2048]{1,0:T(8,128)(2,1)} %collective-permute-done.refs_1_, bf16[256,2048]{1,0:T(8,128)(2,1)} %collective-permute-done.1.refs_2_, ...), custom_call_target="tpu_custom_call" | custom-call | flops 3221225472 | bytes 14155776 | tf_op jit(solution)/shard_map/qkv_kernel/pallas_call | solution.py:248
  84.0 5.8 state_kernel.1.refs_1_
  97.5 8.3 %collective-permute-start.22 = (bf16[4,2,160,128]{3,2,1,0:T(8,128)(2,1)S(1)}, bf16[4,2,160,128]{3,2,1,0:T(8,128)(2,1)S(1)}, u32[]{:S(2)}, u32[]{:S(2)}) collective-permute-start(bf16[4,2,160,128]{3,2,1,0:T(8,128)(2,1)S(1)} %copy-done.25), channel_id=1, source_target_pairs={{0,2},{2,4},{4,6},{1,3},{3,5},{5,7},{8,10},{10,12},{12,14},{9,11},... | collective-permute-start | bytes 983048 | tf_op jit(solution)/shard_map/ppermute | solution.py:162
  107.6 5.9 intra_kernel.1
  127.5 11.6 %collective-permute-done.23 = bf16[4,2,160,128]{3,2,1,0:T(8,128)(2,1)} collective-permute-done((bf16[4,2,160,128]{3,2,1,0:T(8,128)(2,1)}, bf16[4,2,160,128]{3,2,1,0:T(8,128)(2,1)}, u32[]{:S(2)}, u32[]{:S(2)}) %collective-permute-start.23) | collective-permute-done | bytes 327712 | tf_op jit(solution)/shard_map/ppermute | solution.py:162
  142.3 8.1 %output_kernel.1 = (bf16[8,4,64,256]{3,2,1,0:T(8,128)(2,1)S(1)}, f32[4,512,8]{2,1,0:T(8,128)S(1)}) custom-call(s32[9]{0:T(128)S(1)} %pad_add_fusion.refs_0_, bf16[8,4,64,384]{3,2,1,0:T(8,128)(2,1)} %bitcast.97, f32[4,1,512]{2,1,0:T(1,128)S(1)} %copy-done.45, bf16[128,512]{1,0:T(8,128)(2,1)} %constant.59.clone.refs_3_, f32[8,512]{1,0:T(8,128)S(1)} %copy-done.41, ...), custom_call_target="tpu_custom_call" | custom-call | flops 629145600 | bytes 5791744 | tf_op jit(solution)/shard_map/output_kernel/pallas_call | solution.py:723
  163.4 11.0 %collective-permute-done.29 = bf16[128,2048]{1,0:T(8,128)(2,1)S(1)} collective-permute-done((bf16[128,2048]{1,0:T(8,128)(2,1)S(1)}, bf16[128,2048]{1,0:T(8,128)(2,1)S(1)}, u32[]{:S(2)}, u32[]{:S(2)}) %collective-permute-start.29) | collective-permute-done | bytes 524320 | tf_op jit(solution)/shard_map/ppermute | solution.py:70
  181.0 8.8 %collective-permute-done.30.refs_3_ = bf16[128,2048]{1,0:T(8,128)(2,1)S(1)} collective-permute-done((bf16[128,2048]{1,0:T(8,128)(2,1)S(1)}, bf16[128,2048]{1,0:T(8,128)(2,1)S(1)}, u32[]{:S(2)}, u32[]{:S(2)}) %collective-permute-start.30) | collective-permute-done | bytes 524320 | tf_op jit(solution)/shard_map/ppermute | solution.py:70
  189.8 9.6 %collective-permute-done.33.refs_5_ = bf16[128,2048]{1,0:T(8,128)(2,1)S(1)} collective-permute-done((bf16[128,2048]{1,0:T(8,128)(2,1)S(1)}, bf16[128,2048]{1,0:T(8,128)(2,1)S(1)}, u32[]{:S(2)}, u32[]{:S(2)}) %collective-permute-start.33) | collective-permute-done | bytes 524320 | tf_op jit(solution)/shard_map/ppermute | solution.py:70
  209.6 8.8 %ffn_in_kernel.3 = (bf16[8,256,1408]{2,1,0:T(8,128)(2,1)}, bf16[8,256,768]{2,1,0:T(8,128)(2,1)}, bf16[8,768,256]{2,1,0:T(8,128)(2,1)}) custom-call(bf16[256,2048]{1,0:T(8,128)(2,1)} %get-tuple-element.131.refs_0_, bf16[256,2048]{1,0:T(8,128)(2,1)} %collective-permute-done.35.refs_1_, bf16[2048,1408]{1,0:T(8,128)(2,1)} %all-gather.10.cloned.1.call-done.refs_2_.refs_4_.refs_11_), custom_call_target="tpu_custom_call" | custom-call | flops 2952790016 | bytes 7864320 | tf_op jit(solution)/shard_map/ffn_in_kernel/pallas_call | solution.py:248
  218.4 13.1 %collective-permute-done.38.refs_0_ = bf16[256,2048]{1,0:T(8,128)(2,1)} collective-permute-done((bf16[256,2048]{1,0:T(8,128)(2,1)}, bf16[256,2048]{1,0:T(8,128)(2,1)}, u32[]{:S(2)}, u32[]{:S(2)}) %collective-permute-start.38) | collective-permute-done | bytes 1048608 | tf_op jit(solution)/shard_map/ppermute | solution.py:70
  238.0 12.8 %ffn_in_kernel.4 = (bf16[8,256,1408]{2,1,0:T(8,128)(2,1)}, bf16[8,256,768]{2,1,0:T(8,128)(2,1)}, bf16[8,768,256]{2,1,0:T(8,128)(2,1)}) custom-call(bf16[256,2048]{1,0:T(8,128)(2,1)} %gate.21.refs_0_.refs_2_, bf16[256,2048]{1,0:T(8,128)(2,1)} %collective-permute-done.37.refs_1_.refs_3_, ...), custom_call_target="tpu_custom_call", output_to_operand_aliasing={{0}: (5, {}), {1}: (6, {}), {2}: (7, {})} | custom-call | flops 5905580032 | bytes 15728640 | tf_op jit(solution)/shard_map/ffn_in_kernel/pallas_call | solution.py:248
  255.4 8.8 %ffn_in_kernel.5 = (bf16[8,256,1408]{2,1,0:T(8,128)(2,1)}, bf16[8,256,768]{2,1,0:T(8,128)(2,1)}, bf16[8,768,256]{2,1,0:T(8,128)(2,1)}) custom-call(bf16[128,2048]{1,0:T(8,128)(2,1)} %gate.23.refs_0_.refs_6_, bf16[128,2048]{1,0:T(8,128)(2,1)} %gate.24.refs_1_.refs_7_, ...), custom_call_target="tpu_custom_call", output_to_operand_aliasing={{0}: (5, {}), {1}: (6, {}), {2}: (7, {})} | custom-call | flops 2952790016 | bytes 7864320 | tf_op jit(solution)/shard_map/ffn_in_kernel/pallas_call | solution.py:248
  264.2 13.1 %down_grad_kernel.1.refs_12_ = bf16[8,704,256]{2,1,0:T(8,128)(2,1)} custom-call(bf16[256,2048]{1,0:T(8,128)(2,1)} %gate.17.refs_0_, bf16[256,2048]{1,0:T(8,128)(2,1)} %collective-permute-done.11.refs_1_, bf16[256,2048]{1,0:T(8,128)(2,1)} %copy-done.61, bf16[256,2048]{1,0:T(8,128)(2,1)} %collective-permute-done.13.refs_3_, ...), custom_call_target="tpu_custom_call" | custom-call | flops 5905580032 | bytes 14417920 | tf_op jit(solution)/shard_map/down_grad_kernel/pallas_call | solution.py:279
  280.5 14.8 %ffn_back_kernel.1.refs_0_.refs_1_.refs_2_.refs_3_.refs_10_ = bf16[8,256,1408]{2,1,0:T(8,128)(2,1)} custom-call(bf16[256,2048]{1,0:T(8,128)(2,1)} %gate.17.refs_0_, bf16[256,2048]{1,0:T(8,128)(2,1)} %collective-permute-done.11.refs_1_, bf16[256,2048]{1,0:T(8,128)(2,1)} %copy-done.61, bf16[256,2048]{1,0:T(8,128)(2,1)} %collective-permute-done.13.refs_3_, ...), custom_call_target="tpu_custom_call" | custom-call | flops 5905580032 | bytes 17039360 | tf_op jit(solution)/shard_map/ffn_back_kernel/pallas_call | solution.py:248
  295.3 18.1 %parts_nt.2 = (bf16[256,2048]{1,0:T(8,128)(2,1)}, bf16[256,2048]{1,0:T(8,128)(2,1)}, bf16[256,2048]{1,0:T(8,128)(2,1)}, bf16[256,2048]{1,0:T(8,128)(2,1)}, bf16[...) custom-call(bf16[8,256,1408]{2,1,0:T(8,128)(2,1)} %ffn_back_kernel.1.re, ...), custom_call_target="tpu_custom_call" | custom-call | flops 11811160064 | bytes 14155776 | tf_op jit(solution)/shard_map/parts_nt/pallas_call | solution.py:505
  325.8 13.5 %gu_grad_kernel.2 = (bf16[1024,1408]{1,0:T(8,128)(2,1)}, f32[1024,128]{1,0:T(8,128)}) custom-call(bf16[256,2048]{1,0:T(8,128)(2,1)} %get-tuple-element.131.refs_0_, bf16[256,2048]{1,0:T(8,128)(2,1)} %collective-permute-done.35.refs_1_, bf16[256,2048]{1,0:T(8,128)(2,1)} %gate.21.refs_0_.refs_2_, bf16[256,2048]{1,0:T(8,128)(2,1)} %collective-permute-done.37.refs_1_.refs_3_, ...), custom_call_target="tpu_custom_call" | custom-call | flops 5905580032 | bytes 23330816 | tf_op jit(solution)/shard_map/gu_grad_kernel/pallas_call | solution.py:279
  339.4 7.6 %collective-permute-done.45.refs_0_ = bf16[128,2048]{1,0:T(8,128)(2,1)} collective-permute-done((bf16[128,2048]{1,0:T(8,128)(2,1)}, bf16[128,2048]{1,0:T(8,128)(2,1)}, u32[]{:S(2)}, u32[]{:S(2)}) %collective-permute-start.45) | collective-permute-done | bytes 524320 | tf_op jit(solution)/shard_map/ppermute | solution.py:70
  353.2 13.5 %gu_grad_kernel.3 = (bf16[1024,1408]{1,0:T(8,128)(2,1)}, f32[1024,128]{1,0:T(8,128)}) custom-call(bf16[256,2048]{1,0:T(8,128)(2,1)} %get-tuple-element.131.refs_0_, bf16[256,2048]{1,0:T(8,128)(2,1)} %collective-permute-done.35.refs_1_, bf16[256,2048]{1,0:T(8,128)(2,1)} %gate.21.refs_0_.refs_2_, bf16[256,2048]{1,0:T(8,128)(2,1)} %collective-permute-done.37.refs_1_.refs_3_, ...), custom_call_target="tpu_custom_call" | custom-call | flops 5905580032 | bytes 23330816 | tf_op jit(solution)/shard_map/gu_grad_kernel/pallas_call | solution.py:279
  377.7 11.0 %parts_blocks.1 = (bf16[256,2048]{1,0:T(8,128)(2,1)}, bf16[256,2048]{1,0:T(8,128)(2,1)}, bf16[256,2048]{1,0:T(8,128)(2,1)}, bf16[256,2048]{1,0:T(8,128)(2,1)}, b...) custom-call(bf16[8,256,768]{2,1,0:T(8,128)(2,1)} %get-tuple-element., ...), custom_call_target="tpu_custom_call" | custom-call | flops 5905580032 | bytes 11272192 | tf_op jit(solution)/shard_map/parts_blocks/pallas_call | solution.py:505
  388.8 11.8 %collective-permute-done.53.refs_0_ = bf16[256,2048]{1,0:T(8,128)(2,1)} collective-permute-done((bf16[256,2048]{1,0:T(8,128)(2,1)}, bf16[256,2048]{1,0:T(8,128)(2,1)}, u32[]{:S(2)}, u32[]{:S(2)}) %collective-permute-start.53) | collective-permute-done | bytes 1048608 | tf_op jit(solution)/shard_map/ppermute | solution.py:70
  407.4 6.4 %do_kernel.2.refs_2_ = bf16[8,256,256]{2,1,0:T(8,128)(2,1)} custom-call(bf16[256,2048]{1,0:T(8,128)(2,1)} %get-tuple-element.158.refs_5_.refs_0_, bf16[256,2048]{1,0:T(8,128)(2,1)} %get-tuple-element.172.refs_1_, bf16[256,2048]{1,0:T(8,128)(2,1)} %get-tuple-element.170.refs_2_, bf16[256,2048]{1,0:T(8,128)(2,1)} %collective-permute-done.59.refs_3_, ...), custom_call_target="tpu_custom_call" | custom-call | flops 1610612736 | bytes 8388608 | tf_op jit(solution)/shard_map/do_kernel/pallas_call | solution.py:248
  427.9 6.3 back_state_kernel.1.refs_1_.refs_10_
  446.2 15.5 %collective-permute-start.63 = (bf16[4,2,160,128]{3,2,1,0:T(8,128)(2,1)S(1)}, bf16[4,2,160,128]{3,2,1,0:T(8,128)(2,1)}, u32[]{:S(2)}, u32[]{:S(2)}) collective-permute-start(bf16[4,2,160,128]{3,2,1,0:T(8,128)(2,1)S(1)} %copy-done.1), channel_id=1, source_target_pairs={{2,0},{4,2},{6,4},{3,1},{5,3},{7,5},{10,8},{12,10},{14,12},{11,9},... | collective-permute-start | bytes 983048 | tf_op jit(solution)/shard_map/ppermute | solution.py:162
  464.8 15.1 %back_intra_kernel.1 = (f32[4,512,256]{2,1,0:T(8,128)}, f32[4,512,256]{2,1,0:T(8,128)}, f32[4,512,256]{2,1,0:T(8,128)}) custom-call(s32[9]{0:T(128)S(1)} %pad_add_fusion.refs_0_, bf16[8,4,64,384]{3,2,1,0:T(8,128)(2,1)} %bitcast.99, f32[4,1,512]{2,1,0:T(1,128)S(1)} %copy-done.45, bf16[128,512]{1,0:T(8,128)(2,1)} %constant.59.clone.refs_3_, ...), custom_call_target="tpu_custom_call" | custom-call | flops 2642411520 | bytes 10969088 | tf_op jit(solution)/shard_map/back_intra_kernel/pallas_call | solution.py:723
  489.4 6.3 proj_grad_kernel.1.refs_4_
  516.4 8.9 %back_output_kernel.1 = (bf16[8,4,64,384]{3,2,1,0:T(8,128)(2,1)S(1)}, bf16[8,4,64,384]{3,2,1,0:T(8,128)(2,1)S(1)}) custom-call(s32[9]{0:T(128)S(1)} %pad_add_fusion.refs_0_, bf16[8,4,64,384]{3,2,1,0:T(8,128)(2,1)} %bitcast.100, f32[4,1,512]{2,1,0:T(1,128)S(1)} %copy-done.45, bf16[128,512]{1,0:T(8,128)(2,1)} %constant.59.clone.refs_3_, ...), custom_call_target="tpu_custom_call" | custom-call | flops 1258291200 | bytes 13000704 | tf_op jit(solution)/shard_map/back_output_kernel/pallas_call | solution.py:723
  530.3 9.5 %qkv_grad_kernel.1.refs_5_ = bf16[4,4,128,384]{3,2,1,0:T(8,128)(2,1)} custom-call(bf16[256,2048]{1,0:T(8,128)(2,1)} %gate.15.refs_0_, bf16[256,2048]{1,0:T(8,128)(2,1)} %collective-permute-done.refs_1_, bf16[256,2048]{1,0:T(8,128)(2,1)} %collective-permute-done.1.refs_2_, bf16[256,2048]{1,0:T(8,128)(2,1)} %collective-permute-done.2.refs_3_, ...), custom_call_target="tpu_custom_call" | custom-call | flops 3221225472 | bytes 12582912 | tf_op jit(solution)/shard_map/qkv_grad_kernel/pallas_call | solution.py:279
  539.7 7.9 %parts_nt.3 = (bf16[256,2048]{1,0:T(8,128)(2,1)S(1)}, bf16[256,2048]{1,0:T(8,128)(2,1)}, bf16[256,2048]{1,0:T(8,128)(2,1)S(1)}, bf16[256,2048]{1,0:T(8,128)(2,1)...) custom-call(bf16[8,256,384]{2,1,0:T(8,128)(2,1)} %bitcast.89, ...), custom_call_target="tpu_custom_call" | custom-call | flops 3221225472 | bytes 9961472 | tf_op jit(solution)/shard_map/parts_nt/pallas_call | solution.py:505
  565.3 7.5 %collective-permute-done.81 = bf16[128,2048]{1,0:T(8,128)(2,1)S(1)} collective-permute-done((bf16[128,2048]{1,0:T(8,128)(2,1)S(1)}, bf16[128,2048]{1,0:T(8,128)(2,1)S(1)}, u32[]{:S(2)}, u32[]{:S(2)}) %collective-permute-start.81) | collective-permute-done | bytes 524320 | tf_op jit(solution)/shard_map/ppermute | solution.py:70
  580.6 7.3 %reduce-scatter.14.cloned.1.call-done = bf16[512,384]{1,0:T(8,128)(2,1)} async-done(((bf16[2048,384]{1,0:T(8,128)(2,1)}), bf16[512,384]{1,0:T(8,128)(2,1)}) %reduce-scatter.14.cloned.1.call-update) | async-done | bytes 393232 | tf_op jit(solution)/shard_map/reduce_scatter | solution.py:1045
  (492 shorter events, 283.9 us)
Async XLA Ops:
  26.6 45.2 %all-gather.12.cloned.1.call-start = ((), (), s32[]{:S(2)}) async-start(), calls=%async_computation.15 | async-start | bytes 1966080 | tf_op jit(solution)/shard_map/all_gather | solution.py:796
  29.3 123.0 %all-gather.8.cloned.1.call-start = ((), (), s32[]{:S(2)}) async-start(), calls=%async_computation.8 | async-start | bytes 1310720 | tf_op jit(solution)/shard_map/all_gather | solution.py:795
  29.4 25.2 %collective-permute-start.1 = (bf16[256,2048]{1,0:T(8,128)(2,1)}, bf16[256,2048]{1,0:T(8,128)(2,1)}, u32[]{:S(2)}, u32[]{:S(2)}) collective-permute-start(bf16[256,2048]{1,0:T(8,128)(2,1)} %gate.15.refs_0_), channel_id=1, source_target_pairs={{0,16},{16,0},{1,17},{17,1},{2,18},{18,2},{3,19},{19,3},{4,20},{20... | collective-permute-start | bytes 3145736 | tf_op jit(solution)/shard_map/ppermute | solution.py:70
  32.4 26.3 %collective-permute-start.3 = (bf16[256,2048]{1,0:T(8,128)(2,1)}, bf16[256,2048]{1,0:T(8,128)(2,1)}, u32[]{:S(2)}, u32[]{:S(2)}) collective-permute-start(bf16[256,2048]{1,0:T(8,128)(2,1)} %gate.15.refs_0_), channel_id=1, source_target_pairs={{0,1},{1,0},{2,3},{3,2},{4,5},{5,4},{6,7},{7,6},{8,9},{9,8},{10,11... | collective-permute-start | bytes 3145736 | tf_op jit(solution)/shard_map/ppermute | solution.py:70
  34.7 28.2 %collective-permute-start.10 = (s32[4,256]{1,0:T(4,128)S(1)}, s32[4,256]{1,0:T(4,128)S(1)}, u32[]{:S(2)}, u32[]{:S(2)}) collective-permute-start(s32[4,256]{1,0:T(4,128)S(1)} %reshape.284), channel_id=1, source_target_pairs={{0,1},{1,0},{2,3},{3,2},{4,5},{5,4},{6,7},{7,6},{8,9},{9,8},{10,11... | collective-permute-start | bytes 12296 | tf_op jit(solution)/shard_map/ppermute | solution.py:70
  40.9 31.9 %collective-permute-start = (bf16[256,2048]{1,0:T(8,128)(2,1)S(1)}, bf16[256,2048]{1,0:T(8,128)(2,1)}, u32[]{:S(2)}, u32[]{:S(2)}) collective-permute-start(bf16[256,2048]{1,0:T(8,128)(2,1)S(1)} %copy-done.50), channel_id=1, source_target_pairs={{0,8},{8,0},{1,9},{9,1},{2,10},{10,2},{3,11},{11,3},{4,12},{12,4},... | collective-permute-start | bytes 3145736 | tf_op jit(solution)/shard_map/ppermute | solution.py:70
  64.1 145.4 %all-gather.10.cloned.1.call-start = ((), (), s32[]{:S(2)}) async-start(), calls=%async_computation.9 | async-start | bytes 7208960 | tf_op jit(solution)/shard_map/all_gather | solution.py:837
  94.2 186.3 %all-gather.6.cloned.1.call-start = ((), (), s32[]{:S(2)}) async-start(), calls=%async_computation.7 | async-start | bytes 3604480 | tf_op jit(solution)/shard_map/all_gather | solution.py:843
  95.6 25.1 %collective-permute-start.12 = (bf16[256,2048]{1,0:T(8,128)(2,1)}, bf16[256,2048]{1,0:T(8,128)(2,1)S(1)}, u32[]{:S(2)}, u32[]{:S(2)}) collective-permute-start(bf16[256,2048]{1,0:T(8,128)(2,1)} %gate.17.refs_0_), channel_id=1, source_target_pairs={{0,16},{16,0},{1,17},{17,1},{2,18},{18,2},{3,19},{19,3},{4,20},{20... | collective-permute-start | bytes 3145736 | tf_op jit(solution)/shard_map/ppermute | solution.py:70
  96.9 25.8 %collective-permute-start.14 = (bf16[256,2048]{1,0:T(8,128)(2,1)}, bf16[256,2048]{1,0:T(8,128)(2,1)}, u32[]{:S(2)}, u32[]{:S(2)}) collective-permute-start(bf16[256,2048]{1,0:T(8,128)(2,1)} %gate.17.refs_0_), channel_id=1, source_target_pairs={{0,1},{1,0},{2,3},{3,2},{4,5},{5,4},{6,7},{7,6},{8,9},{9,8},{10,11... | collective-permute-start | bytes 3145736 | tf_op jit(solution)/shard_map/ppermute | solution.py:70
  205.0 217.6 %reduce-scatter.6.cloned.1.call-start = ((), (), s32[]{:S(2)}) async-start(), calls=%async_computation.10 | async-start | bytes 3604480 | tf_op jit(solution)/shard_map/reduce_scatter | solution.py:905
  205.5 25.9 %collective-permute-start.38 = (bf16[256,2048]{1,0:T(8,128)(2,1)}, bf16[256,2048]{1,0:T(8,128)(2,1)}, u32[]{:S(2)}, u32[]{:S(2)}) collective-permute-start(bf16[256,2048]{1,0:T(8,128)(2,1)} %get-tuple-element.131.refs_0_), channel_id=1, source_target_pairs={{0,1},{1,0},{2,3},{3,2},{4,5},{5,4},{6,7},{7,6},{8,9},{9,8},{10,11... | collective-permute-start | bytes 3145736 | tf_op jit(solution)/shard_map/ppermute | solution.py:70
  207.4 25.6 %collective-permute-start.34 = (bf16[256,2048]{1,0:T(8,128)(2,1)}, bf16[256,2048]{1,0:T(8,128)(2,1)}, u32[]{:S(2)}, u32[]{:S(2)}) collective-permute-start(bf16[256,2048]{1,0:T(8,128)(2,1)} %get-tuple-element.131.refs_0_), channel_id=1, source_target_pairs={{0,16},{16,0},{1,17},{17,1},{2,18},{18,2},{3,19},{19,3},{4,20},{20... | collective-permute-start | bytes 3145736 | tf_op jit(solution)/shard_map/ppermute | solution.py:70
  232.9 31.2 %collective-permute-start.11 = (bf16[256,2048]{1,0:T(8,128)(2,1)}, bf16[256,2048]{1,0:T(8,128)(2,1)}, u32[]{:S(2)}, u32[]{:S(2)}) collective-permute-start(bf16[256,2048]{1,0:T(8,128)(2,1)} %gate.17.refs_0_), channel_id=1, source_target_pairs={{0,8},{8,0},{1,9},{9,1},{2,10},{10,2},{3,11},{11,3},{4,12},{12,4},... | collective-permute-start | bytes 3145736 | tf_op jit(solution)/shard_map/ppermute | solution.py:70
  277.3 185.2 %reduce-scatter.8.cloned.1.call-start = ((), (), s32[]{:S(2)}) async-start(), calls=%async_computation.11 | async-start | bytes 3604480 | tf_op jit(solution)/shard_map/reduce_scatter | solution.py:955
  347.1 156.4 %reduce-scatter.10.cloned.1.call-start = ((), (), s32[]{:S(2)}) async-start(), calls=%async_computation.12 | async-start | bytes 3604480 | tf_op jit(solution)/shard_map/reduce_scatter | solution.py:955
  375.4 25.1 %collective-permute-start.53 = (bf16[256,2048]{1,0:T(8,128)(2,1)}, bf16[256,2048]{1,0:T(8,128)(2,1)}, u32[]{:S(2)}, u32[]{:S(2)}) collective-permute-start(bf16[256,2048]{1,0:T(8,128)(2,1)} %get-tuple-element.158.refs_5_.refs_0_), channel_id=1, source_target_pairs={{0,1},{1,0},{2,3},{3,2},{4,5},{5,4},{6,7},{7,6},{8,9},{9,8},{10,11... | collective-permute-start | bytes 3145736 | tf_op jit(solution)/shard_map/ppermute | solution.py:70
  376.0 24.9 %collective-permute-start.54 = (bf16[256,2048]{1,0:T(8,128)(2,1)}, bf16[256,2048]{1,0:T(8,128)(2,1)}, u32[]{:S(2)}, u32[]{:S(2)}) collective-permute-start(bf16[256,2048]{1,0:T(8,128)(2,1)} %get-tuple-element.158.refs_5_.refs_0_), channel_id=1, source_target_pairs={{0,16},{16,0},{1,17},{17,1},{2,18},{18,2},{3,19},{19,3},{4,20},{20... | collective-permute-start | bytes 3145736 | tf_op jit(solution)/shard_map/ppermute | solution.py:70
  377.5 23.4 %collective-permute-start.55 = (bf16[256,2048]{1,0:T(8,128)(2,1)}, bf16[256,2048]{1,0:T(8,128)(2,1)}, u32[]{:S(2)}, u32[]{:S(2)}) collective-permute-start(bf16[256,2048]{1,0:T(8,128)(2,1)} %get-tuple-element.158.refs_5_.refs_0_), channel_id=1, source_target_pairs={{0,8},{8,0},{1,9},{9,1},{2,10},{10,2},{3,11},{11,3},{4,12},{12,4},... | collective-permute-start | bytes 3145736 | tf_op jit(solution)/shard_map/ppermute | solution.py:70
  377.5 151.8 %reduce-scatter.12.cloned.1.call-start = ((), (), s32[]{:S(2)}) async-start(), calls=%async_computation.13 | async-start | bytes 1310720 | tf_op jit(solution)/shard_map/reduce_scatter | solution.py:1007
  407.4 27.5 %collective-permute-start.69 = (bf16[256,2048]{1,0:T(8,128)(2,1)}, bf16[256,2048]{1,0:T(8,128)(2,1)}, u32[]{:S(2)}, u32[]{:S(2)}) collective-permute-start(bf16[256,2048]{1,0:T(8,128)(2,1)} %get-tuple-element.182), channel_id=1, source_target_pairs={{0,8},{8,0},{1,9},{9,1},{2,10},{10,2},{3,11},{11,3},{4,12},{12,4},... | collective-permute-start | bytes 3145736 | tf_op jit(solution)/shard_map/ppermute | solution.py:70
  437.0 43.6 %collective-permute-start.70 = (bf16[128,2048]{1,0:T(8,128)(2,1)}, bf16[128,2048]{1,0:T(8,128)(2,1)}, u32[]{:S(2)}, u32[]{:S(2)}) collective-permute-start(bf16[128,2048]{1,0:T(8,128)(2,1)} %add_convert_fusion.8.refs_14_), channel_id=1, source_target_pairs={{0,16},{16,0},{1,17},{17,1},{2,18},{18,2},{3,19},{19,3},{4,20},{20... | collective-permute-start | bytes 1572872 | tf_op jit(solution)/shard_map/ppermute | solution.py:70
  440.6 40.0 %collective-permute-start.68 = (bf16[128,2048]{1,0:T(8,128)(2,1)}, bf16[128,2048]{1,0:T(8,128)(2,1)}, u32[]{:S(2)}, u32[]{:S(2)}) collective-permute-start(bf16[128,2048]{1,0:T(8,128)(2,1)} %add_convert_fusion.9.refs_13_), channel_id=1, source_target_pairs={{0,1},{1,0},{2,3},{3,2},{4,5},{5,4},{6,7},{7,6},{8,9},{9,8},{10,11... | collective-permute-start | bytes 1572872 | tf_op jit(solution)/shard_map/ppermute | solution.py:70
  444.2 36.4 %collective-permute-start.65 = (bf16[128,2048]{1,0:T(8,128)(2,1)}, bf16[128,2048]{1,0:T(8,128)(2,1)}, u32[]{:S(2)}, u32[]{:S(2)}) collective-permute-start(bf16[128,2048]{1,0:T(8,128)(2,1)} %get-tuple-element.269.refs_11_), channel_id=1, source_target_pairs={{0,1},{1,0},{2,3},{3,2},{4,5},{5,4},{6,7},{7,6},{8,9},{9,8},{10,11... | collective-permute-start | bytes 1572872 | tf_op jit(solution)/shard_map/ppermute | solution.py:70
  445.6 35.0 %collective-permute-start.66 = (bf16[128,2048]{1,0:T(8,128)(2,1)}, bf16[128,2048]{1,0:T(8,128)(2,1)}, u32[]{:S(2)}, u32[]{:S(2)}) collective-permute-start(bf16[128,2048]{1,0:T(8,128)(2,1)} %get-tuple-element.268.refs_12_), channel_id=1, source_target_pairs={{0,16},{16,0},{1,17},{17,1},{2,18},{18,2},{3,19},{19,3},{4,20},{20... | collective-permute-start | bytes 1572872 | tf_op jit(solution)/shard_map/ppermute | solution.py:70
  446.2 33.7 %collective-permute-start.63 = (bf16[4,2,160,128]{3,2,1,0:T(8,128)(2,1)S(1)}, bf16[4,2,160,128]{3,2,1,0:T(8,128)(2,1)}, u32[]{:S(2)}, u32[]{:S(2)}) collective-permute-start(bf16[4,2,160,128]{3,2,1,0:T(8,128)(2,1)S(1)} %copy-done.1), channel_id=1, source_target_pairs={{2,0},{4,2},{6,4},{3,1},{5,3},{7,5},{10,8},{12,10},{14,12},{11,9},... | collective-permute-start | bytes 983048 | tf_op jit(solution)/shard_map/ppermute | solution.py:162
  503.0 84.9 %reduce-scatter.14.cloned.1.call-start = ((), (), s32[]{:S(2)}) async-start(), calls=%async_computation.14 | async-start | bytes 1966080 | tf_op jit(solution)/shard_map/reduce_scatter | solution.py:1045
  565.3 38.4 %collective-permute-start.76 = (bf16[256,2048]{1,0:T(8,128)(2,1)}, bf16[256,2048]{1,0:T(8,128)(2,1)}, u32[]{:S(2)}, u32[]{:S(2)}) collective-permute-start(bf16[256,2048]{1,0:T(8,128)(2,1)} %get-tuple-element.205), channel_id=1, source_target_pairs={{0,8},{8,0},{1,9},{9,1},{2,10},{10,2},{3,11},{11,3},{4,12},{12,4},... | collective-permute-start | bytes 3145736 | tf_op jit(solution)/shard_map/ppermute | solution.py:70
  575.7 27.9 %collective-permute-start.82 = (bf16[128,2048]{1,0:T(8,128)(2,1)}, bf16[128,2048]{1,0:T(8,128)(2,1)S(1)}, u32[]{:S(2)}, u32[]{:S(2)}) collective-permute-start(bf16[128,2048]{1,0:T(8,128)(2,1)} %get-tuple-element.263), channel_id=1, source_target_pairs={{0,16},{16,0},{1,17},{17,1},{2,18},{18,2},{3,19},{19,3},{4,20},{20... | collective-permute-start | bytes 1572872 | tf_op jit(solution)/shard_map/ppermute | solution.py:70
  577.8 26.6 %collective-permute-start.78 = (bf16[128,2048]{1,0:T(8,128)(2,1)}, bf16[128,2048]{1,0:T(8,128)(2,1)}, u32[]{:S(2)}, u32[]{:S(2)}) collective-permute-start(bf16[128,2048]{1,0:T(8,128)(2,1)} %get-tuple-element.265), channel_id=1, source_target_pairs={{0,1},{1,0},{2,3},{3,2},{4,5},{5,4},{6,7},{7,6},{8,9},{9,8},{10,11... | collective-permute-start | bytes 1572872 | tf_op jit(solution)/shard_map/ppermute | solution.py:70
  579.2 30.7 %collective-permute-start.84 = (bf16[128,2048]{1,0:T(8,128)(2,1)}, bf16[128,2048]{1,0:T(8,128)(2,1)}, u32[]{:S(2)}, u32[]{:S(2)}) collective-permute-start(bf16[128,2048]{1,0:T(8,128)(2,1)} %get-tuple-element.264), channel_id=1, source_target_pairs={{0,1},{1,0},{2,3},{3,2},{4,5},{5,4},{6,7},{7,6},{8,9},{9,8},{10,11... | collective-permute-start | bytes 1572872 | tf_op jit(solution)/shard_map/ppermute | solution.py:70
  587.9 31.0 %all-to-all-start.1 = ((bf16[8,64,384]{2,1,0:T(8,128)(2,1)}), bf16[8,64,384]{2,1,0:T(8,128)(2,1)S(1)}, u32[]{:S(2)}, u32[]{:S(2)}) async-start(bf16[8,64,384]{2,1,0:T(8,128)(2,1)} %bitcast.111), calls=%async_computation.6 | async-start | bytes 786432 | tf_op jit(solution)/shard_map/all_to_all | solution.py:1049
  (155 other events, 1328.1 us)
Sparse Core Ops, SparseCore 0:
  29.6 40.7 all-gather.11
  71.9 27.4 all-gather.7
  101.6 107.9 all-gather.9
  211.0 69.5 all-gather.5
  282.7 67.7 reduce-scatter.5
  352.7 64.2 reduce-scatter.7
  419.3 62.9 reduce-scatter.9
  503.1 26.1 reduce-scatter.11
  553.4 34.4 reduce-scatter.13

commit v6 on v5

--- a/solution.py
+++ b/solution.py
@@ -1027,9 +1027,9 @@
         )
         return [late["qkv"]]
 
-    qkv_g = qkv_side([proj_r])[0]
+    qkv_g = qkv_side([])[0]
     own, other, y, yc, x_, xc, xy, xyc = parts_call(
-        dqkv.reshape(8, tokens, PAYLOAD), w_qkv, "nt", [qkv_g], 28
+        dqkv.reshape(8, tokens, PAYLOAD), w_qkv, "nt", [qkv_g, proj_r], 28
     )
     other, yc, xc, xyc = (swap(part, "core") for part in (other, yc, xc, xyc))
     to_x = pair_sum(xy, xyc, 0, half).astype(BF16)

time: 640 us -> 638 us (level)
  transfers between devices with their start and end apart: 98 -> 98, of which waited for: 35 -> 33; matrix products, arithmetic and copies ran while one was open for 14% -> 13% of each run, Pallas kernels for 33% -> 35%
where the time goes in v6:
time: 638 us; the launch traced here: 627 us
  Pallas kernels  229 us (36%)
  waiting for transfers between devices  155 us (24%)
  starting transfers between devices  98.9 us (16%)
  local copies, waits for them, and re-layouts  73.9 us (12%)
  other arithmetic  54.4 us (9%)
  between operations  15.5 us (2%)
    ppermute x81, waiting for transfers between devices, swap(): return lax.ppermute(value, axis, [(0, 1), (1, 0)])  123 us
    pallas_call x7, Pallas kernels, slot_call(): pl.pallas_call(wrapped, grid=(count,), in_specs=[pl.BlockSpec(memory_spac...  65.2 us
    ppermute x81, starting transfers between devices, swap(): return lax.ppermute(value, axis, [(0, 1), (1, 0)])  56.7 us
    pallas_call x5, Pallas kernels, grad_call(): pl.pallas_call(wrapped, grid=(steps or width // tile,), in_specs=[pl.Bloc...  55.9 us
    pallas_call x6, Pallas kernels, attention_call(): pl.pallas_call(wrapped, out_shape=far_out([a for a, _ in outs], kernel is...  50 us
    pallas_call x4, Pallas kernels, parts_call(): pl.pallas_call(kernel, grid=(width // tile,), in_specs=[pl.BlockSpec((2,...  41.9 us
    unnamed x183, local copies, waits for them, and re-layouts  39.6 us
    ppermute x4, starting transfers between devices, walk_steps(): came = lax.ppermute(now, 'row', pairs)  27.3 us
  transfers between devices with their start and end apart: 98, of which 33 were waited for; matrix products, arithmetic and copies ran while one was open for 13% of the time, Pallas kernels for 35%

profile of v6, /device:TPU:16, one launch (start us, length us, event | category | flops | bytes accessed | tf_op | source)
XLA Modules:
  0.0 627.3 jit_solution(8862210627591151857)
XLA Ops:
  41.0 13.6 %collective-permute-done.1.refs_2_ = bf16[256,2048]{1,0:T(8,128)(2,1)} collective-permute-done((bf16[256,2048]{1,0:T(8,128)(2,1)}, bf16[256,2048]{1,0:T(8,128)(2,1)}, u32[]{:S(2)}, u32[]{:S(2)}) %collective-permute-start.1) | collective-permute-done | bytes 1048608 | tf_op jit(solution)/shard_map/ppermute | solution.py:70
  74.5 9.5 %qkv_kernel.1 = (bf16[8,256,384]{2,1,0:T(8,128)(2,1)}, f32[8,256,128]{2,1,0:T(8,128)}, bf16[2048,384]{1,0:T(8,128)(2,1)}) custom-call(bf16[256,2048]{1,0:T(8,128)(2,1)} %gate.15.refs_0_, bf16[256,2048]{1,0:T(8,128)(2,1)} %collective-permute-done.refs_1_, bf16[256,2048]{1,0:T(8,128)(2,1)} %collective-permute-done.1.refs_2_, ...), custom_call_target="tpu_custom_call" | custom-call | flops 3221225472 | bytes 14155776 | tf_op jit(solution)/shard_map/qkv_kernel/pallas_call | solution.py:248
  97.5 8.3 %collective-permute-start.22 = (bf16[4,2,160,128]{3,2,1,0:T(8,128)(2,1)S(1)}, bf16[4,2,160,128]{3,2,1,0:T(8,128)(2,1)S(1)}, u32[]{:S(2)}, u32[]{:S(2)}) collective-permute-start(bf16[4,2,160,128]{3,2,1,0:T(8,128)(2,1)S(1)} %copy-done.25), channel_id=1, source_target_pairs={{0,2},{2,4},{4,6},{1,3},{3,5},{5,7},{8,10},{10,12},{12,14},{9,11},... | collective-permute-start | bytes 983048 | tf_op jit(solution)/shard_map/ppermute | solution.py:162
  107.6 5.9 intra_kernel.1
  127.5 11.6 %collective-permute-done.23 = bf16[4,2,160,128]{3,2,1,0:T(8,128)(2,1)} collective-permute-done((bf16[4,2,160,128]{3,2,1,0:T(8,128)(2,1)}, bf16[4,2,160,128]{3,2,1,0:T(8,128)(2,1)}, u32[]{:S(2)}, u32[]{:S(2)}) %collective-permute-start.23) | collective-permute-done | bytes 327712 | tf_op jit(solution)/shard_map/ppermute | solution.py:162
  142.3 8.1 %output_kernel.1 = (bf16[8,4,64,256]{3,2,1,0:T(8,128)(2,1)S(1)}, f32[4,512,8]{2,1,0:T(8,128)S(1)}) custom-call(s32[9]{0:T(128)S(1)} %pad_add_fusion.refs_0_, bf16[8,4,64,384]{3,2,1,0:T(8,128)(2,1)} %bitcast.97, f32[4,1,512]{2,1,0:T(1,128)S(1)} %copy-done.45, bf16[128,512]{1,0:T(8,128)(2,1)} %constant.59.clone.refs_3_, f32[8,512]{1,0:T(8,128)S(1)} %copy-done.41, ...), custom_call_target="tpu_custom_call" | custom-call | flops 629145600 | bytes 5791744 | tf_op jit(solution)/shard_map/output_kernel/pallas_call | solution.py:723
  163.4 11.0 %collective-permute-done.29 = bf16[128,2048]{1,0:T(8,128)(2,1)S(1)} collective-permute-done((bf16[128,2048]{1,0:T(8,128)(2,1)S(1)}, bf16[128,2048]{1,0:T(8,128)(2,1)S(1)}, u32[]{:S(2)}, u32[]{:S(2)}) %collective-permute-start.29) | collective-permute-done | bytes 524320 | tf_op jit(solution)/shard_map/ppermute | solution.py:70
  181.0 8.8 %collective-permute-done.30.refs_3_ = bf16[128,2048]{1,0:T(8,128)(2,1)S(1)} collective-permute-done((bf16[128,2048]{1,0:T(8,128)(2,1)S(1)}, bf16[128,2048]{1,0:T(8,128)(2,1)S(1)}, u32[]{:S(2)}, u32[]{:S(2)}) %collective-permute-start.30) | collective-permute-done | bytes 524320 | tf_op jit(solution)/shard_map/ppermute | solution.py:70
  189.8 9.6 %collective-permute-done.33.refs_5_ = bf16[128,2048]{1,0:T(8,128)(2,1)S(1)} collective-permute-done((bf16[128,2048]{1,0:T(8,128)(2,1)S(1)}, bf16[128,2048]{1,0:T(8,128)(2,1)S(1)}, u32[]{:S(2)}, u32[]{:S(2)}) %collective-permute-start.33) | collective-permute-done | bytes 524320 | tf_op jit(solution)/shard_map/ppermute | solution.py:70
  209.6 8.8 %ffn_in_kernel.3 = (bf16[8,256,1408]{2,1,0:T(8,128)(2,1)}, bf16[8,256,768]{2,1,0:T(8,128)(2,1)}, bf16[8,768,256]{2,1,0:T(8,128)(2,1)}) custom-call(bf16[256,2048]{1,0:T(8,128)(2,1)} %get-tuple-element.131.refs_0_, bf16[256,2048]{1,0:T(8,128)(2,1)} %collective-permute-done.35.refs_1_, bf16[2048,1408]{1,0:T(8,128)(2,1)} %all-gather.10.cloned.1.call-done.refs_2_.refs_4_.refs_11_), custom_call_target="tpu_custom_call" | custom-call | flops 2952790016 | bytes 7864320 | tf_op jit(solution)/shard_map/ffn_in_kernel/pallas_call | solution.py:248
  218.4 13.1 %collective-permute-done.38.refs_0_ = bf16[256,2048]{1,0:T(8,128)(2,1)} collective-permute-done((bf16[256,2048]{1,0:T(8,128)(2,1)}, bf16[256,2048]{1,0:T(8,128)(2,1)}, u32[]{:S(2)}, u32[]{:S(2)}) %collective-permute-start.38) | collective-permute-done | bytes 1048608 | tf_op jit(solution)/shard_map/ppermute | solution.py:70
  238.0 12.8 %ffn_in_kernel.4 = (bf16[8,256,1408]{2,1,0:T(8,128)(2,1)}, bf16[8,256,768]{2,1,0:T(8,128)(2,1)}, bf16[8,768,256]{2,1,0:T(8,128)(2,1)}) custom-call(bf16[256,2048]{1,0:T(8,128)(2,1)} %gate.21.refs_0_.refs_2_, bf16[256,2048]{1,0:T(8,128)(2,1)} %collective-permute-done.37.refs_1_.refs_3_, ...), custom_call_target="tpu_custom_call", output_to_operand_aliasing={{0}: (5, {}), {1}: (6, {}), {2}: (7, {})} | custom-call | flops 5905580032 | bytes 15728640 | tf_op jit(solution)/shard_map/ffn_in_kernel/pallas_call | solution.py:248
  255.4 8.8 %ffn_in_kernel.5 = (bf16[8,256,1408]{2,1,0:T(8,128)(2,1)}, bf16[8,256,768]{2,1,0:T(8,128)(2,1)}, bf16[8,768,256]{2,1,0:T(8,128)(2,1)}) custom-call(bf16[128,2048]{1,0:T(8,128)(2,1)} %gate.23.refs_0_.refs_6_, bf16[128,2048]{1,0:T(8,128)(2,1)} %gate.24.refs_1_.refs_7_, ...), custom_call_target="tpu_custom_call", output_to_operand_aliasing={{0}: (5, {}), {1}: (6, {}), {2}: (7, {})} | custom-call | flops 2952790016 | bytes 7864320 | tf_op jit(solution)/shard_map/ffn_in_kernel/pallas_call | solution.py:248
  264.2 13.1 %down_grad_kernel.1.refs_12_ = bf16[8,704,256]{2,1,0:T(8,128)(2,1)} custom-call(bf16[256,2048]{1,0:T(8,128)(2,1)} %gate.17.refs_0_, bf16[256,2048]{1,0:T(8,128)(2,1)} %collective-permute-done.11.refs_1_, bf16[256,2048]{1,0:T(8,128)(2,1)} %copy-done.63, bf16[256,2048]{1,0:T(8,128)(2,1)} %collective-permute-done.13.refs_3_, ...), custom_call_target="tpu_custom_call" | custom-call | flops 5905580032 | bytes 14417920 | tf_op jit(solution)/shard_map/down_grad_kernel/pallas_call | solution.py:279
  280.5 14.8 %ffn_back_kernel.1.refs_0_.refs_1_.refs_2_.refs_3_.refs_10_ = bf16[8,256,1408]{2,1,0:T(8,128)(2,1)} custom-call(bf16[256,2048]{1,0:T(8,128)(2,1)} %gate.17.refs_0_, bf16[256,2048]{1,0:T(8,128)(2,1)} %collective-permute-done.11.refs_1_, bf16[256,2048]{1,0:T(8,128)(2,1)} %copy-done.63, bf16[256,2048]{1,0:T(8,128)(2,1)} %collective-permute-done.13.refs_3_, ...), custom_call_target="tpu_custom_call" | custom-call | flops 5905580032 | bytes 17039360 | tf_op jit(solution)/shard_map/ffn_back_kernel/pallas_call | solution.py:248
  295.3 18.1 %parts_nt.2 = (bf16[256,2048]{1,0:T(8,128)(2,1)}, bf16[256,2048]{1,0:T(8,128)(2,1)}, bf16[256,2048]{1,0:T(8,128)(2,1)}, bf16[256,2048]{1,0:T(8,128)(2,1)}, bf16[...) custom-call(bf16[8,256,1408]{2,1,0:T(8,128)(2,1)} %ffn_back_kernel.1.re, ...), custom_call_target="tpu_custom_call" | custom-call | flops 11811160064 | bytes 14155776 | tf_op jit(solution)/shard_map/parts_nt/pallas_call | solution.py:505
  325.8 13.5 %gu_grad_kernel.2 = (bf16[1024,1408]{1,0:T(8,128)(2,1)}, f32[1024,128]{1,0:T(8,128)}) custom-call(bf16[256,2048]{1,0:T(8,128)(2,1)} %get-tuple-element.131.refs_0_, bf16[256,2048]{1,0:T(8,128)(2,1)} %collective-permute-done.35.refs_1_, bf16[256,2048]{1,0:T(8,128)(2,1)} %gate.21.refs_0_.refs_2_, bf16[256,2048]{1,0:T(8,128)(2,1)} %collective-permute-done.37.refs_1_.refs_3_, ...), custom_call_target="tpu_custom_call" | custom-call | flops 5905580032 | bytes 23330816 | tf_op jit(solution)/shard_map/gu_grad_kernel/pallas_call | solution.py:279
  339.4 7.6 %collective-permute-done.45.refs_0_ = bf16[128,2048]{1,0:T(8,128)(2,1)} collective-permute-done((bf16[128,2048]{1,0:T(8,128)(2,1)}, bf16[128,2048]{1,0:T(8,128)(2,1)}, u32[]{:S(2)}, u32[]{:S(2)}) %collective-permute-start.45) | collective-permute-done | bytes 524320 | tf_op jit(solution)/shard_map/ppermute | solution.py:70
  353.2 13.5 %gu_grad_kernel.3 = (bf16[1024,1408]{1,0:T(8,128)(2,1)}, f32[1024,128]{1,0:T(8,128)}) custom-call(bf16[256,2048]{1,0:T(8,128)(2,1)} %get-tuple-element.131.refs_0_, bf16[256,2048]{1,0:T(8,128)(2,1)} %collective-permute-done.35.refs_1_, bf16[256,2048]{1,0:T(8,128)(2,1)} %gate.21.refs_0_.refs_2_, bf16[256,2048]{1,0:T(8,128)(2,1)} %collective-permute-done.37.refs_1_.refs_3_, ...), custom_call_target="tpu_custom_call" | custom-call | flops 5905580032 | bytes 23330816 | tf_op jit(solution)/shard_map/gu_grad_kernel/pallas_call | solution.py:279
  377.7 11.0 %parts_blocks.1 = (bf16[256,2048]{1,0:T(8,128)(2,1)}, bf16[256,2048]{1,0:T(8,128)(2,1)}, bf16[256,2048]{1,0:T(8,128)(2,1)}, bf16[256,2048]{1,0:T(8,128)(2,1)}, b...) custom-call(bf16[8,256,768]{2,1,0:T(8,128)(2,1)} %get-tuple-element., ...), custom_call_target="tpu_custom_call" | custom-call | flops 5905580032 | bytes 11272192 | tf_op jit(solution)/shard_map/parts_blocks/pallas_call | solution.py:505
  388.8 11.8 %collective-permute-done.53.refs_0_ = bf16[256,2048]{1,0:T(8,128)(2,1)} collective-permute-done((bf16[256,2048]{1,0:T(8,128)(2,1)}, bf16[256,2048]{1,0:T(8,128)(2,1)}, u32[]{:S(2)}, u32[]{:S(2)}) %collective-permute-start.53) | collective-permute-done | bytes 1048608 | tf_op jit(solution)/shard_map/ppermute | solution.py:70
  407.4 6.4 %do_kernel.2.refs_2_ = bf16[8,256,256]{2,1,0:T(8,128)(2,1)} custom-call(bf16[256,2048]{1,0:T(8,128)(2,1)} %get-tuple-element.158.refs_5_.refs_0_, bf16[256,2048]{1,0:T(8,128)(2,1)} %get-tuple-element.172.refs_1_, bf16[256,2048]{1,0:T(8,128)(2,1)} %get-tuple-element.170.refs_2_, bf16[256,2048]{1,0:T(8,128)(2,1)} %collective-permute-done.59.refs_3_, ...), custom_call_target="tpu_custom_call" | custom-call | flops 1610612736 | bytes 8388608 | tf_op jit(solution)/shard_map/do_kernel/pallas_call | solution.py:248
  427.9 6.3 back_state_kernel.1.refs_1_.refs_10_
  446.2 15.5 %collective-permute-start.63 = (bf16[4,2,160,128]{3,2,1,0:T(8,128)(2,1)S(1)}, bf16[4,2,160,128]{3,2,1,0:T(8,128)(2,1)}, u32[]{:S(2)}, u32[]{:S(2)}) collective-permute-start(bf16[4,2,160,128]{3,2,1,0:T(8,128)(2,1)S(1)} %copy-done.1), channel_id=1, source_target_pairs={{2,0},{4,2},{6,4},{3,1},{5,3},{7,5},{10,8},{12,10},{14,12},{11,9},... | collective-permute-start | bytes 983048 | tf_op jit(solution)/shard_map/ppermute | solution.py:162
  464.8 15.1 %back_intra_kernel.1 = (f32[4,512,256]{2,1,0:T(8,128)}, f32[4,512,256]{2,1,0:T(8,128)}, f32[4,512,256]{2,1,0:T(8,128)}) custom-call(s32[9]{0:T(128)S(1)} %pad_add_fusion.refs_0_, bf16[8,4,64,384]{3,2,1,0:T(8,128)(2,1)} %bitcast.99, f32[4,1,512]{2,1,0:T(1,128)S(1)} %copy-done.45, bf16[128,512]{1,0:T(8,128)(2,1)} %constant.59.clone.refs_3_, ...), custom_call_target="tpu_custom_call" | custom-call | flops 2642411520 | bytes 10969088 | tf_op jit(solution)/shard_map/back_intra_kernel/pallas_call | solution.py:723
  489.4 6.3 %proj_grad_kernel.1.refs_4_ = bf16[256,2048]{1,0:T(8,128)(2,1)S(1)} custom-call(bf16[256,2048]{1,0:T(8,128)(2,1)} %get-tuple-element.158.refs_5_.refs_0_, bf16[256,2048]{1,0:T(8,128)(2,1)} %get-tuple-element.172.refs_1_, bf16[256,2048]{1,0:T(8,128)(2,1)} %get-tuple-element.170.refs_2_, bf16[256,2048]{1,0:T(8,128)(2,1)} %collective-permute-done.59.refs_3_, ...), custom_call_target="tpu_custom_call" | custom-call | flops 2147483648 | bytes 10485760 | tf_op jit(solution)/shard_map/proj_grad_kernel/pallas_call | solution.py:279
  516.4 8.9 %back_output_kernel.1 = (bf16[8,4,64,384]{3,2,1,0:T(8,128)(2,1)S(1)}, bf16[8,4,64,384]{3,2,1,0:T(8,128)(2,1)S(1)}) custom-call(s32[9]{0:T(128)S(1)} %pad_add_fusion.refs_0_, bf16[8,4,64,384]{3,2,1,0:T(8,128)(2,1)} %bitcast.100, f32[4,1,512]{2,1,0:T(1,128)S(1)} %copy-done.45, bf16[128,512]{1,0:T(8,128)(2,1)} %constant.59.clone.refs_3_, ...), custom_call_target="tpu_custom_call" | custom-call | flops 1258291200 | bytes 13000704 | tf_op jit(solution)/shard_map/back_output_kernel/pallas_call | solution.py:723
  527.7 9.5 %qkv_grad_kernel.1.refs_5_ = bf16[4,4,128,384]{3,2,1,0:T(8,128)(2,1)} custom-call(bf16[256,2048]{1,0:T(8,128)(2,1)} %gate.15.refs_0_, bf16[256,2048]{1,0:T(8,128)(2,1)} %collective-permute-done.refs_1_, bf16[256,2048]{1,0:T(8,128)(2,1)} %collective-permute-done.1.refs_2_, bf16[256,2048]{1,0:T(8,128)(2,1)} %collective-permute-done.2.refs_3_, ...), custom_call_target="tpu_custom_call" | custom-call | flops 3221225472 | bytes 12582912 | tf_op jit(solution)/shard_map/qkv_grad_kernel/pallas_call | solution.py:279
  538.2 7.9 %parts_nt.3 = (bf16[256,2048]{1,0:T(8,128)(2,1)S(1)}, bf16[256,2048]{1,0:T(8,128)(2,1)}, bf16[256,2048]{1,0:T(8,128)(2,1)S(1)}, bf16[256,2048]{1,0:T(8,128)(2,1)...) custom-call(bf16[8,256,384]{2,1,0:T(8,128)(2,1)} %bitcast.89, ...), custom_call_target="tpu_custom_call" | custom-call | flops 3221225472 | bytes 9961472 | tf_op jit(solution)/shard_map/parts_nt/pallas_call | solution.py:505
  560.5 10.7 %collective-permute-done.81 = bf16[128,2048]{1,0:T(8,128)(2,1)S(1)} collective-permute-done((bf16[128,2048]{1,0:T(8,128)(2,1)S(1)}, bf16[128,2048]{1,0:T(8,128)(2,1)S(1)}, u32[]{:S(2)}, u32[]{:S(2)}) %collective-permute-start.81) | collective-permute-done | bytes 524320 | tf_op jit(solution)/shard_map/ppermute | solution.py:70
  579.3 6.0 reduce-scatter.14.cloned.1.call-done
  601.0 7.2 %collective-permute-done.84.refs_4_ = bf16[128,2048]{1,0:T(8,128)(2,1)} collective-permute-done((bf16[128,2048]{1,0:T(8,128)(2,1)}, bf16[128,2048]{1,0:T(8,128)(2,1)}, u32[]{:S(2)}, u32[]{:S(2)}) %collective-permute-start.84) | collective-permute-done | bytes 524320 | tf_op jit(solution)/shard_map/ppermute | solution.py:70
  (492 shorter events, 278.8 us)
Async XLA Ops:
  26.6 45.2 %all-gather.12.cloned.1.call-start = ((), (), s32[]{:S(2)}) async-start(), calls=%async_computation.15 | async-start | bytes 1966080 | tf_op jit(solution)/shard_map/all_gather | solution.py:796
  29.3 123.0 %all-gather.8.cloned.1.call-start = ((), (), s32[]{:S(2)}) async-start(), calls=%async_computation.8 | async-start | bytes 1310720 | tf_op jit(solution)/shard_map/all_gather | solution.py:795
  29.4 25.2 %collective-permute-start.1 = (bf16[256,2048]{1,0:T(8,128)(2,1)}, bf16[256,2048]{1,0:T(8,128)(2,1)}, u32[]{:S(2)}, u32[]{:S(2)}) collective-permute-start(bf16[256,2048]{1,0:T(8,128)(2,1)} %gate.15.refs_0_), channel_id=1, source_target_pairs={{0,16},{16,0},{1,17},{17,1},{2,18},{18,2},{3,19},{19,3},{4,20},{20... | collective-permute-start | bytes 3145736 | tf_op jit(solution)/shard_map/ppermute | solution.py:70
  32.4 26.3 %collective-permute-start.3 = (bf16[256,2048]{1,0:T(8,128)(2,1)}, bf16[256,2048]{1,0:T(8,128)(2,1)}, u32[]{:S(2)}, u32[]{:S(2)}) collective-permute-start(bf16[256,2048]{1,0:T(8,128)(2,1)} %gate.15.refs_0_), channel_id=1, source_target_pairs={{0,1},{1,0},{2,3},{3,2},{4,5},{5,4},{6,7},{7,6},{8,9},{9,8},{10,11... | collective-permute-start | bytes 3145736 | tf_op jit(solution)/shard_map/ppermute | solution.py:70
  34.7 28.2 %collective-permute-start.10 = (s32[4,256]{1,0:T(4,128)S(1)}, s32[4,256]{1,0:T(4,128)S(1)}, u32[]{:S(2)}, u32[]{:S(2)}) collective-permute-start(s32[4,256]{1,0:T(4,128)S(1)} %reshape.284), channel_id=1, source_target_pairs={{0,1},{1,0},{2,3},{3,2},{4,5},{5,4},{6,7},{7,6},{8,9},{9,8},{10,11... | collective-permute-start | bytes 12296 | tf_op jit(solution)/shard_map/ppermute | solution.py:70
  40.9 31.9 %collective-permute-start = (bf16[256,2048]{1,0:T(8,128)(2,1)S(1)}, bf16[256,2048]{1,0:T(8,128)(2,1)}, u32[]{:S(2)}, u32[]{:S(2)}) collective-permute-start(bf16[256,2048]{1,0:T(8,128)(2,1)S(1)} %copy-done.50), channel_id=1, source_target_pairs={{0,8},{8,0},{1,9},{9,1},{2,10},{10,2},{3,11},{11,3},{4,12},{12,4},... | collective-permute-start | bytes 3145736 | tf_op jit(solution)/shard_map/ppermute | solution.py:70
  64.1 145.4 %all-gather.10.cloned.1.call-start = ((), (), s32[]{:S(2)}) async-start(), calls=%async_computation.9 | async-start | bytes 7208960 | tf_op jit(solution)/shard_map/all_gather | solution.py:837
  94.2 186.3 %all-gather.6.cloned.1.call-start = ((), (), s32[]{:S(2)}) async-start(), calls=%async_computation.7 | async-start | bytes 3604480 | tf_op jit(solution)/shard_map/all_gather | solution.py:843
  95.6 25.1 %collective-permute-start.12 = (bf16[256,2048]{1,0:T(8,128)(2,1)}, bf16[256,2048]{1,0:T(8,128)(2,1)S(1)}, u32[]{:S(2)}, u32[]{:S(2)}) collective-permute-start(bf16[256,2048]{1,0:T(8,128)(2,1)} %gate.17.refs_0_), channel_id=1, source_target_pairs={{0,16},{16,0},{1,17},{17,1},{2,18},{18,2},{3,19},{19,3},{4,20},{20... | collective-permute-start | bytes 3145736 | tf_op jit(solution)/shard_map/ppermute | solution.py:70
  96.9 25.8 %collective-permute-start.14 = (bf16[256,2048]{1,0:T(8,128)(2,1)}, bf16[256,2048]{1,0:T(8,128)(2,1)}, u32[]{:S(2)}, u32[]{:S(2)}) collective-permute-start(bf16[256,2048]{1,0:T(8,128)(2,1)} %gate.17.refs_0_), channel_id=1, source_target_pairs={{0,1},{1,0},{2,3},{3,2},{4,5},{5,4},{6,7},{7,6},{8,9},{9,8},{10,11... | collective-permute-start | bytes 3145736 | tf_op jit(solution)/shard_map/ppermute | solution.py:70
  205.0 217.6 %reduce-scatter.6.cloned.1.call-start = ((), (), s32[]{:S(2)}) async-start(), calls=%async_computation.10 | async-start | bytes 3604480 | tf_op jit(solution)/shard_map/reduce_scatter | solution.py:905
  205.5 25.9 %collective-permute-start.38 = (bf16[256,2048]{1,0:T(8,128)(2,1)}, bf16[256,2048]{1,0:T(8,128)(2,1)}, u32[]{:S(2)}, u32[]{:S(2)}) collective-permute-start(bf16[256,2048]{1,0:T(8,128)(2,1)} %get-tuple-element.131.refs_0_), channel_id=1, source_target_pairs={{0,1},{1,0},{2,3},{3,2},{4,5},{5,4},{6,7},{7,6},{8,9},{9,8},{10,11... | collective-permute-start | bytes 3145736 | tf_op jit(solution)/shard_map/ppermute | solution.py:70
  207.4 25.6 %collective-permute-start.34 = (bf16[256,2048]{1,0:T(8,128)(2,1)}, bf16[256,2048]{1,0:T(8,128)(2,1)}, u32[]{:S(2)}, u32[]{:S(2)}) collective-permute-start(bf16[256,2048]{1,0:T(8,128)(2,1)} %get-tuple-element.131.refs_0_), channel_id=1, source_target_pairs={{0,16},{16,0},{1,17},{17,1},{2,18},{18,2},{3,19},{19,3},{4,20},{20... | collective-permute-start | bytes 3145736 | tf_op jit(solution)/shard_map/ppermute | solution.py:70
  232.9 31.2 %collective-permute-start.11 = (bf16[256,2048]{1,0:T(8,128)(2,1)}, bf16[256,2048]{1,0:T(8,128)(2,1)}, u32[]{:S(2)}, u32[]{:S(2)}) collective-permute-start(bf16[256,2048]{1,0:T(8,128)(2,1)} %gate.17.refs_0_), channel_id=1, source_target_pairs={{0,8},{8,0},{1,9},{9,1},{2,10},{10,2},{3,11},{11,3},{4,12},{12,4},... | collective-permute-start | bytes 3145736 | tf_op jit(solution)/shard_map/ppermute | solution.py:70
  277.3 185.2 %reduce-scatter.8.cloned.1.call-start = ((), (), s32[]{:S(2)}) async-start(), calls=%async_computation.11 | async-start | bytes 3604480 | tf_op jit(solution)/shard_map/reduce_scatter | solution.py:955
  347.1 156.4 %reduce-scatter.10.cloned.1.call-start = ((), (), s32[]{:S(2)}) async-start(), calls=%async_computation.12 | async-start | bytes 3604480 | tf_op jit(solution)/shard_map/reduce_scatter | solution.py:955
  375.4 25.1 %collective-permute-start.53 = (bf16[256,2048]{1,0:T(8,128)(2,1)}, bf16[256,2048]{1,0:T(8,128)(2,1)}, u32[]{:S(2)}, u32[]{:S(2)}) collective-permute-start(bf16[256,2048]{1,0:T(8,128)(2,1)} %get-tuple-element.158.refs_5_.refs_0_), channel_id=1, source_target_pairs={{0,1},{1,0},{2,3},{3,2},{4,5},{5,4},{6,7},{7,6},{8,9},{9,8},{10,11... | collective-permute-start | bytes 3145736 | tf_op jit(solution)/shard_map/ppermute | solution.py:70
  376.0 24.9 %collective-permute-start.54 = (bf16[256,2048]{1,0:T(8,128)(2,1)}, bf16[256,2048]{1,0:T(8,128)(2,1)}, u32[]{:S(2)}, u32[]{:S(2)}) collective-permute-start(bf16[256,2048]{1,0:T(8,128)(2,1)} %get-tuple-element.158.refs_5_.refs_0_), channel_id=1, source_target_pairs={{0,16},{16,0},{1,17},{17,1},{2,18},{18,2},{3,19},{19,3},{4,20},{20... | collective-permute-start | bytes 3145736 | tf_op jit(solution)/shard_map/ppermute | solution.py:70
  377.5 159.7 %reduce-scatter.12.cloned.1.call-start = ((), (), s32[]{:S(2)}) async-start(), calls=%async_computation.13 | async-start | bytes 1310720 | tf_op jit(solution)/shard_map/reduce_scatter | solution.py:1007
  407.4 27.5 %collective-permute-start.69 = (bf16[256,2048]{1,0:T(8,128)(2,1)}, bf16[256,2048]{1,0:T(8,128)(2,1)}, u32[]{:S(2)}, u32[]{:S(2)}) collective-permute-start(bf16[256,2048]{1,0:T(8,128)(2,1)} %get-tuple-element.182), channel_id=1, source_target_pairs={{0,8},{8,0},{1,9},{9,1},{2,10},{10,2},{3,11},{11,3},{4,12},{12,4},... | collective-permute-start | bytes 3145736 | tf_op jit(solution)/shard_map/ppermute | solution.py:70
  437.0 43.6 %collective-permute-start.70 = (bf16[128,2048]{1,0:T(8,128)(2,1)}, bf16[128,2048]{1,0:T(8,128)(2,1)}, u32[]{:S(2)}, u32[]{:S(2)}) collective-permute-start(bf16[128,2048]{1,0:T(8,128)(2,1)} %add_convert_fusion.8.refs_14_), channel_id=1, source_target_pairs={{0,16},{16,0},{1,17},{17,1},{2,18},{18,2},{3,19},{19,3},{4,20},{20... | collective-permute-start | bytes 1572872 | tf_op jit(solution)/shard_map/ppermute | solution.py:70
  440.6 40.0 %collective-permute-start.68 = (bf16[128,2048]{1,0:T(8,128)(2,1)}, bf16[128,2048]{1,0:T(8,128)(2,1)}, u32[]{:S(2)}, u32[]{:S(2)}) collective-permute-start(bf16[128,2048]{1,0:T(8,128)(2,1)} %add_convert_fusion.9.refs_13_), channel_id=1, source_target_pairs={{0,1},{1,0},{2,3},{3,2},{4,5},{5,4},{6,7},{7,6},{8,9},{9,8},{10,11... | collective-permute-start | bytes 1572872 | tf_op jit(solution)/shard_map/ppermute | solution.py:70
  444.2 36.4 %collective-permute-start.65 = (bf16[128,2048]{1,0:T(8,128)(2,1)}, bf16[128,2048]{1,0:T(8,128)(2,1)}, u32[]{:S(2)}, u32[]{:S(2)}) collective-permute-start(bf16[128,2048]{1,0:T(8,128)(2,1)} %get-tuple-element.269.refs_11_), channel_id=1, source_target_pairs={{0,1},{1,0},{2,3},{3,2},{4,5},{5,4},{6,7},{7,6},{8,9},{9,8},{10,11... | collective-permute-start | bytes 1572872 | tf_op jit(solution)/shard_map/ppermute | solution.py:70
  445.6 35.0 %collective-permute-start.66 = (bf16[128,2048]{1,0:T(8,128)(2,1)}, bf16[128,2048]{1,0:T(8,128)(2,1)}, u32[]{:S(2)}, u32[]{:S(2)}) collective-permute-start(bf16[128,2048]{1,0:T(8,128)(2,1)} %get-tuple-element.268.refs_12_), channel_id=1, source_target_pairs={{0,16},{16,0},{1,17},{17,1},{2,18},{18,2},{3,19},{19,3},{4,20},{20... | collective-permute-start | bytes 1572872 | tf_op jit(solution)/shard_map/ppermute | solution.py:70
  446.2 33.7 %collective-permute-start.63 = (bf16[4,2,160,128]{3,2,1,0:T(8,128)(2,1)S(1)}, bf16[4,2,160,128]{3,2,1,0:T(8,128)(2,1)}, u32[]{:S(2)}, u32[]{:S(2)}) collective-permute-start(bf16[4,2,160,128]{3,2,1,0:T(8,128)(2,1)S(1)} %copy-done.1), channel_id=1, source_target_pairs={{2,0},{4,2},{6,4},{3,1},{5,3},{7,5},{10,8},{12,10},{14,12},{11,9},... | collective-permute-start | bytes 983048 | tf_op jit(solution)/shard_map/ppermute | solution.py:162
  503.0 82.3 %reduce-scatter.14.cloned.1.call-start = ((), (), s32[]{:S(2)}) async-start(), calls=%async_computation.14 | async-start | bytes 1966080 | tf_op jit(solution)/shard_map/reduce_scatter | solution.py:1045
  560.4 39.7 %collective-permute-start.76 = (bf16[256,2048]{1,0:T(8,128)(2,1)}, bf16[256,2048]{1,0:T(8,128)(2,1)}, u32[]{:S(2)}, u32[]{:S(2)}) collective-permute-start(bf16[256,2048]{1,0:T(8,128)(2,1)} %get-tuple-element.205), channel_id=1, source_target_pairs={{0,8},{8,0},{1,9},{9,1},{2,10},{10,2},{3,11},{11,3},{4,12},{12,4},... | collective-permute-start | bytes 3145736 | tf_op jit(solution)/shard_map/ppermute | solution.py:70
  573.2 27.0 %collective-permute-start.82 = (bf16[128,2048]{1,0:T(8,128)(2,1)}, bf16[128,2048]{1,0:T(8,128)(2,1)S(1)}, u32[]{:S(2)}, u32[]{:S(2)}) collective-permute-start(bf16[128,2048]{1,0:T(8,128)(2,1)} %get-tuple-element.263), channel_id=1, source_target_pairs={{0,16},{16,0},{1,17},{17,1},{2,18},{18,2},{3,19},{19,3},{4,20},{20... | collective-permute-start | bytes 1572872 | tf_op jit(solution)/shard_map/ppermute | solution.py:70
  576.1 24.8 %collective-permute-start.78 = (bf16[128,2048]{1,0:T(8,128)(2,1)}, bf16[128,2048]{1,0:T(8,128)(2,1)}, u32[]{:S(2)}, u32[]{:S(2)}) collective-permute-start(bf16[128,2048]{1,0:T(8,128)(2,1)} %get-tuple-element.265), channel_id=1, source_target_pairs={{0,1},{1,0},{2,3},{3,2},{4,5},{5,4},{6,7},{7,6},{8,9},{9,8},{10,11... | collective-permute-start | bytes 1572872 | tf_op jit(solution)/shard_map/ppermute | solution.py:70
  576.6 31.6 %collective-permute-start.84 = (bf16[128,2048]{1,0:T(8,128)(2,1)}, bf16[128,2048]{1,0:T(8,128)(2,1)}, u32[]{:S(2)}, u32[]{:S(2)}) collective-permute-start(bf16[128,2048]{1,0:T(8,128)(2,1)} %get-tuple-element.264), channel_id=1, source_target_pairs={{0,1},{1,0},{2,3},{3,2},{4,5},{5,4},{6,7},{7,6},{8,9},{9,8},{10,11... | collective-permute-start | bytes 1572872 | tf_op jit(solution)/shard_map/ppermute | solution.py:70
  585.3 30.1 %all-to-all-start.1 = ((bf16[8,64,384]{2,1,0:T(8,128)(2,1)}), bf16[8,64,384]{2,1,0:T(8,128)(2,1)S(1)}, u32[]{:S(2)}, u32[]{:S(2)}) async-start(bf16[8,64,384]{2,1,0:T(8,128)(2,1)} %bitcast.111), calls=%async_computation.6 | async-start | bytes 786432 | tf_op jit(solution)/shard_map/all_to_all | solution.py:1049
  591.5 27.0 %collective-permute-start.86 = (bf16[64,2048]{1,0:T(8,128)(2,1)}, bf16[64,2048]{1,0:T(8,128)(2,1)}, u32[]{:S(2)}, u32[]{:S(2)}) collective-permute-start(bf16[64,2048]{1,0:T(8,128)(2,1)} %gate.29), channel_id=1, source_target_pairs={{0,0},{2,1},{4,2},{6,3},{1,4},{3,5},{5,6},{7,7},{8,8},{10,9},{12,1... | collective-permute-start | bytes 786440 | tf_op jit(solution)/shard_map/ppermute | solution.py:1046
  (155 other events, 1347.4 us)
Sparse Core Ops, SparseCore 0:
  29.6 40.7 all-gather.11
  71.9 27.4 all-gather.7
  101.6 107.9 all-gather.9
  211.0 69.5 all-gather.5
  282.7 67.7 reduce-scatter.5
  352.7 64.2 reduce-scatter.7
  419.3 62.9 reduce-scatter.9
  503.1 26.1 reduce-scatter.11
  552.0 33.3 reduce-scatter.13
